TPU v7x, 32 devices: a whole 2x2x4 slice. The times are simulated.
32 devices in a mesh: dp: 16 (over z, y, x), fsdp: 2 (over core).
Axes of the slice: x: 2, y: 2, z: 4, core: 2. Of those that a mesh axis runs over, the one named last changes fastest.
Arguments:
- tokens: bfloat16 [2, 18432, 1024], P(None, ('dp', 'fsdp')), may hold values from -6 to 6
- cotangent: bfloat16 [2, 18432, 1024], P(None, ('dp', 'fsdp')), may hold values from -6 to 6
- images: int32 [2, 16, 3], P(None, 'dp'), may hold values from 0 to 4, as said below
- attention_weight: float32 [4096, 1024], P(('dp', 'fsdp')), may hold values from -1 to 1
- attention_first: float32 [4096, 1024], P(('dp', 'fsdp')), may hold values from -0.00048828125 to 0.00048828125
- attention_second: float32 [4096, 1024], P(('dp', 'fsdp')), may hold values from 7.7838555e-11 to 3.1135422e-10
- widen_weight: float32 [1024, 5632], P(None, ('dp', 'fsdp')), may hold values from -0.1875 to 0.1875
- widen_first: float32 [1024, 5632], P(None, ('dp', 'fsdp')), may hold values from -0.00048828125 to 0.00048828125
- widen_second: float32 [1024, 5632], P(None, ('dp', 'fsdp')), may hold values from 7.7838555e-11 to 3.1135422e-10
- narrow_weight: float32 [2816, 1024], P(('dp', 'fsdp')), may hold values from -0.109375 to 0.109375
- narrow_first: float32 [2816, 1024], P(('dp', 'fsdp')), may hold values from -0.00048828125 to 0.00048828125
- narrow_second: float32 [2816, 1024], P(('dp', 'fsdp')), may hold values from 7.7838555e-11 to 3.1135422e-10
- norm_gains: float32 [2048], P(('dp', 'fsdp')), may hold values from 0.5 to 1.5
- gains_first: float32 [2048], P(('dp', 'fsdp')), may hold values from -0.0014648438 to 0.0014648438
- gains_second: float32 [2048], P(('dp', 'fsdp')), may hold values from 7.00547e-10 to 2.802188e-09
Outputs:
- block_output: float32 [2, 18432, 1024], P(None, ('dp', 'fsdp'))
- input_grad: float32 [2, 18432, 1024], P(None, ('dp', 'fsdp'))
- attention_master: float32 [4096, 1024], P(('dp', 'fsdp'))
- attention_mean: float32 [4096, 1024], P(('dp', 'fsdp'))
- attention_square: float32 [4096, 1024], P(('dp', 'fsdp'))
- widen_master: float32 [1024, 5632], P(None, ('dp', 'fsdp'))
- widen_mean: float32 [1024, 5632], P(None, ('dp', 'fsdp'))
- widen_square: float32 [1024, 5632], P(None, ('dp', 'fsdp'))
- narrow_master: float32 [2816, 1024], P(('dp', 'fsdp'))
- narrow_mean: float32 [2816, 1024], P(('dp', 'fsdp'))
- narrow_square: float32 [2816, 1024], P(('dp', 'fsdp'))
- gains_master: float32 [2048], P(('dp', 'fsdp'))
- gains_mean: float32 [2048], P(('dp', 'fsdp'))
- gains_square: float32 [2048], P(('dp', 'fsdp'))
- grad_norm: float32 [], replicated
Inputs may be any that keep to these rules, and one draw needn't show every extreme that they name: Each packed row's 3 slots are one of (4, 0, 0), (1, 1, 1), (2, 1, 0), (1, 2, 0): the images of the row's items in order, a 0 marking an empty slot.
All inputs are finite; a program needn't handle non-finite values.
Results may differ from a plain program's by a relative error of at most 0.014.
The roundings to bfloat16 on the way count: a program that leaves them out, or rounds other values in their place, can miss the bound.
Values may be sent and summed in bfloat16 or wider, within the bound.
A program may use at most 320 MiB of HBM per device.

v0:
```python
import jax
import jax.numpy as jnp
from jax import lax
from jax.sharding import PartitionSpec as P

HD = 64
TEXT = 128
PATCH = 256
ROW = 1152


NORM_EPS = 1e-06
MASKED = -1000000000.0
BETA_FIRST = 0.9
BETA_SECOND = 0.999
ADAM_EPS = 1e-08
MATRIX_RATE = 0.05
GAIN_RATE = 0.3
DECAY = 0.1
CLIP_LIMIT = 1.0
STEP_VALUE = 10.0


def gelu_tanh(values):
    return (
        0.5
        * values
        * (1.0 + jnp.tanh(0.7978845608028654 * (values + 0.044715 * values * values * values)))
    )


def gated_units(gate_pre, upward):
    return gelu_tanh(gate_pre) * upward


def rms_scale(values, gain_vector):
    return (
        values
        * lax.rsqrt(jnp.mean(values * values, axis=-1, keepdims=True) + NORM_EPS)
        * gain_vector
    )


def segment_ids(counts):
    item_sizes = jnp.where(counts > 0, TEXT + PATCH * counts, 0)
    item_ends = jnp.cumsum(item_sizes)
    places = jnp.arange(ROW, dtype=jnp.int32)
    return jnp.sum((places[:, None] >= item_ends[None, :]).astype(jnp.int32), axis=1)


def contract_rows(left, right):
    return lax.dot_general(
        left, right, (((0,), (0,)), ((), ())), preferred_element_type=jnp.float32
    )


def contract_cols(left, right):
    return lax.dot_general(
        left, right, (((1,), (1,)), ((), ())), preferred_element_type=jnp.float32
    )


def head_pairs(values):
    return values.reshape(values.shape[0], values.shape[1] // (2 * HD), 2 * HD).transpose(1, 0, 2)


def from_pairs(values):
    return values.transpose(1, 0, 2).reshape(values.shape[1], values.shape[0] * values.shape[2])


def flat_grads(grads):
    return (
        grads[0].reshape(-1, 128),
        grads[1].reshape(-1, 128),
        grads[2].reshape(-1, 128),
        grads[3],
    )


def shard_grads(reduced, model_width):
    widen_part = reduced[1].reshape(-1, model_width).T
    return (
        reduced[0].reshape(-1, model_width),
        widen_part,
        reduced[2].reshape(-1, model_width),
        reduced[3],
    )


def pair_forward(query_rows, key_rows, value_rows, same_item):
    query_heads = query_rows.reshape(query_rows.shape[0], 2, HD)
    key_heads = key_rows.reshape(key_rows.shape[0], 2, HD)
    value_heads = value_rows.reshape(value_rows.shape[0], 2, HD)
    scores = jnp.einsum("shd,khd->hsk", query_heads, key_heads, preferred_element_type=jnp.float32)
    scores = jnp.where(same_item[None], scores, MASKED)
    row_top = jnp.max(scores, axis=-1, keepdims=True)
    shifted = jnp.exp(scores - row_top)
    row_total = jnp.sum(shifted, axis=-1, keepdims=True)
    attend = shifted / row_total
    log_total = (row_top + jnp.log(row_total))[..., 0]
    mixed_heads = jnp.einsum(
        "hsk,khd->shd", attend.astype(jnp.bfloat16), value_heads, preferred_element_type=jnp.float32
    )
    return (mixed_heads.reshape(query_rows.shape[0], 2 * HD), log_total)


def pair_backward(query_rows, key_rows, value_rows, grad_rows, log_total, same_item):
    query_heads = query_rows.reshape(query_rows.shape[0], 2, HD)
    key_heads = key_rows.reshape(key_rows.shape[0], 2, HD)
    value_heads = value_rows.reshape(value_rows.shape[0], 2, HD)
    grad_heads = grad_rows.reshape(grad_rows.shape[0], 2, HD)
    scores = jnp.einsum("shd,khd->hsk", query_heads, key_heads, preferred_element_type=jnp.float32)
    scores = jnp.where(same_item[None], scores, MASKED)
    attend = jnp.exp(scores - log_total[..., None])
    grad_attend = jnp.einsum(
        "shd,khd->hsk", grad_heads, value_heads, preferred_element_type=jnp.float32
    )
    inner_sum = jnp.sum(attend * grad_attend, axis=-1, keepdims=True)
    grad_scores = (attend * (grad_attend - inner_sum)).astype(jnp.bfloat16)
    grad_query = jnp.einsum(
        "hsk,khd->shd", grad_scores, key_heads, preferred_element_type=jnp.float32
    )
    grad_key = jnp.einsum(
        "hsk,shd->khd", grad_scores, query_heads, preferred_element_type=jnp.float32
    )
    grad_value = jnp.einsum(
        "hsk,shd->khd", attend.astype(jnp.bfloat16), grad_heads, preferred_element_type=jnp.float32
    )
    query_count = query_rows.shape[0]
    key_count = key_rows.shape[0]
    return (
        grad_query.reshape(query_count, 2 * HD),
        grad_key.reshape(key_count, 2 * HD),
        grad_value.reshape(key_count, 2 * HD),
    )


def adam_update(master, first, second, gradient, factors, rate, decay):
    clip_factor, first_fix, second_fix = factors
    clipped = clip_factor * gradient
    first_new = BETA_FIRST * first + (1.0 - BETA_FIRST) * clipped
    second_new = BETA_SECOND * second + (1.0 - BETA_SECOND) * clipped * clipped
    master_new = master - rate * (
        first_new / first_fix / (jnp.sqrt(second_new / second_fix) + ADAM_EPS) + decay * master
    )
    return (master_new, first_new, second_new)


def local(
    tokens,
    cotangent,
    images,
    attention_weight,
    attention_first,
    attention_second,
    widen_weight,
    widen_first,
    widen_second,
    narrow_weight,
    narrow_first,
    narrow_second,
    norm_gains,
    gains_first,
    gains_second,
):
    model_width = tokens.shape[2]
    row_count = tokens.shape[1]
    hidden_width = narrow_weight.shape[0] * lax.axis_size(("dp", "fsdp"))
    half_index = lax.axis_index("fsdp")
    attention_low = attention_weight.astype(jnp.bfloat16)
    widen_low = widen_weight.astype(jnp.bfloat16)
    narrow_low = narrow_weight.astype(jnp.bfloat16)
    gains_low = norm_gains.astype(jnp.bfloat16)

    def forward(full_weights, rows_in, same_item):
        attention_full, widen_full, narrow_full, gains_full = full_weights
        matrices = attention_full.reshape(4, model_width, model_width)
        first_gain = gains_full[:model_width].astype(jnp.float32)
        second_gain = gains_full[model_width:].astype(jnp.float32)
        inputs = rows_in.astype(jnp.float32)
        normed = rms_scale(inputs, first_gain).astype(jnp.bfloat16)
        projected = jnp.einsum(
            "sd,jde->jse", normed, matrices[:3], preferred_element_type=jnp.float32
        ).astype(jnp.bfloat16)
        keys_all, values_all = (
            lax.all_gather(projected[1], "fsdp", axis=0, tiled=True),
            lax.all_gather(projected[2], "fsdp", axis=0, tiled=True),
        )
        mixed_heads, log_total = lax.map(
            lambda pieces: pair_forward(pieces[0], pieces[1], pieces[2], same_item),
            (head_pairs(projected[0]), head_pairs(keys_all), head_pairs(values_all)),
        )
        mixed_heads = from_pairs(mixed_heads).astype(jnp.bfloat16)
        hidden_one = inputs + jnp.dot(mixed_heads, matrices[3], preferred_element_type=jnp.float32)
        second = rms_scale(hidden_one, second_gain).astype(jnp.bfloat16)
        widened = jnp.dot(second, widen_full, preferred_element_type=jnp.float32)
        gate_pre = widened[:, :hidden_width]
        upward = widened[:, hidden_width:]
        hidden = gated_units(gate_pre, upward).astype(jnp.bfloat16)
        result = hidden_one + jnp.dot(hidden, narrow_full, preferred_element_type=jnp.float32)
        saved = (
            inputs,
            normed,
            projected[0],
            keys_all,
            values_all,
            log_total,
            mixed_heads,
            hidden_one,
            second,
            gate_pre,
            upward,
            hidden,
        )
        return (result, saved)

    def backward(full_weights, saved, grad_rows, same_item):
        attention_full, widen_full, narrow_full, gains_full = full_weights
        matrices = attention_full.reshape(4, model_width, model_width)
        first_gain = gains_full[:model_width].astype(jnp.float32)
        second_gain = gains_full[model_width:].astype(jnp.float32)
        (
            inputs,
            normed,
            query_rows,
            keys_all,
            values_all,
            log_total,
            mixed_heads,
            hidden_one,
            second,
            gate_pre,
            upward,
            hidden,
        ) = saved
        grad_narrow = contract_rows(hidden, grad_rows)
        grad_hidden = contract_cols(grad_rows, narrow_full)
        unused_value, gated_back = jax.vjp(gated_units, gate_pre, upward)
        grad_gate, grad_up = gated_back(grad_hidden)
        grad_widened = jnp.concatenate([grad_gate, grad_up], axis=1).astype(jnp.bfloat16)
        grad_widen_cols = contract_rows(grad_widened, second)
        grad_second = contract_cols(grad_widened, widen_full)
        unused_norm, second_back = jax.vjp(rms_scale, hidden_one, second_gain)
        grad_from_norm, grad_gain_two = second_back(grad_second)
        grad_hidden_one = grad_rows.astype(jnp.float32) + grad_from_norm
        grad_branch = grad_hidden_one.astype(jnp.bfloat16)
        grad_output_proj = contract_rows(mixed_heads, grad_branch)
        grad_mixed = contract_cols(grad_branch, matrices[3]).astype(jnp.bfloat16)
        grad_query, grad_key, grad_value = lax.map(
            lambda pieces: pair_backward(
                pieces[0], pieces[1], pieces[2], pieces[3], pieces[4], same_item
            ),
            (
                head_pairs(query_rows),
                head_pairs(keys_all),
                head_pairs(values_all),
                head_pairs(grad_mixed),
                log_total,
            ),
        )
        own_key, own_value = (
            lax.psum_scatter(
                from_pairs(grad_key).astype(jnp.bfloat16), "fsdp", scatter_dimension=0, tiled=True
            ).astype(jnp.float32),
            lax.psum_scatter(
                from_pairs(grad_value).astype(jnp.bfloat16), "fsdp", scatter_dimension=0, tiled=True
            ).astype(jnp.float32),
        )
        grad_projected = jnp.stack([from_pairs(grad_query), own_key, own_value]).astype(
            jnp.bfloat16
        )
        grad_qkv = jnp.einsum(
            "sd,jse->jde", normed, grad_projected, preferred_element_type=jnp.float32
        )
        grad_normed = jnp.einsum(
            "jse,jde->sd", grad_projected, matrices[:3], preferred_element_type=jnp.float32
        )
        unused_first, first_back = jax.vjp(rms_scale, inputs, first_gain)
        grad_from_first, grad_gain_one = first_back(grad_normed)
        input_rows = grad_hidden_one + grad_from_first
        grad_attention = jnp.concatenate([grad_qkv, grad_output_proj[None]], axis=0).reshape(
            4 * model_width, model_width
        )
        grad_gains = jnp.concatenate([grad_gain_one, grad_gain_two])
        return (input_rows, (grad_attention, grad_widen_cols, grad_narrow, grad_gains))

    start_grads = (
        jnp.zeros((4 * model_width, model_width), jnp.float32),
        jnp.zeros((2 * hidden_width, model_width), jnp.float32),
        jnp.zeros((hidden_width, model_width), jnp.float32),
        jnp.zeros((2 * model_width,), jnp.float32),
    )

    def micro_step(running, pieces):
        rows_in, grad_rows, counts = pieces
        seg_full = segment_ids(counts)
        seg_own = lax.dynamic_slice_in_dim(seg_full, half_index * row_count, row_count)
        same_item = seg_own[:, None] == seg_full[None, :]
        forward_weights = (
            lax.all_gather(attention_low, ("dp", "fsdp"), axis=0, tiled=True),
            lax.all_gather(widen_low, ("dp", "fsdp"), axis=1, tiled=True),
            lax.all_gather(narrow_low, ("dp", "fsdp"), axis=0, tiled=True),
            lax.all_gather(gains_low, ("dp", "fsdp"), axis=0, tiled=True),
        )
        result, saved = forward(forward_weights, rows_in, same_item)
        backward_weights = (
            lax.all_gather(attention_low, ("dp", "fsdp"), axis=0, tiled=True),
            lax.all_gather(widen_low, ("dp", "fsdp"), axis=1, tiled=True),
            lax.all_gather(narrow_low, ("dp", "fsdp"), axis=0, tiled=True),
            lax.all_gather(gains_low, ("dp", "fsdp"), axis=0, tiled=True),
        )
        input_rows, gradients = backward(backward_weights, saved, grad_rows, same_item)
        running = tuple((total + fresh for total, fresh in zip(running, gradients)))
        return (running, (result, input_rows))

    totals, (block_output, input_grad) = lax.scan(
        micro_step, start_grads, (tokens, cotangent, images[:, 0, :])
    )
    flat_list = flat_grads(totals)
    summed = (
        lax.psum_scatter(flat_list[0], ("dp", "fsdp"), scatter_dimension=0, tiled=True),
        lax.psum_scatter(flat_list[1], ("dp", "fsdp"), scatter_dimension=0, tiled=True),
        lax.psum_scatter(flat_list[2], ("dp", "fsdp"), scatter_dimension=0, tiled=True),
        lax.psum_scatter(flat_list[3], ("dp", "fsdp"), scatter_dimension=0, tiled=True),
    )
    reduced = shard_grads(summed, model_width)
    local_squares = (
        jnp.sum(reduced[0] * reduced[0])
        + jnp.sum(reduced[1] * reduced[1])
        + jnp.sum(reduced[2] * reduced[2])
        + jnp.sum(reduced[3] * reduced[3])
    )
    grad_norm = jnp.sqrt(lax.psum(local_squares, ("dp", "fsdp")))
    clip_factor = jnp.minimum(1.0, CLIP_LIMIT / (grad_norm + 1e-06))
    step_value = jnp.float32(STEP_VALUE)
    factors = (
        clip_factor,
        1.0 - jnp.power(jnp.float32(BETA_FIRST), step_value),
        1.0 - jnp.power(jnp.float32(BETA_SECOND), step_value),
    )
    attention_master, attention_mean, attention_square = adam_update(
        attention_weight, attention_first, attention_second, reduced[0], factors, MATRIX_RATE, DECAY
    )
    widen_master, widen_mean, widen_square = adam_update(
        widen_weight, widen_first, widen_second, reduced[1], factors, MATRIX_RATE, DECAY
    )
    narrow_master, narrow_mean, narrow_square = adam_update(
        narrow_weight, narrow_first, narrow_second, reduced[2], factors, MATRIX_RATE, DECAY
    )
    gains_master, gains_mean, gains_square = adam_update(
        norm_gains, gains_first, gains_second, reduced[3], factors, GAIN_RATE, 0.0
    )
    return (
        block_output,
        input_grad,
        attention_master,
        attention_mean,
        attention_square,
        widen_master,
        widen_mean,
        widen_square,
        narrow_master,
        narrow_mean,
        narrow_square,
        gains_master,
        gains_mean,
        gains_square,
        grad_norm,
    )


def solution(mesh):
    placed = (
        P(None, ("dp", "fsdp"), None),
        P(None, ("dp", "fsdp"), None),
        P(None, "dp", None),
        P(("dp", "fsdp"), None),
        P(("dp", "fsdp"), None),
        P(("dp", "fsdp"), None),
        P(None, ("dp", "fsdp")),
        P(None, ("dp", "fsdp")),
        P(None, ("dp", "fsdp")),
        P(("dp", "fsdp"), None),
        P(("dp", "fsdp"), None),
        P(("dp", "fsdp"), None),
        P(("dp", "fsdp")),
        P(("dp", "fsdp")),
        P(("dp", "fsdp")),
    )
    return jax.shard_map(
        local,
        mesh=mesh,
        in_specs=placed,
        out_specs=(
            P(None, ("dp", "fsdp"), None),
            P(None, ("dp", "fsdp"), None),
            P(("dp", "fsdp"), None),
            P(("dp", "fsdp"), None),
            P(("dp", "fsdp"), None),
            P(None, ("dp", "fsdp")),
            P(None, ("dp", "fsdp")),
            P(None, ("dp", "fsdp")),
            P(("dp", "fsdp"), None),
            P(("dp", "fsdp"), None),
            P(("dp", "fsdp"), None),
            P(("dp", "fsdp")),
            P(("dp", "fsdp")),
            P(("dp", "fsdp")),
            P(),
        ),
        check_vma=False,
    )
```

profile of v0, /device:TPU:0, one launch (start us, length us, event | category | flops | bytes accessed | tf_op | source)
XLA Modules:
  0.0 1677.6 jit_solution(11807096123481081183)
XLA Ops:
  12.5 999.1 %while.73 = (s32[]{:T(128)}, f32[4096,1024]{1,0:T(8,128)}, f32[5632,1024]{1,0:T(8,128)}, f32[2816,1024]{1,0:T(8,128)}, f32[2048]{0:T(1024)}, /*index=5*/f32[2,57...) while((s32[]{:T(128)}, f32[4096,1024]{1,0:T(8,128)}, ...), condition=%wide.region_18.19_spmd.clone, body=%wide.region_0.18_spmd.clone.sunk | while | flops 45746876416 | bytes 740799360 | solution.py:316
  14.2 42.5 %all-reduce.4 = bf16[2048]{0:T(1024)(128)(2,1)S(1)} all-reduce(bf16[2048]{0:T(1024)(128)(2,1)S(1)} %dynamic-update-slice.3), channel_id=1, replica_groups=mesh['dp'=16,'fsdp'=2] {'dp','fsdp'}, use_global_device_ids=true, to_apply=%add | all-reduce | flops 2048 | bytes 8192 | tf_op jit(solution)/shard_map/while
  58.4 39.4 %all-gather.14.cloned.1.call-done = bf16[4096,1024]{1,0:T(8,128)(2,1)} async-done(((bf16[128,1024]{1,0:T(8,128)(2,1)}), bf16[4096,1024]{1,0:T(8,128)(2,1)}) %all-gather.14.cloned.1.call-update) | async-done | bytes 8388624 | tf_op jit(solution)/shard_map/while/body/eval_jaxpr/all_gather | solution.py:300
  111.4 5.7 all-gather.16.cloned.1.call-done
  120.1 10.7 all-gather.18.cloned.1.call-done
  136.3 59.2 %while.74 = (s32[]{:T(128)}, bf16[8,576,128]{1,2,0:T(8,128)(2,1)}, f32[8,2,576]{2,1,0:T(2,128)}, bf16[8,1152,128]{1,2,0:T(8,128)(2,1)S(1)}, bf16[8,576,128]{1,2,...) while((s32[]{:T(128)}, bf16[8,576,128]{1,2,0:T(8,128)(2,1)}, ...), condition=%wide.region_7.7_spmd.clone, body=%wide.region_4.6_spmd.clone.sunk | while | flops 349690752 | bytes 19968356 | solution.py:189
  195.5 5.2 multiply_reduce_fusion.11
  200.8 25.7 %all-gather.20.cloned.1.call-done = bf16[1024,5632]{0,1:T(8,128)(2,1)} async-done(((bf16[1024,176]{0,1:T(8,128)(2,1)}), bf16[1024,5632]{0,1:T(8,128)(2,1)}) %all-gather.20.cloned.1.call-update) | async-done | bytes 11534352 | tf_op jit(solution)/shard_map/while/body/eval_jaxpr/all_gather | solution.py:301
  226.5 13.3 fusion.176
  239.8 55.6 %all-gather.22.cloned.1.call-done = bf16[2816,1024]{1,0:T(8,128)(2,1)} async-done(((bf16[88,1024]{1,0:T(8,128)(2,1)}), bf16[2816,1024]{1,0:T(8,128)(2,1)}) %all-gather.22.cloned.1.call-update) | async-done | bytes 5767184 | tf_op jit(solution)/shard_map/while/body/eval_jaxpr/all_gather | solution.py:309
  295.4 16.1 fusion.177
  311.5 13.0 multiply_reduce_fusion.12
  332.4 90.6 %while.75 = (s32[]{:T(128)}, bf16[8,576,128]{1,2,0:T(8,128)(2,1)}, bf16[8,1152,128]{1,2,0:T(8,128)(2,1)}, bf16[8,1152,128]{1,2,0:T(8,128)(2,1)}, bf16[8,1152,128...) while((s32[]{:T(128)}, bf16[8,576,128]{1,2,0:T(8,128)(2,1)}, ...), condition=%wide.region_12.12_spmd.clone, body=%wide.region_10.11_spmd.clone.sunk | while | flops 860625792 | bytes 46643592 | solution.py:249
  427.4 5.0 copy.71
  432.4 5.2 convolution_bitcast_fusion.4
  439.2 9.3 bitcast_dynamic-update-slice_fusion.4
  448.6 7.5 select_add_fusion.5
  456.1 16.1 select_add_fusion.4
  472.3 9.4 fusion.180
  481.8 6.2 convolution_bitcast_fusion.5
  492.2 10.9 bitcast_add_fusion.2
  507.7 40.3 %all-reduce.4 = bf16[2048]{0:T(1024)(128)(2,1)S(1)} all-reduce(bf16[2048]{0:T(1024)(128)(2,1)S(1)} %dynamic-update-slice.3), channel_id=1, replica_groups=mesh['dp'=16,'fsdp'=2] {'dp','fsdp'}, use_global_device_ids=true, to_apply=%add | all-reduce | flops 2048 | bytes 8192 | tf_op jit(solution)/shard_map/while
  549.7 38.0 %all-gather.14.cloned.1.call-done = bf16[4096,1024]{1,0:T(8,128)(2,1)} async-done(((bf16[128,1024]{1,0:T(8,128)(2,1)}), bf16[4096,1024]{1,0:T(8,128)(2,1)}) %all-gather.14.cloned.1.call-update) | async-done | bytes 8388624 | tf_op jit(solution)/shard_map/while/body/eval_jaxpr/all_gather | solution.py:300
  601.3 5.7 all-gather.16.cloned.1.call-done
  610.0 10.5 all-gather.18.cloned.1.call-done
  626.0 59.2 %while.74 = (s32[]{:T(128)}, bf16[8,576,128]{1,2,0:T(8,128)(2,1)}, f32[8,2,576]{2,1,0:T(2,128)}, bf16[8,1152,128]{1,2,0:T(8,128)(2,1)S(1)}, bf16[8,576,128]{1,2,...) while((s32[]{:T(128)}, bf16[8,576,128]{1,2,0:T(8,128)(2,1)}, ...), condition=%wide.region_7.7_spmd.clone, body=%wide.region_4.6_spmd.clone.sunk | while | flops 349690752 | bytes 19968356 | solution.py:189
  685.3 5.2 multiply_reduce_fusion.11
  690.5 25.9 %all-gather.20.cloned.1.call-done = bf16[1024,5632]{0,1:T(8,128)(2,1)} async-done(((bf16[1024,176]{0,1:T(8,128)(2,1)}), bf16[1024,5632]{0,1:T(8,128)(2,1)}) %all-gather.20.cloned.1.call-update) | async-done | bytes 11534352 | tf_op jit(solution)/shard_map/while/body/eval_jaxpr/all_gather | solution.py:301
  716.4 13.3 fusion.176
  729.7 55.6 %all-gather.22.cloned.1.call-done = bf16[2816,1024]{1,0:T(8,128)(2,1)} async-done(((bf16[88,1024]{1,0:T(8,128)(2,1)}), bf16[2816,1024]{1,0:T(8,128)(2,1)}) %all-gather.22.cloned.1.call-update) | async-done | bytes 5767184 | tf_op jit(solution)/shard_map/while/body/eval_jaxpr/all_gather | solution.py:309
  785.2 16.4 fusion.177
  801.7 13.0 multiply_reduce_fusion.12
  822.6 90.5 %while.75 = (s32[]{:T(128)}, bf16[8,576,128]{1,2,0:T(8,128)(2,1)}, bf16[8,1152,128]{1,2,0:T(8,128)(2,1)}, bf16[8,1152,128]{1,2,0:T(8,128)(2,1)}, bf16[8,1152,128...) while((s32[]{:T(128)}, bf16[8,576,128]{1,2,0:T(8,128)(2,1)}, ...), condition=%wide.region_12.12_spmd.clone, body=%wide.region_10.11_spmd.clone.sunk | while | flops 860625792 | bytes 46643592 | solution.py:249
  922.1 5.2 convolution_bitcast_fusion.4
  929.0 9.3 bitcast_dynamic-update-slice_fusion.4
  938.4 10.4 select_add_fusion.5
  948.8 22.0 %select_add_fusion.4 = f32[5632,1024]{1,0:T(8,128)} fusion(f32[5632,1024]{1,0:T(8,128)} %get-tuple-element.887, pred[]{:T(512)S(6)} %compare.3, bf16[576,2816]{1,0:T(8,128)(2,1)} %copy-done.44, bf16[576,2816]{1,0:T(8,128)(2,1)} %copy-done.43, f32[576,1024]{1,0:T(8,128)S(1)} %copy-done.6, f32[1024]{0:T(1024)S(1)} %get-tuple-element.758, ...), kind=kOutput, calls=%fused_computation.27.clone.1 | convolution fusion | flops 6670057472 | bytes 54991104 | tf_op jit(solution)/shard_map/while/body/eval_jaxpr/dot_general | solution.py:52
  970.9 9.4 fusion.180
  980.3 6.2 convolution_bitcast_fusion.5
  990.8 14.0 bitcast_add_fusion.2
  1011.6 13.3 reshape.263
  1025.0 18.1 %reshape.261 = f32[32768,128]{1,0:T(8,128)} reshape(f32[4096,1024]{1,0:T(8,128)} %get-tuple-element.288) | data formatting | bytes 33554432 | tf_op jit(solution)/shard_map/reshape | solution.py:73
  1043.1 24.6 %reshape.262 = f32[45056,128]{1,0:T(8,128)} reshape(f32[5632,1024]{1,0:T(8,128)} %get-tuple-element.289) | data formatting | bytes 46137344 | tf_op jit(solution)/shard_map/reshape | solution.py:74
  1068.5 42.4 %all-reduce.2 = f32[2048]{0:T(1024)S(1)} all-reduce(f32[2048]{0:T(1024)S(1)} %copy-done.34), channel_id=9, replica_groups=mesh['dp'=16,'fsdp'=2] {'dp','fsdp'}, use_global_device_ids=true, to_apply=%region_25.26.clone | all-reduce | flops 2048 | bytes 16384
  1111.5 67.6 %reduce-scatter.10.cloned.1.call-done = f32[704,128]{1,0:T(8,128)} async-done(((f32[22528,128]{1,0:T(8,128)}), f32[704,128]{1,0:T(8,128)}) %reduce-scatter.10.cloned.1.call-update) | async-done | bytes 360464 | tf_op jit(solution)/shard_map/reduce_scatter | solution.py:323
  1180.7 179.4 %reduce-scatter.6.cloned.1.call-done = f32[1024,128]{1,0:T(8,128)} async-done(((f32[32768,128]{1,0:T(8,128)}), f32[1024,128]{1,0:T(8,128)}) %reduce-scatter.6.cloned.1.call-update) | async-done | bytes 524304 | tf_op jit(solution)/shard_map/reduce_scatter | solution.py:321
  1361.9 248.2 %reduce-scatter.8.cloned.1.call-done = f32[1408,128]{1,0:T(8,128)} async-done(((f32[45056,128]{1,0:T(8,128)}), f32[1408,128]{1,0:T(8,128)}) %reduce-scatter.8.cloned.1.call-update) | async-done | bytes 720912 | tf_op jit(solution)/shard_map/reduce_scatter | solution.py:322
  1614.7 44.6 %psum.7 = f32[]{:T(128)} all-reduce(f32[]{:T(128)S(6)} %add.212), channel_id=1, replica_groups=mesh['dp'=16,'fsdp'=2] {'dp','fsdp'}, use_global_device_ids=true, to_apply=%region_27.28 | all-reduce | flops 1 | bytes 8 | tf_op jit(solution)/shard_map/psum | solution.py:333
  (633 shorter events, 414.6 us)
Async XLA Ops:
  12.5 88.7 %copy-start.10 = (bf16[1024,176]{0,1:T(8,128)(2,1)}, bf16[1024,176]{0,1:T(8,128)(2,1)S(1)}, u32[]{:S(2)}) copy-start(bf16[1024,176]{0,1:T(8,128)(2,1)S(1)} %get-tuple-element.921) | copy-start | bytes 1081348 | tf_op jit(solution)/shard_map/while
  12.5 88.7 %copy-start.14 = (bf16[88,1024]{1,0:T(8,128)(2,1)}, bf16[88,1024]{1,0:T(8,128)(2,1)S(1)}, u32[]{:S(2)}) copy-start(bf16[88,1024]{1,0:T(8,128)(2,1)S(1)} %get-tuple-element.922) | copy-start | bytes 540676 | tf_op jit(solution)/shard_map/while
  12.5 85.2 %all-gather.14.cloned.1.call-start = ((), (), s32[]{:S(2)}) async-start(), calls=%async_computation.8 | async-start | bytes 8650752 | tf_op jit(solution)/shard_map/while/body/eval_jaxpr/all_gather | solution.py:300
  13.3 103.9 %all-gather.16.cloned.1.call-start = ((), (), s32[]{:S(2)}) async-start(), calls=%async_computation.9 | async-start | bytes 3538944 | tf_op jit(solution)/shard_map/while/body/eval_jaxpr/all_gather | solution.py:187
  58.3 42.9 %copy-start.20 = (f32[576]{0:T(1024)}, f32[576]{0:T(1024)S(1)}, u32[]{:S(2)}) copy-start(f32[576]{0:T(1024)S(1)} %fusion.171) | copy-start | bytes 6916 | tf_op jit(solution)/shard_map/while
  58.3 42.9 %copy-start.28 = (f32[576]{0:T(1024)}, f32[576]{0:T(1024)S(1)}, u32[]{:S(2)}) copy-start(f32[576]{0:T(1024)S(1)} %fusion.172) | copy-start | bytes 6916 | tf_op jit(solution)/shard_map/while
  58.4 42.9 %copy-start.26 = (f32[1024]{0:T(1024)}, f32[1024]{0:T(1024)S(1)}, u32[]{:S(2)}) copy-start(f32[1024]{0:T(1024)S(1)} %get-tuple-element.750) | copy-start | bytes 12292 | tf_op jit(solution)/shard_map/while
  58.4 42.9 %copy-start.3 = (bf16[2,576,1024]{2,1,0:T(8,128)(2,1)S(1)}, bf16[2,576,1024]{2,1,0:T(8,128)(2,1)}, u32[]{:S(2)}) copy-start(bf16[2,576,1024]{2,1,0:T(8,128)(2,1)} %get-tuple-element.915) | copy-start | bytes 7077892 | tf_op jit(solution)/shard_map/while
  107.4 23.4 %all-gather.18.cloned.1.call-start = ((), (), s32[]{:S(2)}) async-start(), calls=%async_computation.10 | async-start | bytes 3538944 | tf_op jit(solution)/shard_map/while/body/eval_jaxpr/all_gather | solution.py:186
  108.2 118.3 %all-gather.20.cloned.1.call-start = ((), (), s32[]{:S(2)}) async-start(), calls=%async_computation.11 | async-start | bytes 11894784 | tf_op jit(solution)/shard_map/while/body/eval_jaxpr/all_gather | solution.py:301
  108.7 186.7 %all-gather.22.cloned.1.call-start = ((), (), s32[]{:S(2)}) async-start(), calls=%async_computation.12 | async-start | bytes 5947392 | tf_op jit(solution)/shard_map/while/body/eval_jaxpr/all_gather | solution.py:309
  109.3 362.9 %reduce-scatter.12.cloned.1.call-start = ((), (), s32[]{:S(2)}) async-start(), calls=%async_computation.13 | async-start | bytes 3538944 | tf_op jit(solution)/shard_map/while/body/eval_jaxpr/reduce_scatter | solution.py:265
  200.8 123.8 %copy-start.30 = (f32[576]{0:T(1024)}, f32[576]{0:T(1024)S(1)}, u32[]{:S(2)}) copy-start(f32[576]{0:T(1024)S(1)} %fusion.175) | copy-start | bytes 6916 | tf_op jit(solution)/shard_map/while
  295.4 16.1 copy-start.5
  311.5 13.1 copy-start.43
  311.5 13.1 copy-start.44
  311.5 13.1 copy-start.8
  427.3 44.9 %reduce-scatter.14.cloned.1.call-start = ((), (), s32[]{:S(2)}) async-start(), calls=%async_computation.14 | async-start | bytes 3538944 | tf_op jit(solution)/shard_map/while/body/eval_jaxpr/reduce_scatter | solution.py:262
  456.1 16.2 copy-start.27
  456.1 16.2 copy-start.29
  492.2 10.9 copy-start.7
  506.0 85.1 %copy-start.10 = (bf16[1024,176]{0,1:T(8,128)(2,1)}, bf16[1024,176]{0,1:T(8,128)(2,1)S(1)}, u32[]{:S(2)}) copy-start(bf16[1024,176]{0,1:T(8,128)(2,1)S(1)} %get-tuple-element.921) | copy-start | bytes 1081348 | tf_op jit(solution)/shard_map/while
  506.0 85.1 %copy-start.14 = (bf16[88,1024]{1,0:T(8,128)(2,1)}, bf16[88,1024]{1,0:T(8,128)(2,1)S(1)}, u32[]{:S(2)}) copy-start(bf16[88,1024]{1,0:T(8,128)(2,1)S(1)} %get-tuple-element.922) | copy-start | bytes 540676 | tf_op jit(solution)/shard_map/while
  506.0 81.6 %all-gather.14.cloned.1.call-start = ((), (), s32[]{:S(2)}) async-start(), calls=%async_computation.8 | async-start | bytes 8650752 | tf_op jit(solution)/shard_map/while/body/eval_jaxpr/all_gather | solution.py:300
  506.8 100.2 %all-gather.16.cloned.1.call-start = ((), (), s32[]{:S(2)}) async-start(), calls=%async_computation.9 | async-start | bytes 3538944 | tf_op jit(solution)/shard_map/while/body/eval_jaxpr/all_gather | solution.py:187
  549.6 41.5 %copy-start.20 = (f32[576]{0:T(1024)}, f32[576]{0:T(1024)S(1)}, u32[]{:S(2)}) copy-start(f32[576]{0:T(1024)S(1)} %fusion.171) | copy-start | bytes 6916 | tf_op jit(solution)/shard_map/while
  549.6 41.5 %copy-start.28 = (f32[576]{0:T(1024)}, f32[576]{0:T(1024)S(1)}, u32[]{:S(2)}) copy-start(f32[576]{0:T(1024)S(1)} %fusion.172) | copy-start | bytes 6916 | tf_op jit(solution)/shard_map/while
  549.6 41.5 %copy-start.26 = (f32[1024]{0:T(1024)}, f32[1024]{0:T(1024)S(1)}, u32[]{:S(2)}) copy-start(f32[1024]{0:T(1024)S(1)} %get-tuple-element.750) | copy-start | bytes 12292 | tf_op jit(solution)/shard_map/while
  549.7 41.5 %copy-start.3 = (bf16[2,576,1024]{2,1,0:T(8,128)(2,1)S(1)}, bf16[2,576,1024]{2,1,0:T(8,128)(2,1)}, u32[]{:S(2)}) copy-start(bf16[2,576,1024]{2,1,0:T(8,128)(2,1)} %get-tuple-element.915) | copy-start | bytes 7077892 | tf_op jit(solution)/shard_map/while
  597.3 23.3 %all-gather.18.cloned.1.call-start = ((), (), s32[]{:S(2)}) async-start(), calls=%async_computation.10 | async-start | bytes 3538944 | tf_op jit(solution)/shard_map/while/body/eval_jaxpr/all_gather | solution.py:186
  597.9 118.5 %all-gather.20.cloned.1.call-start = ((), (), s32[]{:S(2)}) async-start(), calls=%async_computation.11 | async-start | bytes 11894784 | tf_op jit(solution)/shard_map/while/body/eval_jaxpr/all_gather | solution.py:301
  598.6 186.6 %all-gather.22.cloned.1.call-start = ((), (), s32[]{:S(2)}) async-start(), calls=%async_computation.12 | async-start | bytes 5947392 | tf_op jit(solution)/shard_map/while/body/eval_jaxpr/all_gather | solution.py:309
  599.2 371.6 %reduce-scatter.12.cloned.1.call-start = ((), (), s32[]{:S(2)}) async-start(), calls=%async_computation.13 | async-start | bytes 3538944 | tf_op jit(solution)/shard_map/while/body/eval_jaxpr/reduce_scatter | solution.py:265
  690.5 124.3 %copy-start.30 = (f32[576]{0:T(1024)}, f32[576]{0:T(1024)S(1)}, u32[]{:S(2)}) copy-start(f32[576]{0:T(1024)S(1)} %fusion.175) | copy-start | bytes 6916 | tf_op jit(solution)/shard_map/while
  785.2 16.4 copy-start.5
  801.7 13.1 copy-start.43
  801.7 13.1 copy-start.44
  801.7 13.1 copy-start.8
  917.4 53.4 %reduce-scatter.14.cloned.1.call-start = ((), (), s32[]{:S(2)}) async-start(), calls=%async_computation.14 | async-start | bytes 3538944 | tf_op jit(solution)/shard_map/while/body/eval_jaxpr/reduce_scatter | solution.py:262
  938.3 10.4 copy-start.6
  948.8 22.1 %copy-start.27 = (f32[1024]{0:T(1024)S(1)}, f32[1024]{0:T(1024)}, u32[]{:S(2)}) copy-start(f32[1024]{0:T(1024)} %copy-done.26) | copy-start | bytes 12292 | tf_op jit(solution)/shard_map/while
  948.8 22.1 %copy-start.29 = (f32[576]{0:T(1024)S(1)}, f32[576]{0:T(1024)}, u32[]{:S(2)}) copy-start(f32[576]{0:T(1024)} %copy-done.28) | copy-start | bytes 6916 | tf_op jit(solution)/shard_map/while
  990.8 14.0 copy-start.7
  1011.6 167.5 %reduce-scatter.10.cloned.1.call-start = ((), (), s32[]{:S(2)}) async-start(), calls=%async_computation.7 | async-start | bytes 11894784 | tf_op jit(solution)/shard_map/reduce_scatter | solution.py:323
  1025.0 335.1 %reduce-scatter.6.cloned.1.call-start = ((), (), s32[]{:S(2)}) async-start(), calls=%async_computation.5 | async-start | bytes 17301504 | tf_op jit(solution)/shard_map/reduce_scatter | solution.py:321
  1043.1 567.0 %reduce-scatter.8.cloned.1.call-start = ((), (), s32[]{:S(2)}) async-start(), calls=%async_computation.6 | async-start | bytes 23789568 | tf_op jit(solution)/shard_map/reduce_scatter | solution.py:322
  1361.9 300.1 %copy-start.19 = (f32[1024,128]{1,0:T(8,128)S(1)}, f32[1024,128]{1,0:T(8,128)}, u32[]{:S(2)}) copy-start(f32[1024,128]{1,0:T(8,128)} %reduce-scatter.6.cloned.1.call-done) | copy-start | bytes 1572868
  1610.1 51.7 %copy-start.17 = (f32[1408,128]{1,0:T(8,128)S(1)}, f32[1408,128]{1,0:T(8,128)}, u32[]{:S(2)}) copy-start(f32[1408,128]{1,0:T(8,128)} %reduce-scatter.8.cloned.1.call-done) | copy-start | bytes 2162692
  (47 other events, 202.7 us)
Sparse Core Ops, SparseCore 0:
  16.8 80.9 all-gather.13
  107.5 9.5 all-gather.15
  118.7 12.1 all-gather.17
  134.1 92.3 all-gather.19
  229.8 65.6 all-gather.21
  427.5 8.8 reduce-scatter.11
  438.7 11.0 reduce-scatter.13
  510.3 77.2 all-gather.13
  597.4 9.5 all-gather.15
  608.4 12.1 all-gather.17
  624.0 92.3 all-gather.19
  719.6 65.5 all-gather.21
  917.5 8.8 reduce-scatter.11
  928.6 11.0 reduce-scatter.13
Sparse Core Ops, SparseCore 1:
  1025.0 154.0 reduce-scatter.9
  1181.2 178.8 reduce-scatter.5
  1362.3 247.8 reduce-scatter.7
where the time goes:
time: 1680 us
  waiting for transfers between devices  772 us (46%)
  matrix products  350 us (21%)
  local copies, waits for them, and re-layouts  247 us (15%)
  blocking collectives  170 us (10%)
  other arithmetic  110 us (7%)
  between operations  20.4 us (1%)
    reduce_scatter x1, waiting for transfers between devices, local(): lax.psum_scatter(flat_list[1], ('dp', 'fsdp'), scatter_dimension=0, tiled...  248 us
    reduce_scatter x1, waiting for transfers between devices, local(): lax.psum_scatter(flat_list[0], ('dp', 'fsdp'), scatter_dimension=0, tiled...  179 us
    all_gather x2, waiting for transfers between devices, micro_step(): lax.all_gather(narrow_low, ('dp', 'fsdp'), axis=0, tiled=True)  111 us
    while x2, blocking collectives  82.8 us
    dynamic_slice x96, local copies, waits for them, and re-layouts, forward(): lax.map(lambda pieces: pair_forward(pieces[0], pieces[1], pieces[2], same...  77.6 us
    all_gather x2, waiting for transfers between devices, micro_step(): lax.all_gather(attention_low, ('dp', 'fsdp'), axis=0, tiled=True)  77.3 us
    reduce_scatter x1, waiting for transfers between devices, local(): lax.psum_scatter(flat_list[2], ('dp', 'fsdp'), scatter_dimension=0, tiled...  67.6 us
    dot_general x6, matrix products, contract_rows(): lax.dot_general(left, right, (((0,), (0,)), ((), ())), preferred_element_...  66.5 us
  transfers between devices with their start and end apart: 17, of which 13 were waited for; matrix products, arithmetic and copies ran while one was open for 19% of the time, Pallas kernels for 0%

commit v1 on v0

v1 whole, which is shorter than its diff:
```python
import functools

import jax
import jax.numpy as jnp
from jax import lax
from jax.experimental import pallas as pl
from jax.experimental.pallas import tpu as pltpu
from jax.sharding import PartitionSpec as P

HD = 64
TEXT = 128
PATCH = 256
ROW = 1152
WIDTH = 1024
HALF = ROW // 2
TILE = 384
WINDOWS = ((0, 640), (0, 1024), (384, 1152))
FF_BLOCK = 256

NORM_EPS = 1e-06
MASKED = -1000000000.0
BETA_FIRST = 0.9
BETA_SECOND = 0.999
ADAM_EPS = 1e-08
MATRIX_RATE = 0.05
GAIN_RATE = 0.3
DECAY = 0.1
CLIP_LIMIT = 1.0
STEP_VALUE = 10.0
GELU_SCALE = 0.7978845608028654
GELU_CUBE = 0.044715

BF16 = jnp.bfloat16
F32 = jnp.float32
MESH = pl.DeviceIdType.MESH
ANY = pl.BlockSpec(memory_space=pl.ANY)
VMEM_WHOLE = pl.BlockSpec(memory_space=pltpu.VMEM)
DMA = pltpu.SemaphoreType.DMA
VMEM_LIMIT = 60 * 2**20

NT = (((1,), (1,)), ((), ()))
TN = (((0,), (0,)), ((), ()))


def dot(left, right, dims=(((1,), (0,)), ((), ()))):
    return lax.dot_general(left, right, dims, preferred_element_type=F32)


class Place:
    def __init__(self):
        self.dp = lax.axis_index("dp")
        self.core = lax.axis_index("fsdp")
        self.z = self.dp // 4
        self.y = lax.rem(self.dp // 2, 2)
        self.x = lax.rem(self.dp, 2)
        flip_y = 1 - self.y
        flip_x = 1 - self.x
        is_zero = self.core == 0
        self.own = (self.y, self.x)
        self.first = (jnp.where(is_zero, self.y, flip_y), jnp.where(is_zero, flip_x, self.x))
        self.second = (jnp.where(is_zero, flip_y, self.y), jnp.where(is_zero, self.x, flip_x))
        self.across = (flip_y, flip_x)

    def at(self, z, spot):
        return (z * 4 + spot[0] * 2 + spot[1], self.core)

    def above(self, step):
        return self.at(lax.rem(self.z + step, 4), self.own)

    def to_first(self):
        return self.at(self.z, self.first)

    def to_second(self):
        return self.at(self.z, self.second)

    def sibling(self):
        return (self.dp, 1 - self.core)

    def greet(self):
        barrier = pltpu.get_barrier_semaphore()
        peers = [self.above(1), self.above(2), self.above(3)]
        peers += [self.to_first(), self.to_second(), self.sibling()]
        for peer in peers:
            pl.semaphore_signal(barrier, inc=1, device_id=peer, device_id_type=MESH)
        pl.semaphore_wait(barrier, len(peers))


def remote(source, target, send_sem, recv_sem, device):
    return pltpu.make_async_remote_copy(
        src_ref=source,
        dst_ref=target,
        send_sem=send_sem,
        recv_sem=recv_sem,
        device_id=device,
        device_id_type=MESH,
    )


def gather_kernel(chunks, arrays, *refs):
    ins = refs[:arrays]
    tokens, cotangent = refs[arrays : arrays + 2]
    outs = refs[arrays + 2 : 2 * arrays + 2]
    tokens_row, cotangent_row = refs[2 * arrays + 2 : 2 * arrays + 4]
    (own_sem, z_send, z_recv, p_send, p_recv, c_send, c_recv, t_own, t_send, t_recv) = refs[
        2 * arrays + 4 :
    ]
    here = Place()
    here.greet()
    count = len(chunks)
    core = here.core

    halves = []
    for index, (source, target) in enumerate(
        ((tokens, tokens_row), (cotangent, cotangent_row))
    ):
        halves.append(
            (
                pltpu.make_async_copy(source.at[core], target.at[core], t_own.at[index]),
                remote(
                    source.at[1 - core],
                    target.at[core],
                    t_send.at[index],
                    t_recv.at[index],
                    here.sibling(),
                ),
            )
        )

    def spot(k, where):
        array, start, rows = chunks[k]
        return outs[array].at[:, where[0], where[1], core, pl.ds(start, rows), :]

    def mine(k):
        array, start, rows = chunks[k]
        return (
            ins[array].at[pl.ds(start, rows), :],
            outs[array].at[here.z, here.y, here.x, core, pl.ds(start, rows), :],
        )

    def keep(k):
        source, target = mine(k)
        return pltpu.make_async_copy(source, target, own_sem.at[k])

    def along_z(k, step):
        source, target = mine(k)
        return remote(
            source, target, z_send.at[k, step - 1], z_recv.at[k, step - 1], here.above(step)
        )

    def plane(k, index, where, device):
        return remote(
            spot(k, where), spot(k, where), p_send.at[k, index], p_recv.at[k, index], device
        )

    def to_first(k):
        return plane(k, 0, here.own, here.to_first())

    def to_second(k):
        return plane(k, 1, here.own, here.to_second())

    def pass_on(k):
        return plane(k, 2, here.first, here.to_second())

    columns = (here.own, here.first, here.second, here.across)

    def to_sibling(k, index):
        where = columns[index]
        return remote(
            spot(k, where), spot(k, where), c_send.at[k, index], c_recv.at[k, index], here.sibling()
        )

    for tick in range(count + 3):
        if tick < count:
            keep(tick).start()
            for step in (2, 1, 3):
                along_z(tick, step).start()
        if tick == 0:
            for local, across in halves:
                across.start()
                local.start()
        k = tick - 1
        if 0 <= k < count:
            keep(k).wait()
            for step in (1, 2, 3):
                along_z(k, step).wait_recv()
            to_second(k).start()
            to_first(k).start()
            to_sibling(k, 0).start()
        k = tick - 2
        if 0 <= k < count:
            to_first(k).wait_recv()
            pass_on(k).start()
            to_sibling(k, 1).start()
            to_second(k).wait_recv()
            to_sibling(k, 2).start()
        k = tick - 3
        if 0 <= k < count:
            pass_on(k).wait_recv()
            to_sibling(k, 3).start()
    for k in range(count):
        for step in (1, 2, 3):
            along_z(k, step).wait_send()
        to_first(k).wait_send()
        to_second(k).wait_send()
        pass_on(k).wait_send()
        for index in range(4):
            to_sibling(k, index).wait()
    for local, across in halves:
        local.wait()
        across.wait()


def cut(index, rows, most):
    pieces = -(-rows // most)
    step = -(-rows // (pieces * 16)) * 16
    return [(index, at, min(step, rows - at)) for at in range(0, rows, step)]


def gather_all(shards, tokens, cotangent, most=48):
    chunks = []
    for index, shard in enumerate(shards):
        chunks += cut(index, shard.shape[0], most)
    count = len(chunks)
    gathered = [jax.ShapeDtypeStruct((4, 2, 2, 2) + s.shape, s.dtype) for s in shards]
    rows = jax.ShapeDtypeStruct((2, HALF, WIDTH), BF16)
    results = pl.pallas_call(
        functools.partial(gather_kernel, chunks, len(shards)),
        out_shape=gathered + [rows, rows],
        in_specs=[ANY] * (len(shards) + 2),
        out_specs=[ANY] * (len(shards) + 2),
        scratch_shapes=[
            DMA((count,)),
            DMA((count, 3)),
            DMA((count, 3)),
            DMA((count, 3)),
            DMA((count, 3)),
            DMA((count, 4)),
            DMA((count, 4)),
            DMA((2,)),
            DMA((2,)),
            DMA((2,)),
        ],
        compiler_params=pltpu.CompilerParams(collective_id=0, has_side_effects=True),
        name="gather_weights",
    )(*shards, tokens, cotangent)
    return results[:-2], results[-2], results[-1]


def reduce_kernel(chunks, arrays, *refs):
    ins = refs[:arrays]
    gains, result, forward = refs[arrays : arrays + 3]
    outs = refs[arrays + 3 : 2 * arrays + 3]
    gains_out, square_out, result_out, forward_out = refs[2 * arrays + 3 : 2 * arrays + 7]
    own = refs[2 * arrays + 7 : 3 * arrays + 7]
    from_core = refs[3 * arrays + 7 : 4 * arrays + 7]
    from_second = refs[4 * arrays + 7 : 5 * arrays + 7]
    from_first = refs[5 * arrays + 7 : 6 * arrays + 7]
    from_z = refs[6 * arrays + 7 : 7 * arrays + 7]
    (
        small,
        tiny,
        own_sem,
        c_send,
        c_recv,
        p_send,
        p_recv,
        z_send,
        z_recv,
        g_send,
        g_recv,
        n_send,
        n_recv,
        t_own,
        t_send,
        t_recv,
    ) = refs[7 * arrays + 7 :]
    here = Place()
    here.greet()
    count = len(chunks)
    core = here.core

    halves = []
    for index, (source, target) in enumerate(((result, result_out), (forward, forward_out))):
        halves.append(
            (
                pltpu.make_async_copy(source.at[core], target.at[core], t_own.at[index]),
                remote(
                    source.at[1 - core],
                    target.at[core],
                    t_send.at[index],
                    t_recv.at[index],
                    here.sibling(),
                ),
            )
        )

    def part(k):
        array, start, rows = chunks[k]
        return array, pl.ds(start, rows)

    def load(k):
        array, rows = part(k)
        return pltpu.make_async_copy(
            ins[array].at[:, :, :, core, rows, :], own[array].at[:, :, :, rows, :], own_sem.at[k]
        )

    def swap_core(k):
        array, rows = part(k)
        return remote(
            ins[array].at[:, :, :, 1 - core, rows, :],
            from_core[array].at[:, :, :, rows, :],
            c_send.at[k],
            c_recv.at[k],
            here.sibling(),
        )

    def send_second(k, index):
        array, rows = part(k)
        where = here.second if index == 0 else here.across
        return remote(
            own[array].at[:, where[0], where[1], rows, :],
            from_second[array].at[index, :, rows, :],
            p_send.at[k, index],
            p_recv.at[k, index],
            here.to_second(),
        )

    def send_first(k):
        array, rows = part(k)
        return remote(
            own[array].at[:, here.first[0], here.first[1], rows, :],
            from_first[array].at[:, rows, :],
            p_send.at[k, 2],
            p_recv.at[k, 2],
            here.to_first(),
        )

    def send_z(k, step):
        array, rows = part(k)
        other = lax.rem(here.z + step, 4)
        return remote(
            own[array].at[other, here.y, here.x, rows, :],
            from_z[array].at[step - 1, rows, :],
            z_send.at[k, step - 1],
            z_recv.at[k, step - 1],
            here.above(step),
        )

    def add(mine, other):
        return (mine.astype(F32) + other.astype(F32)).astype(BF16)

    def after_core(k):
        array, rows = part(k)

        def body(i, carry):
            z, y, x = i // 4, lax.rem(i // 2, 2), lax.rem(i, 2)
            own[array][z, y, x, rows, :] = add(
                own[array][z, y, x, rows, :], from_core[array][z, y, x, rows, :]
            )
            return carry

        lax.fori_loop(0, 16, body, 0)

    def after_second(k, index):
        array, rows = part(k)
        where = here.own if index == 0 else here.first

        def body(z, carry):
            own[array][z, where[0], where[1], rows, :] = add(
                own[array][z, where[0], where[1], rows, :], from_second[array][index, z, rows, :]
            )
            return carry

        lax.fori_loop(0, 4, body, 0)

    def after_first(k):
        array, rows = part(k)

        def body(z, carry):
            own[array][z, here.y, here.x, rows, :] = add(
                own[array][z, here.y, here.x, rows, :], from_first[array][z, rows, :]
            )
            return carry

        lax.fori_loop(0, 4, body, 0)

    def after_z(k):
        array, rows = part(k)
        total = own[array][here.z, here.y, here.x, rows, :].astype(F32)
        for step in range(3):
            total = total + from_z[array][step, rows, :].astype(F32)
        outs[array][rows, :] = total
        return jnp.sum((total * total).reshape(-1, 8, 128), axis=0)

    def everywhere(buffer, value, send, recv):
        stages = (here.sibling(), here.to_first(), here.to_second())
        for index, device in enumerate(stages):
            buffer[2 * index] = value
            copy = remote(
                buffer.at[2 * index],
                buffer.at[2 * index + 1],
                send.at[index],
                recv.at[index],
                device,
            )
            copy.start()
            yield
            copy.wait()
            value = buffer[2 * index] + buffer[2 * index + 1]
        buffer[6 + here.z] = value
        copies = [
            remote(
                buffer.at[6 + here.z],
                buffer.at[6 + here.z],
                send.at[2 + step],
                recv.at[2 + step],
                here.above(step),
            )
            for step in (1, 2, 3)
        ]
        for copy in copies:
            copy.start()
        yield
        for copy in copies:
            copy.wait()
        yield (buffer[6] + buffer[7]) + (buffer[8] + buffer[9])

    squares = jnp.zeros((8, 128), F32)
    gains_steps = everywhere(small, gains[...], g_send, g_recv)
    for tick in range(count + 4):
        if tick < count:
            swap_core(tick).start()
            load(tick).start()
        if tick == 1:
            for local, across in halves:
                across.start()
                local.start()
        k = tick - 1
        if 0 <= k < count:
            load(k).wait()
            swap_core(k).wait_recv()
            after_core(k)
            for index in (1, 0):
                send_second(k, index).start()
        k = tick - 2
        if 0 <= k < count:
            send_second(k, 1).wait_recv()
            after_second(k, 1)
            send_first(k).start()
            send_second(k, 0).wait_recv()
            after_second(k, 0)
        k = tick - 3
        if 0 <= k < count:
            send_first(k).wait_recv()
            after_first(k)
            for step in (2, 1, 3):
                send_z(k, step).start()
        k = tick - 4
        if 0 <= k < count:
            for step in (1, 2, 3):
                send_z(k, step).wait_recv()
            squares = squares + after_z(k)
        if tick < 5:
            gains_total = next(gains_steps)
    gains_out[...] = gains_total
    norm_steps = everywhere(tiny, squares, n_send, n_recv)
    for _ in range(5):
        total = next(norm_steps)
    square_out[...] = jnp.broadcast_to(
        jnp.sum(total) + jnp.sum(gains_total * gains_total), (8, 128)
    )
    for k in range(count):
        swap_core(k).wait_send()
        for index in (1, 0):
            send_second(k, index).wait_send()
        send_first(k).wait_send()
        for step in (1, 2, 3):
            send_z(k, step).wait_send()
    for local, across in halves:
        local.wait()
        across.wait()


def reduce_all(gradients, gains, result, forward, most=48):
    chunks = []
    for index, gradient in enumerate(gradients):
        chunks += cut(index, gradient.shape[4], most)
    count, arrays = len(chunks), len(gradients)
    shapes = [g.shape[4:] for g in gradients]
    padded = [(-(-s[0] // 16) * 16, s[1]) for s in shapes]
    exchanged = jax.ShapeDtypeStruct((2, HALF, WIDTH), F32)
    scratch = [pltpu.VMEM((4, 2, 2) + s, BF16) for s in padded]
    scratch += [pltpu.VMEM((4, 2, 2) + s, BF16) for s in padded]
    scratch += [pltpu.VMEM((2, 4) + s, BF16) for s in padded]
    scratch += [pltpu.VMEM((4,) + s, BF16) for s in padded]
    scratch += [pltpu.VMEM((3,) + s, BF16) for s in padded]
    scratch += [
        pltpu.VMEM((10, 16, 128), F32),
        pltpu.VMEM((10, 8, 128), F32),
        DMA((count,)),
        DMA((count,)),
        DMA((count,)),
        DMA((count, 3)),
        DMA((count, 3)),
        DMA((count, 3)),
        DMA((count, 3)),
        DMA((6,)),
        DMA((6,)),
        DMA((6,)),
        DMA((6,)),
        DMA((2,)),
        DMA((2,)),
        DMA((2,)),
    ]
    return pl.pallas_call(
        functools.partial(reduce_kernel, chunks, arrays),
        out_shape=[jax.ShapeDtypeStruct(s, F32) for s in shapes]
        + [
            jax.ShapeDtypeStruct((16, 128), F32),
            jax.ShapeDtypeStruct((8, 128), F32),
            exchanged,
            exchanged,
        ],
        in_specs=[ANY] * arrays + [VMEM_WHOLE, ANY, ANY],
        out_specs=[VMEM_WHOLE] * arrays + [VMEM_WHOLE, VMEM_WHOLE, ANY, ANY],
        scratch_shapes=scratch,
        compiler_params=pltpu.CompilerParams(
            collective_id=1, has_side_effects=True, vmem_limit_bytes=VMEM_LIMIT
        ),
        name="reduce_gradients",
    )(*gradients, gains, result, forward)


def item_ends(counts):
    sizes = [jnp.where(counts[i] > 0, TEXT + PATCH * counts[i], 0) for i in range(3)]
    return sizes[0], sizes[0] + sizes[1], sizes[0] + sizes[1] + sizes[2]


def segments(ends, start, size, axis):
    shape = (size, 1) if axis == 0 else (1, size)
    place = start + lax.broadcasted_iota(jnp.int32, shape, axis)
    one = jnp.ones(shape, jnp.int32)
    none = jnp.zeros(shape, jnp.int32)
    return sum(jnp.where(place >= end, one, none) for end in ends)


def attend_kernel(counts, q_ref, k_ref, v_ref, o_ref, log_ref):
    pair = pl.program_id(0)
    ends = item_ends(counts)
    lane = lax.broadcasted_iota(jnp.int32, (1, 2 * HD), 1)
    in_head = (lane < HD, lane >= HD)

    @pl.when(pair == 0)
    def _():
        log_ref[...] = jnp.zeros_like(log_ref)

    def run(masked):
        for index in range(ROW // TILE):
            low, high = WINDOWS[index] if masked else (0, ROW)
            rows = pl.ds(index * TILE, TILE)
            query = q_ref[0, rows, :]
            key = k_ref[0, low:high, :]
            value = v_ref[0, low:high, :]
            if masked:
                same = segments(ends, index * TILE, TILE, 0) == segments(ends, low, high - low, 1)
            mixed = []
            logs = log_ref[rows, :]
            for head in range(2):
                scores = dot(jnp.where(in_head[head], query, jnp.zeros_like(query)), key, NT)
                if masked:
                    scores = jnp.where(same, scores, MASKED)
                top = jnp.max(scores, axis=-1, keepdims=True)
                weight = jnp.exp(scores - top).astype(BF16)
                both = dot(weight, jnp.where(in_head[head], value, jnp.ones_like(value)))
                other = pltpu.roll(both, HD, 1)
                mixed.append(both / other)
                total = jnp.where(in_head[head], other, both)
                logs = jnp.where(lane == 2 * pair + head, top + jnp.log(total), logs)
            log_ref[rows, :] = logs
            o_ref[rows, :] = jnp.where(in_head[0], mixed[0], mixed[1]).astype(BF16)

    whole = ends[0] == ROW

    @pl.when(whole)
    def _():
        run(False)

    @pl.when(jnp.logical_not(whole))
    def _():
        run(True)


def attend(counts, projected):
    pairs = WIDTH // (2 * HD)

    def pick(which):
        return pl.BlockSpec((1, ROW, 2 * HD), lambda p, c, which=which: (which, 0, p))

    return pl.pallas_call(
        attend_kernel,
        out_shape=[
            jax.ShapeDtypeStruct((ROW, WIDTH), BF16),
            jax.ShapeDtypeStruct((ROW, 128), F32),
        ],
        grid_spec=pltpu.PrefetchScalarGridSpec(
            num_scalar_prefetch=1,
            grid=(pairs,),
            in_specs=[pick(0), pick(1), pick(2)],
            out_specs=[
                pl.BlockSpec((ROW, 2 * HD), lambda p, c: (0, p)),
                pl.BlockSpec((ROW, 128), lambda p, c: (0, 0)),
            ],
        ),
        compiler_params=pltpu.CompilerParams(vmem_limit_bytes=VMEM_LIMIT),
        name="attend",
    )(counts, projected, projected, projected)


def attend_back_kernel(counts, q_ref, k_ref, v_ref, o_ref, do_ref, log_ref, out_ref, dk, dv):
    pair = pl.program_id(0)
    ends = item_ends(counts)
    lane = lax.broadcasted_iota(jnp.int32, (1, 2 * HD), 1)
    in_head = (lane < HD, lane >= HD)
    pick = jnp.where(
        (lax.broadcasted_iota(jnp.int32, (8, 2 * HD), 1) < HD)
        == (lax.broadcasted_iota(jnp.int32, (8, 2 * HD), 0) == 0),
        jnp.ones((8, 2 * HD), F32),
        jnp.zeros((8, 2 * HD), F32),
    )

    def only(values, head):
        return jnp.where(in_head[head], values, jnp.zeros_like(values))

    def run(masked):
        dk[...] = jnp.zeros_like(dk)
        dv[...] = jnp.zeros_like(dv)
        for index in range(ROW // TILE):
            low, high = WINDOWS[index] if masked else (0, ROW)
            rows = pl.ds(index * TILE, TILE)
            query = q_ref[0, rows, :]
            grad = do_ref[rows, :]
            key = k_ref[0, low:high, :]
            value = v_ref[0, low:high, :]
            inner = lax.dot_general(
                pick,
                grad.astype(F32) * o_ref[rows, :].astype(F32),
                NT,
                precision=lax.Precision.HIGHEST,
                preferred_element_type=F32,
            )
            if masked:
                same = segments(ends, low, high - low, 0) == segments(ends, index * TILE, TILE, 1)
            dq = None
            for head in range(2):
                log_total = log_ref[pl.ds(2 * pair + head, 1), index * TILE : (index + 1) * TILE]
                scores = dot(only(key, head), query, NT)
                if masked:
                    scores = jnp.where(same, scores, MASKED)
                weight = jnp.exp(scores - log_total)
                down = dot(only(value, head), grad, NT)
                slope = (weight * (down - inner[head : head + 1, :])).astype(BF16)
                dv[low:high, :] += dot(weight.astype(BF16), only(grad, head))
                dk[low:high, :] += dot(slope, only(query, head))
                step = dot(slope, only(key, head), TN)
                dq = step if dq is None else dq + step
            out_ref[0, rows, :] = dq.astype(BF16)
        out_ref[1] = dk[...].astype(BF16)
        out_ref[2] = dv[...].astype(BF16)

    whole = ends[0] == ROW

    @pl.when(whole)
    def _():
        run(False)

    @pl.when(jnp.logical_not(whole))
    def _():
        run(True)


def attend_back(counts, projected, mixed, grad_mixed, log_rows):
    pairs = WIDTH // (2 * HD)

    def pick(which):
        return pl.BlockSpec((1, ROW, 2 * HD), lambda p, c, which=which: (which, 0, p))

    column = pl.BlockSpec((ROW, 2 * HD), lambda p, c: (0, p))
    return pl.pallas_call(
        attend_back_kernel,
        out_shape=jax.ShapeDtypeStruct((3, ROW, WIDTH), BF16),
        grid_spec=pltpu.PrefetchScalarGridSpec(
            num_scalar_prefetch=1,
            grid=(pairs,),
            in_specs=[
                pick(0),
                pick(1),
                pick(2),
                column,
                column,
                pl.BlockSpec((2 * pairs, ROW), lambda p, c: (0, 0)),
            ],
            out_specs=pl.BlockSpec((3, ROW, 2 * HD), lambda p, c: (0, 0, p)),
            scratch_shapes=[pltpu.VMEM((ROW, 2 * HD), F32), pltpu.VMEM((ROW, 2 * HD), F32)],
        ),
        compiler_params=pltpu.CompilerParams(vmem_limit_bytes=VMEM_LIMIT),
        name="attend_back",
    )(counts, projected, projected, projected, mixed, grad_mixed, log_rows)


def feed_kernel(
    n2_ref, cot_ref, h1_ref, gain_ref, widen_ref, narrow_ref,
    result_ref, dh1_ref, e_ref, gain_grad_ref, widen_grad_ref, narrow_grad_ref,
    back,
):
    step = pl.program_id(0)
    n2 = n2_ref[...]
    cot = cot_ref[...]
    wide_gate, wide_up, narrow = widen_ref[0], widen_ref[1], narrow_ref[...]
    gate = dot(n2, wide_gate, NT)
    up = dot(n2, wide_up, NT)
    down = dot(cot, narrow, NT)
    square = gate * gate
    bend = jnp.tanh(GELU_SCALE * gate * (1.0 + GELU_CUBE * square))
    half = 0.5 * (1.0 + bend)
    curve = gate * half
    slope = half + 0.5 * gate * (1.0 - bend * bend) * (
        GELU_SCALE * (1.0 + 3.0 * GELU_CUBE * square)
    )
    hidden = (curve * up).astype(BF16)
    grad_gate = (down * up * slope).astype(BF16)
    grad_up = (down * curve).astype(BF16)
    narrow_grad_ref[...] = dot(hidden, cot, TN).astype(BF16)
    widen_grad_ref[0] = dot(grad_gate, n2, TN).astype(BF16)
    widen_grad_ref[1] = dot(grad_up, n2, TN).astype(BF16)

    @pl.when(step == 0)
    def _():
        result_ref[...] = h1_ref[...]
        back[...] = jnp.zeros_like(back)

    result_ref[...] += dot(hidden, narrow)
    back[...] += dot(grad_gate, wide_gate) + dot(grad_up, wide_up)

    @pl.when(step == pl.num_programs(0) - 1)
    def _():
        gain = gain_ref[...]

        def tile(i, total):
            rows = pl.ds(pl.multiple_of(i * 64, 64), 64)
            h1 = h1_ref[rows, :]
            grad = back[rows, :]
            scale = lax.rsqrt(jnp.mean(h1 * h1, axis=-1, keepdims=True) + NORM_EPS)
            lifted = gain * grad
            inner = jnp.mean(h1 * lifted, axis=-1, keepdims=True)
            dh1 = (
                cot_ref[rows, :].astype(F32)
                + scale * lifted
                - h1 * (scale * scale * scale * inner)
            )
            dh1_ref[rows, :] = dh1
            e_ref[rows, :] = dh1.astype(BF16)
            return total + jnp.sum((grad * h1 * scale).reshape(8, 8, WIDTH), axis=0)

        total = lax.fori_loop(0, ROW // 64, tile, jnp.zeros((8, WIDTH), F32))
        gain_grad_ref[...] = jnp.sum(total, axis=0, keepdims=True)


def feed(n2, cot, h1, gain, widen, narrow):
    hidden = narrow.shape[0]
    steps = hidden // FF_BLOCK
    whole = lambda *shape: pl.BlockSpec(shape, lambda j: (0,) * len(shape))
    once = lambda *shape: pl.BlockSpec(
        shape, lambda j: (0,) * len(shape), pipeline_mode=pl.Buffered(1)
    )
    wide = pl.BlockSpec((2, FF_BLOCK, WIDTH), lambda j: (0, j, 0))
    tall = pl.BlockSpec((FF_BLOCK, WIDTH), lambda j: (j, 0))
    return pl.pallas_call(
        feed_kernel,
        grid=(steps,),
        out_shape=[
            jax.ShapeDtypeStruct((ROW, WIDTH), F32),
            jax.ShapeDtypeStruct((ROW, WIDTH), F32),
            jax.ShapeDtypeStruct((ROW, WIDTH), BF16),
            jax.ShapeDtypeStruct((1, WIDTH), F32),
            jax.ShapeDtypeStruct((2, hidden, WIDTH), BF16),
            jax.ShapeDtypeStruct((hidden, WIDTH), BF16),
        ],
        in_specs=[
            once(ROW, WIDTH),
            once(ROW, WIDTH),
            once(ROW, WIDTH),
            whole(1, WIDTH),
            wide,
            tall,
        ],
        out_specs=[
            once(ROW, WIDTH),
            once(ROW, WIDTH),
            once(ROW, WIDTH),
            whole(1, WIDTH),
            wide,
            tall,
        ],
        scratch_shapes=[pltpu.VMEM((ROW, WIDTH), F32)],
        compiler_params=pltpu.CompilerParams(vmem_limit_bytes=VMEM_LIMIT),
        name="feed",
    )(n2, cot, h1, gain, widen, narrow)


def rms_scale(values, gain_vector):
    return (
        values
        * lax.rsqrt(jnp.mean(values * values, axis=-1, keepdims=True) + NORM_EPS)
        * gain_vector
    )


def layer(counts, inputs_low, cot, attention, widen, narrow, gains):
    first_gain = gains[:WIDTH].astype(F32)
    second_gain = gains[WIDTH:].astype(F32)
    inputs = inputs_low.astype(F32)
    normed = rms_scale(inputs, first_gain).astype(BF16)
    projected = jnp.einsum(
        "sd,jde->jse", normed, attention[:3], preferred_element_type=F32
    ).astype(BF16)
    mixed, log_columns = attend(counts, projected)
    log_rows = log_columns[:, : WIDTH // HD].T
    h1 = inputs + dot(mixed, attention[3])
    n2 = rms_scale(h1, second_gain).astype(BF16)
    result, dh1, e, grad_gain_two, grad_widen, grad_narrow = feed(
        n2, cot, h1, second_gain[None], widen, narrow
    )
    grad_out = dot(mixed, e, TN).astype(BF16)
    grad_mixed = dot(e, attention[3], NT).astype(BF16)
    grad_projected = attend_back(counts, projected, mixed, grad_mixed, log_rows)
    grad_qkv = jnp.einsum(
        "sd,jse->jde", normed, grad_projected, preferred_element_type=F32
    ).astype(BF16)
    grad_normed = jnp.einsum(
        "jse,jde->sd", grad_projected, attention[:3], preferred_element_type=F32
    )
    scale = lax.rsqrt(jnp.mean(inputs * inputs, axis=-1, keepdims=True) + NORM_EPS)
    lifted = first_gain * grad_normed
    inner = jnp.mean(inputs * lifted, axis=-1, keepdims=True)
    input_rows = dh1 + scale * lifted - inputs * (scale * scale * scale * inner)
    grad_gain_one = jnp.sum(grad_normed * inputs * scale, axis=0)
    grad_attention = jnp.concatenate([grad_qkv, grad_out[None]], axis=0)
    grad_gains = jnp.concatenate([grad_gain_one, grad_gain_two[0]])
    return result, input_rows, grad_attention, grad_widen, grad_narrow, grad_gains


def adam_update(master, first, second, gradient, factors, rate, decay):
    clip_factor, first_fix, second_fix = factors
    clipped = clip_factor * gradient
    first_new = BETA_FIRST * first + (1.0 - BETA_FIRST) * clipped
    second_new = BETA_SECOND * second + (1.0 - BETA_SECOND) * clipped * clipped
    master_new = master - rate * (
        first_new / first_fix / (jnp.sqrt(second_new / second_fix) + ADAM_EPS) + decay * master
    )
    return (master_new, first_new, second_new)


def swap_halves(parts):
    core = lax.axis_index("fsdp")
    got = lax.ppermute(parts[1 - core], "fsdp", [(0, 1), (1, 0)])
    return jnp.where(core == 0, jnp.stack([parts[0], got]), jnp.stack([got, parts[1]]))


def local(
    own_kernels,
    tokens,
    cotangent,
    images,
    attention_weight,
    attention_first,
    attention_second,
    widen_weight,
    widen_first,
    widen_second,
    narrow_weight,
    narrow_first,
    narrow_second,
    norm_gains,
    gains_first,
    gains_second,
):
    axes = ("dp", "fsdp")
    devices = lax.axis_size(axes)
    core = lax.axis_index("fsdp")
    position = lax.axis_index(axes)
    hidden_width = narrow_weight.shape[0] * devices
    gain_count = norm_gains.shape[0]
    attention_low = attention_weight.astype(BF16)
    widen_low = widen_weight.astype(BF16).T
    narrow_low = narrow_weight.astype(BF16)
    gains_low = norm_gains.astype(BF16)
    if own_kernels:
        gains_tile = jnp.zeros((16, 128), BF16).at[0, :gain_count].set(gains_low)
        (attention_full, widen_full, narrow_full, gains_full), tokens_row, cotangent_row = (
            gather_all((attention_low, widen_low, narrow_low, gains_tile), tokens, cotangent)
        )
        gains_full = gains_full.reshape(devices, 16, 128)[:, 0, :gain_count].reshape(-1)
    else:
        attention_full, widen_full, narrow_full, gains_full = (
            lax.all_gather(part, axes, axis=0, tiled=True)
            for part in (attention_low, widen_low, narrow_low, gains_low)
        )
        tokens_row, cotangent_row = swap_halves(tokens), swap_halves(cotangent)
    counts = lax.dynamic_index_in_dim(images[:, 0, :], core, 0, keepdims=False)
    result, input_rows, grad_attention, grad_widen, grad_narrow, grad_gains = layer(
        counts,
        tokens_row.reshape(ROW, WIDTH),
        cotangent_row.reshape(ROW, WIDTH),
        attention_full.reshape(4, WIDTH, WIDTH),
        widen_full.reshape(2, hidden_width, WIDTH),
        narrow_full.reshape(hidden_width, WIDTH),
        gains_full,
    )
    result = result.reshape(2, HALF, WIDTH)
    input_rows = input_rows.reshape(2, HALF, WIDTH)
    if own_kernels:
        grid = (4, 2, 2, 2)
        (
            narrow_sum,
            widen_sum,
            attention_sum,
            gains_total,
            square_total,
            block_output,
            input_grad,
        ) = reduce_all(
            (
                grad_narrow.reshape(grid + (-1, WIDTH)),
                grad_widen.reshape(grid + (-1, WIDTH)),
                grad_attention.reshape(grid + (-1, WIDTH)),
            ),
            grad_gains.reshape(16, 128),
            result,
            input_rows,
        )
        gains_sum = lax.dynamic_slice_in_dim(
            gains_total.reshape(-1), position * gain_count, gain_count
        )
        squares = square_total[0, 0]
    else:
        attention_sum, widen_sum, narrow_sum = (
            lax.psum_scatter(
                grad.astype(F32).reshape(-1, 128), axes, scatter_dimension=0, tiled=True
            ).reshape(-1, WIDTH)
            for grad in (grad_attention, grad_widen, grad_narrow)
        )
        gains_sum = lax.psum_scatter(grad_gains, axes, scatter_dimension=0, tiled=True)
        squares = lax.psum(
            sum(jnp.sum(g * g) for g in (attention_sum, widen_sum, narrow_sum, gains_sum)), axes
        )
        block_output, input_grad = swap_halves(result), swap_halves(input_rows)
    grad_norm = jnp.sqrt(squares)
    clip_factor = jnp.minimum(1.0, CLIP_LIMIT / (grad_norm + 1e-06))
    step_value = jnp.float32(STEP_VALUE)
    factors = (
        clip_factor,
        1.0 - jnp.power(jnp.float32(BETA_FIRST), step_value),
        1.0 - jnp.power(jnp.float32(BETA_SECOND), step_value),
    )
    return (
        block_output,
        input_grad,
        *adam_update(
            attention_weight,
            attention_first,
            attention_second,
            attention_sum,
            factors,
            MATRIX_RATE,
            DECAY,
        ),
        *adam_update(
            widen_weight, widen_first, widen_second, widen_sum.T, factors, MATRIX_RATE, DECAY
        ),
        *adam_update(
            narrow_weight, narrow_first, narrow_second, narrow_sum, factors, MATRIX_RATE, DECAY
        ),
        *adam_update(norm_gains, gains_first, gains_second, gains_sum, factors, GAIN_RATE, 0.0),
        grad_norm,
    )


def solution(mesh):
    both = ("dp", "fsdp")
    rows = P(None, both, None)
    tall = P(both, None)
    wide = P(None, both)
    flat = P(both)
    weights = (tall, tall, tall, wide, wide, wide, tall, tall, tall, flat, flat, flat)
    own_kernels = dict(mesh.shape) == {"dp": 16, "fsdp": 2}
    return jax.shard_map(
        functools.partial(local, own_kernels),
        mesh=mesh,
        in_specs=(rows, rows, P(None, "dp", None)) + weights,
        out_specs=(rows, rows) + weights + (P(),),
        check_vma=False,
    )
```

time: 1680 us -> 636 us (0.38)
  waiting for transfers between devices: 772 us -> 0 us
  Pallas kernels: 0 us -> 522 us
  matrix products: 350 us -> 49.1 us
  local copies, waits for them, and re-layouts: 247 us -> 22.4 us
  blocking collectives: 170 us -> 0 us
  other arithmetic: 110 us -> 29 us
  between operations: 20.4 us -> 3.04 us
    pallas_call x0 -> x5, Pallas kernels: none -> 522 us  [the longest x1 185 us: gather_all(): pl.pallas_call(functools.partial(gather_kernel, chunks, len(shards)), out...]
    reduce_scatter x7 -> x0, waiting for transfers between devices: 495 us -> none  [the longest x1 248 us: local(): lax.psum_scatter(flat_list[1], ('dp', 'fsdp'), scatter_dimension=0, tiled...]
    dot_general x136 -> x6, matrix products: 350 us -> 49.1 us  [the longest x3 18.3 us: dot(): return lax.dot_general(left, right, dims, preferred_element_type=F32)]
    all_gather x10 -> x0, waiting for transfers between devices: 273 us -> none  [the longest x2 111 us: micro_step(): lax.all_gather(narrow_low, ('dp', 'fsdp'), axis=0, tiled=True)]
    while x2 -> x0, blocking collectives: 82.8 us -> none
    dynamic_slice x98 -> x0, local copies, waits for them, and re-layouts: 77.8 us -> none  [the longest x96 77.6 us: forward(): lax.map(lambda pieces: pair_forward(pieces[0], pieces[1], pieces[2], same...]
    reshape x11 -> x0, local copies, waits for them, and re-layouts: 76.6 us -> none  [the longest x1 24.6 us: flat_grads(): grads[1].reshape(-1, 128)]
    psum x1 -> x0, blocking collectives: 44.6 us -> none  [local(): grad_norm = jnp.sqrt(lax.psum(local_squares, ('dp', 'fsdp')))]
  transfers between devices with their start and end apart: 17 -> 0, of which waited for: 13 -> 0; matrix products, arithmetic and copies ran while one was open for 19% -> 0% of each run, Pallas kernels for 0% -> 0%
where the time goes in v1:
time: 636 us; the launch traced here: 625 us
  Pallas kernels  522 us (82%)
  matrix products  49.1 us (8%)
  other arithmetic  29 us (5%)
  local copies, waits for them, and re-layouts  22.4 us (4%)
    pallas_call x1, Pallas kernels, gather_all(): pl.pallas_call(functools.partial(gather_kernel, chunks, len(shards)), out...  185 us
    pallas_call x1, Pallas kernels, reduce_all(): pl.pallas_call(functools.partial(reduce_kernel, chunks, arrays), out_shap...  164 us
    pallas_call x1, Pallas kernels, feed(): pl.pallas_call(feed_kernel, grid=(steps,), out_shape=[jax.ShapeDtypeStruc...  86.4 us
    pallas_call x1, Pallas kernels, attend_back(): pl.pallas_call(attend_back_kernel, out_shape=jax.ShapeDtypeStruct((3, ROW...  54.6 us
    pallas_call x1, Pallas kernels, attend(): pl.pallas_call(attend_kernel, out_shape=[jax.ShapeDtypeStruct((ROW, WIDTH...  32.3 us
    dot_general x3, matrix products, dot(): return lax.dot_general(left, right, dims, preferred_element_type=F32)  18.3 us

profile of v1, /device:TPU:0, one launch (start us, length us, event | category | flops | bytes accessed | tf_op | source)
XLA Modules:
  0.0 625.5 jit_solution(17218586745535009319)
XLA Ops:
  0.6 0.0 copy-start
  0.7 0.7 copy-done
  1.3 0.5 dynamic-slice_bitcast_fusion.counts
  1.8 0.7 convert_bitcast_fusion.2
  2.5 0.6 scatter.4.refs_3_
  3.1 1.7 convert_element_type.81.refs_2_
  4.8 1.8 convert_element_type.79.refs_0_
  6.6 1.9 convert_bitcast_fusion.1.refs_1_
  8.5 184.6 %gather_weights.1 = (bf16[4,2,2,2,128,1024]{5,4,3,2,1,0:T(8,128)(2,1)}, bf16[4,2,2,2,176,1024]{5,4,3,2,1,0:T(8,128)(2,1)}, bf16[4,2,2,2,88,1024]{5,4,3,2,1,0:T(8...) custom-call(bf16[128,1024]{1,0:T(8,128)(2,1)} %convert_element_type., ...), custom_call_target="tpu_custom_call" | custom-call | tf_op jit(solution)/shard_map/gather_weights/pallas_call | solution.py:226
  193.0 2.2 fusion.2
  195.2 0.1 rsqrt.26
  195.3 0.8 slice.53
  196.1 0.8 fusion.15
  196.9 0.1 reshape.190
  197.0 0.7 reshape.192.gain_ref
  197.6 0.1 reshape.191
  197.7 3.1 slice.48
  200.8 3.6 slice.45
  204.5 0.6 fusion.4
  205.1 2.0 copy-done.5
  207.1 9.9 %convert_bitcast_fusion.q_ref.k_ref.v_ref = bf16[3,1152,1024]{2,1,0:T(8,128)(2,1)} fusion(bf16[1152,1024,1]{1,0,2:T(8,128)(2,1)S(1)} %bitcast.96, bf16[3,1024,1024]{2,1,0:T(8,128)(2,1)S(1)} %bitcast.84), kind=kOutput, calls=%fused_computation.1 | convolution fusion | flops 7251296256 | bytes 15728640 | tf_op jit(solution)/shard_map/sd,jde->jse/dot_general | solution.py:823
  217.0 32.3 %attend.1 = (bf16[1152,1024]{1,0:T(8,128)(2,1)}, f32[1152,128]{1,0:T(8,128)}) custom-call(s32[3]{0:T(128)} %dynamic-slice_bitcast_fusion.counts, bf16[3,1152,1024]{2,1,0:T(8,128)(2,1)} %convert_bitcast_fusion.q_ref.k_ref.v_ref, bf16[3,1152,1024]{2,1,0:T(8,128)(2,1)} %convert_bitcast_fusion.q_ref.k_ref.v_ref, ...), custom_call_target="tpu_custom_call" | custom-call | tf_op jit(solution)/shard_map/attend/pallas_call | solution.py:599
  249.3 1.3 copy.34
  250.6 0.6 slice_bitcast_fusion.log_ref
  251.3 5.2 multiply_reduce_fusion
  256.5 2.2 copy-done.3
  258.6 1.8 multiply_convert_fusion.n2_ref
  260.4 86.4 %feed.1 = (f32[1152,1024]{1,0:T(8,128)}, f32[1152,1024]{1,0:T(8,128)}, bf16[1152,1024]{1,0:T(8,128)(2,1)}, f32[1,1024]{1,0:T(1,128)}, bf16[2,2816,1024]{2,1,0:T(8,128)(2,1)}, /*index=5*/bf16[2816,1024]{1,0:T(8,128)(2,1)}) custom-call(bf16[1152,1024]{1,0:T(8,128)(2,1)} %multiply_convert_fusion.n2_ref, bf16[1152,1024]{1,0:T(8,128)(2,1)} %bitcast.97, ...), custom_call_target="tpu_custom_call" | custom-call | tf_op jit(solution)/shard_map/feed/pallas_call | solution.py:777
  346.8 6.4 %convolution_convert_fusion.do_ref = bf16[1152,1024]{1,0:T(8,128)(2,1)} fusion(bf16[1152,1024]{1,0:T(8,128)(2,1)} %get-tuple-element.57, bf16[1024,1024]{1,0:T(8,128)(2,1)} %bitcast.99), kind=kOutput, calls=%fused_computation.21 | convolution fusion | flops 2417098752 | bytes 6815744 | tf_op jit(solution)/shard_map/dot_general | solution.py:46
  353.2 54.6 %attend_back.1 = bf16[3,1152,1024]{2,1,0:T(8,128)(2,1)} custom-call(s32[3]{0:T(128)} %dynamic-slice_bitcast_fusion.counts, bf16[3,1152,1024]{2,1,0:T(8,128)(2,1)} %convert_bitcast_fusion.q_ref.k_ref.v_ref, bf16[3,1152,1024]{2,1,0:T(8,128)(2,1)} %convert_bitcast_fusion.q_ref.k_ref.v_ref, bf16[3,1152,1024]{2,1,0:T(8,128)(2,1)} %convert_bitcast_fusion.q_ref.k_ref.v_ref, ...), custom_call_target="tpu_custom_call" | custom-call | tf_op jit(solution)/shard_map/attend_back/pallas_call | solution.py:688
  407.8 6.8 %convolution_convert_fusion.2 = bf16[1024,1024]{1,0:T(8,128)(2,1)} fusion(bf16[1152,1024]{1,0:T(8,128)(2,1)} %get-tuple-element.51.o_ref, bf16[1152,1024]{1,0:T(8,128)(2,1)} %get-tuple-element.57), kind=kOutput, calls=%fused_computation.24 | convolution fusion | flops 2416967680 | bytes 6815744 | tf_op jit(solution)/shard_map/dot_general | solution.py:46
  414.6 11.7 %fusion.7 = (f32[1152]{0:T(1024)S(1)}, f32[1024]{0:T(1024)S(1)}, f32[1152,1024,1]{1,0,2:T(8,128)S(1)}) fusion(bf16[2,576,1024]{2,1,0:T(8,128)(2,1)S(1)} %copy-done.2, f32[1024]{0:T(1024)S(1)} %reshape.190, f32[1152]{0:T(1024)S(1)} %rsqrt.26, bf16[3,1152,1024]{2,1,0:T(8,128)(2,1)S(1)} %copy-done.4, bf16[3,1024,1024]{2,1,0:T(8,128)(2,1)} %bitcast.85), kind=kOutput, calls=%fused_computation.17 | convolution fusion | flops 7256012800 | bytes 20464640 | tf_op jit(solution)/shard_map/jse,jde->sd/dot_general | solution.py:839
  426.4 3.0 fusion.8
  429.4 9.1 %convolution_convert_fusion.1 = bf16[3,1024,1024]{1,2,0:T(8,128)(2,1)S(1)} fusion(bf16[3,1152,1024]{2,1,0:T(8,128)(2,1)S(1)} %copy-done.4, bf16[1152,1024]{1,0:T(8,128)(2,1)S(1)} %get-tuple-element.84), kind=kOutput, calls=%fused_computation.22 | convolution fusion | flops 7250903040 | bytes 15728640 | tf_op jit(solution)/shard_map/sd,jse->jde/dot_general | solution.py:836
  438.6 0.6 pad_maximum_fusion.1.refs_3_
  439.2 5.5 pad_maximum_fusion.refs_2_
  444.8 0.0 copy-start.7
  444.8 164.0 %reduce_gradients.1 = (f32[88,1024]{1,0:T(8,128)}, f32[176,1024]{1,0:T(8,128)}, f32[128,1024]{1,0:T(8,128)}, f32[16,128]{1,0:T(8,128)}, f32[8,128]{1,0:T(8,128)}...) custom-call(bf16[4,2,2,2,88,1024]{5,4,3,2,1,0:T(8,128)(2,1)} %bitcast.87, bf16[4,2,2,2,176,1024]{5,4,3,2,1,0:T(8,128)(2,1)} %bitcast.82, ...), custom_call_target="tpu_custom_call" | custom-call | tf_op jit(solution)/shard_map/reduce_gradients/pallas_call | solution.py:515
  608.8 0.0 copy-start.10
  608.8 1.3 slice.51
  610.9 1.4 multiply_subtract_fusion.3
  612.3 2.4 multiply_subtract_fusion.2
  614.7 2.9 multiply_subtract_fusion.1
  617.6 1.7 multiply_subtract_fusion
  619.3 0.0 copy-start.1
  619.3 2.2 copy.45
  621.5 0.4 slice-done.1
  621.9 2.2 copy.46
  (45 shorter events, 0.1 us)
Async XLA Ops:
  0.6 0.7 copy-start
  200.8 3.7 copy-start.2
  204.4 2.6 copy-start.5
  256.4 2.2 copy-start.3
  407.8 6.8 %copy-start.4 = (bf16[3,1152,1024]{2,1,0:T(8,128)(2,1)S(1)}, bf16[3,1152,1024]{2,1,0:T(8,128)(2,1)}, u32[]{:S(2)}) copy-start(bf16[3,1152,1024]{2,1,0:T(8,128)(2,1)} %attend_back.1) | copy-start | bytes 21233668
  407.8 18.6 %slice-start.4 = ((s8[4718592]{0:T(1024)(128)(4,1)}), s8[4194304]{0:T(1024)(128)(4,1)S(1)}, s32[]{:S(2)}) async-start(s8[4718592]{0:T(1024)(128)(4,1)} %bitcast.94), calls=%async_computation.4 | async-start | bytes 8388608
  414.6 11.7 %slice-start.5 = ((s8[4718592]{0:T(1024)(128)(4,1)}), s8[524288]{0:T(1024)(128)(4,1)S(1)}, s32[]{:S(2)}) async-start(s8[4718592]{0:T(1024)(128)(4,1)} %bitcast.94), calls=%async_computation.5 | async-start | bytes 1048576
  429.4 9.1 %copy-start.13 = (f32[1,1024]{1,0:T(1,128)S(1)}, f32[1,1024]{1,0:T(1,128)}, u32[]{:S(2)}) copy-start(f32[1,1024]{1,0:T(1,128)} %get-tuple-element.59) | copy-start | bytes 12292
  444.7 166.1 %copy-start.14 = (f32[64]{0:T(128)S(1)}, f32[64]{0:T(128)}, u32[]{:S(2)}) copy-start(f32[64]{0:T(128)} %param.29) | copy-start | bytes 772
  444.7 166.1 %copy-start.15 = (f32[64]{0:T(128)S(1)}, f32[64]{0:T(128)}, u32[]{:S(2)}) copy-start(f32[64]{0:T(128)} %param.31) | copy-start | bytes 772
  444.7 166.1 %copy-start.16 = (f32[64]{0:T(128)S(1)}, f32[64]{0:T(128)}, u32[]{:S(2)}) copy-start(f32[64]{0:T(128)} %param.30) | copy-start | bytes 772
  444.7 167.5 %copy-start.8 = (f32[88,1024]{1,0:T(8,128)S(1)}, f32[88,1024]{1,0:T(8,128)}, u32[]{:S(2)}) copy-start(f32[88,1024]{1,0:T(8,128)} %param.26) | copy-start | bytes 1081348
  444.8 167.5 %copy-start.12 = (f32[88,1024]{1,0:T(8,128)S(1)}, f32[88,1024]{1,0:T(8,128)}, u32[]{:S(2)}) copy-start(f32[88,1024]{1,0:T(8,128)} %param.28) | copy-start | bytes 1081348
  444.8 169.9 %copy-start.7 = (f32[128,1024]{1,0:T(8,128)S(1)}, f32[128,1024]{1,0:T(8,128)}, u32[]{:S(2)}) copy-start(f32[128,1024]{1,0:T(8,128)} %param.20) | copy-start | bytes 1572868
  608.7 8.8 %copy-start.6 = (f32[1024,176]{0,1:T(8,128)S(1)}, f32[1024,176]{0,1:T(8,128)}, u32[]{:S(2)}) copy-start(f32[1024,176]{0,1:T(8,128)} %param.23) | copy-start | bytes 2162692
  608.8 8.8 %copy-start.9 = (f32[1024,176]{0,1:T(8,128)S(1)}, f32[1024,176]{0,1:T(8,128)}, u32[]{:S(2)}) copy-start(f32[1024,176]{0,1:T(8,128)} %param.25) | copy-start | bytes 2162692
  608.8 8.8 %copy-start.10 = (f32[1024,176]{0,1:T(8,128)S(1)}, f32[1024,176]{0,1:T(8,128)}, u32[]{:S(2)}) copy-start(f32[1024,176]{0,1:T(8,128)} %param.24) | copy-start | bytes 2162692
  610.8 6.7 %copy-start.11 = (f32[176,1024]{1,0:T(8,128)S(1)}, f32[176,1024]{1,0:T(8,128)}, u32[]{:S(2)}) copy-start(f32[176,1024]{1,0:T(8,128)} %get-tuple-element.66) | copy-start | bytes 2162692
  612.2 7.1 %slice-start.2 = ((s8[4718592]{0:T(1024)(128)(4,1)}), s8[4194304]{0:T(1024)(128)(4,1)S(1)}, s32[]{:S(2)}) async-start(s8[4718592]{0:T(1024)(128)(4,1)} %bitcast.92), calls=%async_computation.2 | async-start | bytes 8388608
  614.7 4.6 slice-start.3
  617.6 4.0 slice-start
  619.3 2.6 slice-start.1
  619.3 4.8 copy-start.1

commit v2 on v0

v2 whole, which is shorter than its diff:
```python
import functools

import jax
import jax.numpy as jnp
from jax import lax
from jax.experimental import pallas as pl
from jax.experimental.pallas import tpu as pltpu
from jax.sharding import PartitionSpec as P

HD = 64
TEXT = 128
PATCH = 256
ROW = 1152
WIDTH = 1024
HALF = ROW // 2
QUERY_TILE = 576
BACK_TILE = 384
FF_BLOCK = 256

NORM_EPS = 1e-06
MASKED = -(2.0**30)
BETA_FIRST = 0.9
BETA_SECOND = 0.999
ADAM_EPS = 1e-08
MATRIX_RATE = 0.05
GAIN_RATE = 0.3
DECAY = 0.1
CLIP_LIMIT = 1.0
STEP_VALUE = 10.0
GELU_SCALE = 0.7978845608028654
GELU_CUBE = 0.044715

BF16 = jnp.bfloat16
F32 = jnp.float32
MESH = pl.DeviceIdType.MESH
ANY = pl.BlockSpec(memory_space=pl.ANY)
VMEM_WHOLE = pl.BlockSpec(memory_space=pltpu.VMEM)
DMA = pltpu.SemaphoreType.DMA
VMEM_LIMIT = 60 * 2**20

NT = (((1,), (1,)), ((), ()))
TN = (((0,), (0,)), ((), ()))


def dot(left, right, dims=(((1,), (0,)), ((), ()))):
    return lax.dot_general(left, right, dims, preferred_element_type=F32)


class Place:
    def __init__(self):
        self.dp = lax.axis_index("dp")
        self.core = lax.axis_index("fsdp")
        self.z = self.dp // 4
        self.y = lax.rem(self.dp // 2, 2)
        self.x = lax.rem(self.dp, 2)
        flip_y = 1 - self.y
        flip_x = 1 - self.x
        is_zero = self.core == 0
        self.own = (self.y, self.x)
        self.first = (jnp.where(is_zero, self.y, flip_y), jnp.where(is_zero, flip_x, self.x))
        self.second = (jnp.where(is_zero, flip_y, self.y), jnp.where(is_zero, self.x, flip_x))
        self.across = (flip_y, flip_x)

    def at(self, z, spot):
        return (z * 4 + spot[0] * 2 + spot[1], self.core)

    def above(self, step):
        return self.at(lax.rem(self.z + step, 4), self.own)

    def to_first(self):
        return self.at(self.z, self.first)

    def to_second(self):
        return self.at(self.z, self.second)

    def sibling(self):
        return (self.dp, 1 - self.core)

    def greet(self):
        barrier = pltpu.get_barrier_semaphore()
        peers = [self.above(1), self.above(2), self.above(3)]
        peers += [self.to_first(), self.to_second(), self.sibling()]
        for peer in peers:
            pl.semaphore_signal(barrier, inc=1, device_id=peer, device_id_type=MESH)
        pl.semaphore_wait(barrier, len(peers))


def remote(source, target, send_sem, recv_sem, device):
    return pltpu.make_async_remote_copy(
        src_ref=source,
        dst_ref=target,
        send_sem=send_sem,
        recv_sem=recv_sem,
        device_id=device,
        device_id_type=MESH,
    )


def cut(index, rows, most):
    pieces = -(-rows // most)
    step = -(-rows // (pieces * 16)) * 16
    return [(index, at, min(step, rows - at)) for at in range(0, rows, step)]


class Gather:
    def __init__(self, shards, swaps=(), most=48):
        self.arrays = [*shards, *swaps]
        self.shards, self.swaps = len(shards), len(swaps)
        self.chunks = []
        for index, shard in enumerate(shards):
            self.chunks += cut(index, shard.shape[0], most)
        count = len(self.chunks)
        self.ticks = count + 3
        self.in_specs = [VMEM_WHOLE] * len(self.arrays)
        self.out_shapes = [jax.ShapeDtypeStruct((4, 2, 2, 2) + a.shape, a.dtype) for a in shards]
        self.out_shapes += [jax.ShapeDtypeStruct(a.shape, a.dtype) for a in swaps]
        self.out_specs = [ANY] * len(self.arrays)
        self.scratch = [
            DMA((count,)),
            DMA((count, 3)),
            DMA((count, 3)),
            DMA((count, 3)),
            DMA((count, 3)),
            DMA((count, 4)),
            DMA((count, 4)),
            DMA((max(self.swaps, 1),)),
            DMA((max(self.swaps, 1),)),
            DMA((max(self.swaps, 1),)),
        ]

    def bind(self, ins, outs, scratch):
        self.ins, self.outs = ins, outs
        (
            self.own_sem,
            self.z_send,
            self.z_recv,
            self.p_send,
            self.p_recv,
            self.c_send,
            self.c_recv,
            self.s_own,
            self.s_send,
            self.s_recv,
        ) = scratch
        self.here = Place()
        self.columns = (self.here.own, self.here.first, self.here.second, self.here.across)

    def spot(self, k, where):
        array, start, rows = self.chunks[k]
        return self.outs[array].at[:, where[0], where[1], self.here.core, pl.ds(start, rows), :]

    def mine(self, k):
        array, start, rows = self.chunks[k]
        here = self.here
        return (
            self.ins[array].at[pl.ds(start, rows), :],
            self.outs[array].at[here.z, here.y, here.x, here.core, pl.ds(start, rows), :],
        )

    def keep(self, k):
        source, target = self.mine(k)
        return pltpu.make_async_copy(source, target, self.own_sem.at[k])

    def along_z(self, k, step):
        source, target = self.mine(k)
        return remote(
            source,
            target,
            self.z_send.at[k, step - 1],
            self.z_recv.at[k, step - 1],
            self.here.above(step),
        )

    def plane(self, k, index):
        where = self.here.first if index == 2 else self.here.own
        device = self.here.to_first() if index == 0 else self.here.to_second()
        return remote(
            self.spot(k, where),
            self.spot(k, where),
            self.p_send.at[k, index],
            self.p_recv.at[k, index],
            device,
        )

    def to_sibling(self, k, index):
        where = self.columns[index]
        return remote(
            self.spot(k, where),
            self.spot(k, where),
            self.c_send.at[k, index],
            self.c_recv.at[k, index],
            self.here.sibling(),
        )

    def swap(self, index):
        source = self.ins[self.shards + index]
        target = self.outs[self.shards + index]
        core = self.here.core
        return (
            pltpu.make_async_copy(source.at[core], target.at[core], self.s_own.at[index]),
            remote(
                source.at[1 - core],
                target.at[core],
                self.s_send.at[index],
                self.s_recv.at[index],
                self.here.sibling(),
            ),
        )

    def tick(self, tick):
        count = len(self.chunks)
        if tick < count:
            self.keep(tick).start()
            for step in (2, 1, 3):
                self.along_z(tick, step).start()
        if tick == 0:
            for index in range(self.swaps):
                for copy in self.swap(index):
                    copy.start()
        k = tick - 1
        if 0 <= k < count:
            self.keep(k).wait()
            for step in (1, 2, 3):
                self.along_z(k, step).wait_recv()
            self.plane(k, 1).start()
            self.plane(k, 0).start()
            self.to_sibling(k, 0).start()
        k = tick - 2
        if 0 <= k < count:
            self.plane(k, 0).wait_recv()
            self.plane(k, 2).start()
            self.to_sibling(k, 1).start()
            self.plane(k, 1).wait_recv()
            self.to_sibling(k, 2).start()
        k = tick - 3
        if 0 <= k < count:
            self.plane(k, 2).wait_recv()
            self.to_sibling(k, 3).start()

    def finish(self):
        for k in range(len(self.chunks)):
            for step in (1, 2, 3):
                self.along_z(k, step).wait_send()
            for index in range(3):
                self.plane(k, index).wait_send()
            for index in range(4):
                self.to_sibling(k, index).wait()
        for index in range(self.swaps):
            for copy in self.swap(index):
                copy.wait()


class Reduce:
    def __init__(self, gradients, swaps=(), most=48):
        self.arrays = [*gradients, *swaps]
        self.gradients, self.swaps = len(gradients), len(swaps)
        self.chunks = []
        for index, gradient in enumerate(gradients):
            self.chunks += cut(index, gradient.shape[4], most)
        count = len(self.chunks)
        self.ticks = count + 4
        shapes = [g.shape[4:] for g in gradients]
        padded = [(-(-s[0] // 16) * 16, s[1]) for s in shapes]
        self.in_specs = [ANY] * len(self.arrays)
        self.out_shapes = [jax.ShapeDtypeStruct(s, F32) for s in shapes]
        self.out_shapes += [jax.ShapeDtypeStruct(a.shape[1:], a.dtype) for a in swaps]
        self.out_specs = [VMEM_WHOLE] * len(gradients) + [ANY] * len(swaps)
        self.scratch = []
        for lead in ((4, 2, 2), (4, 2, 2), (2, 4), (4,), (3,)):
            self.scratch += [pltpu.VMEM(lead + s, BF16) for s in padded]
        self.scratch += [
            DMA((count,)),
            DMA((count,)),
            DMA((count,)),
            DMA((count, 3)),
            DMA((count, 3)),
            DMA((count, 3)),
            DMA((count, 3)),
            DMA((max(self.swaps, 1),)),
            DMA((max(self.swaps, 1),)),
        ]

    def bind(self, ins, outs, scratch):
        n = self.gradients
        self.ins, self.outs = ins, outs
        self.own, self.from_core, self.from_second, self.from_first, self.from_z = (
            scratch[i * n : (i + 1) * n] for i in range(5)
        )
        (
            self.own_sem,
            self.c_send,
            self.c_recv,
            self.p_send,
            self.p_recv,
            self.z_send,
            self.z_recv,
            self.s_send,
            self.s_recv,
        ) = scratch[5 * n :]
        self.here = Place()

    def part(self, k):
        array, start, rows = self.chunks[k]
        return array, pl.ds(start, rows)

    def load(self, k):
        array, rows = self.part(k)
        return pltpu.make_async_copy(
            self.ins[array].at[:, :, :, self.here.core, rows, :],
            self.own[array].at[:, :, :, rows, :],
            self.own_sem.at[k],
        )

    def swap_core(self, k):
        array, rows = self.part(k)
        return remote(
            self.ins[array].at[:, :, :, 1 - self.here.core, rows, :],
            self.from_core[array].at[:, :, :, rows, :],
            self.c_send.at[k],
            self.c_recv.at[k],
            self.here.sibling(),
        )

    def send_second(self, k, index):
        array, rows = self.part(k)
        where = self.here.second if index == 0 else self.here.across
        return remote(
            self.own[array].at[:, where[0], where[1], rows, :],
            self.from_second[array].at[index, :, rows, :],
            self.p_send.at[k, index],
            self.p_recv.at[k, index],
            self.here.to_second(),
        )

    def send_first(self, k):
        array, rows = self.part(k)
        where = self.here.first
        return remote(
            self.own[array].at[:, where[0], where[1], rows, :],
            self.from_first[array].at[:, rows, :],
            self.p_send.at[k, 2],
            self.p_recv.at[k, 2],
            self.here.to_first(),
        )

    def send_z(self, k, step):
        array, rows = self.part(k)
        here = self.here
        return remote(
            self.own[array].at[lax.rem(here.z + step, 4), here.y, here.x, rows, :],
            self.from_z[array].at[step - 1, rows, :],
            self.z_send.at[k, step - 1],
            self.z_recv.at[k, step - 1],
            here.above(step),
        )

    def swap(self, index):
        source = self.ins[self.gradients + index]
        return remote(
            source.at[1 - self.here.core],
            self.outs[self.gradients + index],
            self.s_send.at[index],
            self.s_recv.at[index],
            self.here.sibling(),
        )

    def add_all(self, k):
        array, rows = self.part(k)
        own, other = self.own[array], self.from_core[array]

        def body(i, carry):
            z, y, x = i // 4, lax.rem(i // 2, 2), lax.rem(i, 2)
            own[z, y, x, rows, :] = both_sum(own[z, y, x, rows, :], other[z, y, x, rows, :])
            return carry

        lax.fori_loop(0, 16, body, 0)

    def add_column(self, k, where, other):
        array, rows = self.part(k)
        own = self.own[array]

        def body(z, carry):
            own[z, where[0], where[1], rows, :] = both_sum(
                own[z, where[0], where[1], rows, :], other[z, rows, :]
            )
            return carry

        lax.fori_loop(0, 4, body, 0)

    def total(self, k):
        array, rows = self.part(k)
        here = self.here
        total = self.own[array][here.z, here.y, here.x, rows, :].astype(F32)
        for step in range(3):
            total = total + self.from_z[array][step, rows, :].astype(F32)
        self.outs[array][rows, :] = total

    def tick(self, tick):
        count = len(self.chunks)
        if tick < count:
            self.swap_core(tick).start()
            self.load(tick).start()
        if tick == 1:
            for index in range(self.swaps):
                self.swap(index).start()
        k = tick - 1
        if 0 <= k < count:
            self.load(k).wait()
            self.swap_core(k).wait_recv()
            self.add_all(k)
            for index in (1, 0):
                self.send_second(k, index).start()
        k = tick - 2
        if 0 <= k < count:
            array = self.chunks[k][0]
            self.send_second(k, 1).wait_recv()
            self.add_column(k, self.here.first, self.from_second[array].at[1])
            self.send_first(k).start()
            self.send_second(k, 0).wait_recv()
            self.add_column(k, self.here.own, self.from_second[array].at[0])
        k = tick - 3
        if 0 <= k < count:
            array = self.chunks[k][0]
            self.send_first(k).wait_recv()
            self.add_column(k, self.here.own, self.from_first[array])
            for step in (2, 1, 3):
                self.send_z(k, step).start()
        k = tick - 4
        if 0 <= k < count:
            for step in (1, 2, 3):
                self.send_z(k, step).wait_recv()
            self.total(k)

    def finish(self):
        for k in range(len(self.chunks)):
            self.swap_core(k).wait_send()
            for index in (1, 0):
                self.send_second(k, index).wait_send()
            self.send_first(k).wait_send()
            for step in (1, 2, 3):
                self.send_z(k, step).wait_send()
        for index in range(self.swaps):
            self.swap(index).wait()


def both_sum(mine, other):
    return (mine.astype(F32) + other.astype(F32)).astype(BF16)


def everywhere(here, buffer, value, send, recv):
    for index, device in enumerate((here.sibling(), here.to_first(), here.to_second())):
        buffer[2 * index] = value
        copy = remote(
            buffer.at[2 * index], buffer.at[2 * index + 1], send.at[index], recv.at[index], device
        )
        copy.start()
        yield
        copy.wait()
        value = buffer[2 * index] + buffer[2 * index + 1]
    buffer[6 + here.z] = value
    copies = [
        remote(
            buffer.at[6 + here.z],
            buffer.at[6 + here.z],
            send.at[2 + step],
            recv.at[2 + step],
            here.above(step),
        )
        for step in (1, 2, 3)
    ]
    for copy in copies:
        copy.start()
    yield
    for copy in copies:
        copy.wait()
    yield (buffer[6] + buffer[7]) + (buffer[8] + buffer[9])


def call(name, body, grid, inner, ins, in_specs, out_shapes, out_specs, scratch=(), comm=None, key=0):
    params = {"vmem_limit_bytes": VMEM_LIMIT}
    if comm is None:

        def kernel(*refs):
            body(lambda point: None, *refs)

        extra = ([], [], [], [], [])
    else:
        params.update(collective_id=key, has_side_effects=True)
        extra = (comm.arrays, comm.in_specs, comm.out_shapes, comm.out_specs, comm.scratch)
        sizes = (len(ins), len(extra[0]), len(out_shapes), len(extra[2]), len(scratch), len(extra[4]))

        def kernel(*refs):
            parts, at = [], 0
            for size in sizes:
                parts.append(refs[at : at + size])
                at += size
            comm.bind(parts[1], parts[3], parts[5])
            step = pl.program_id(0)

            def pump(point):
                for tick in range(comm.ticks):
                    slot = tick * grid * inner // comm.ticks
                    if slot % inner == point:

                        @pl.when(step == slot // inner)
                        def _(tick=tick):
                            if tick == 0:
                                comm.here.greet()
                            comm.tick(tick)

            body(pump, *parts[0], *parts[2], *parts[4])

            @pl.when(step == grid - 1)
            def _():
                comm.finish()

    results = pl.pallas_call(
        kernel,
        grid=(grid,),
        out_shape=[*out_shapes, *extra[2]],
        in_specs=[*in_specs, *extra[1]],
        out_specs=[*out_specs, *extra[3]],
        scratch_shapes=[*scratch, *extra[4]],
        compiler_params=pltpu.CompilerParams(**params),
        name=name,
    )(*ins, *extra[0])
    return results[: len(out_shapes)], results[len(out_shapes) :]


def gather_now(comm, key):
    def kernel(*refs):
        sizes = (len(comm.arrays), len(comm.out_shapes))
        comm.bind(refs[: sizes[0]], refs[sizes[0] : sum(sizes)], refs[sum(sizes) :])
        comm.here.greet()
        for tick in range(comm.ticks):
            comm.tick(tick)
        comm.finish()

    return pl.pallas_call(
        kernel,
        out_shape=comm.out_shapes,
        in_specs=comm.in_specs,
        out_specs=comm.out_specs,
        scratch_shapes=comm.scratch,
        compiler_params=pltpu.CompilerParams(
            collective_id=key, has_side_effects=True, vmem_limit_bytes=VMEM_LIMIT
        ),
        name="gather_first",
    )(*comm.arrays)


def reduce_last(comm, gains, sums, key):
    def kernel(*refs):
        outs = len(comm.out_shapes)
        ins = refs[: len(comm.arrays)]
        gains_ref = refs[len(ins)]
        sums_refs = refs[len(ins) + 1 : len(ins) + 1 + len(sums)]
        at = len(ins) + 1 + len(sums)
        comm_outs, gains_out, square_out = refs[at : at + outs], refs[at + outs], refs[at + outs + 1]
        small, tiny, g_send, g_recv, n_send, n_recv = refs[at + outs + 2 : at + outs + 8]
        comm.bind(ins, comm_outs, refs[at + outs + 8 :])
        here = comm.here
        here.greet()
        gains_steps = everywhere(here, small, gains_ref[...], g_send, g_recv)
        for tick in range(comm.ticks):
            comm.tick(tick)
            if tick < 5:
                gains_total = next(gains_steps)
        gains_out[...] = gains_total
        squares = jnp.zeros((8, 128), F32)
        for ref in (*sums_refs, *comm_outs[: comm.gradients]):
            values = ref[...]
            squares = squares + jnp.sum((values * values).reshape(-1, 8, 128), axis=0)
        for total in everywhere(here, tiny, squares, n_send, n_recv):
            pass
        square_out[...] = jnp.broadcast_to(
            jnp.sum(total) + jnp.sum(gains_total * gains_total), (8, 128)
        )
        comm.finish()

    return pl.pallas_call(
        kernel,
        out_shape=[
            *comm.out_shapes,
            jax.ShapeDtypeStruct((16, 128), F32),
            jax.ShapeDtypeStruct((8, 128), F32),
        ],
        in_specs=[*comm.in_specs, VMEM_WHOLE, *([VMEM_WHOLE] * len(sums))],
        out_specs=[*comm.out_specs, VMEM_WHOLE, VMEM_WHOLE],
        scratch_shapes=[
            pltpu.VMEM((10, 16, 128), F32),
            pltpu.VMEM((10, 8, 128), F32),
            DMA((6,)),
            DMA((6,)),
            DMA((6,)),
            DMA((6,)),
            *comm.scratch,
        ],
        compiler_params=pltpu.CompilerParams(
            collective_id=key, has_side_effects=True, vmem_limit_bytes=VMEM_LIMIT
        ),
        name="reduce_last",
    )(*comm.arrays, gains, *sums)


def segment_lanes(counts):
    sizes = [jnp.where(counts[i] > 0, TEXT + PATCH * counts[i], 0) for i in range(3)]
    ends = (sizes[0], sizes[0] + sizes[1], sizes[0] + sizes[1] + sizes[2])
    places = jnp.arange(ROW, dtype=jnp.int32)[:, None]
    segment = sum((places >= end).astype(jnp.int32) for end in ends)
    lane = jnp.arange(2 * HD, dtype=jnp.int32)[None, :] % HD
    same = lane == segment
    queries = jnp.where((lane < 4) & ~same, MASKED, 0.0).astype(BF16)
    return queries, jnp.where(same, 1.0, 0.0).astype(BF16)


def lanes_of_heads():
    lane = lax.broadcasted_iota(jnp.int32, (1, 2 * HD), 1)
    return lane, (lane < HD, lane >= HD)


def attend_body(pump, q_ref, k_ref, v_ref, mq_ref, mk_ref, o_ref, log_ref):
    pair = pl.program_id(0)
    lane, in_head = lanes_of_heads()

    @pl.when(pair == 0)
    def _():
        log_ref[...] = jnp.zeros_like(log_ref)

    key = jnp.concatenate([k_ref[0], mk_ref[...]], axis=1)
    value = v_ref[0]
    values = [jnp.where(mine, value, jnp.ones_like(value)) for mine in in_head]
    for index in range(ROW // QUERY_TILE):
        pump(index)
        rows = pl.ds(index * QUERY_TILE, QUERY_TILE)
        query, extra = q_ref[0, rows, :], mq_ref[rows, :]
        mixed = []
        logs = log_ref[rows, :]
        for head in range(2):
            masked = jnp.where(in_head[head], query, jnp.zeros_like(query))
            scores = dot(jnp.concatenate([masked, extra], axis=1), key, NT)
            top = jnp.max(scores, axis=-1, keepdims=True)
            weight = jnp.exp(scores - top).astype(BF16)
            both = dot(weight, values[head])
            other = pltpu.roll(both, HD, 1)
            mixed.append(both / other)
            total = jnp.where(in_head[head], other, both)
            logs = jnp.where(lane == 2 * pair + head, top + jnp.log(total), logs)
        log_ref[rows, :] = logs
        o_ref[rows, :] = jnp.where(in_head[0], mixed[0], mixed[1]).astype(BF16)


PAIRS = WIDTH // (2 * HD)


def third(which):
    return pl.BlockSpec((1, ROW, 2 * HD), lambda p: (which, 0, p))


def attend(projected, extras, comm=None, key=0):
    whole = pl.BlockSpec((ROW, 128), lambda p: (0, 0))
    return call(
        "attend",
        attend_body,
        PAIRS,
        ROW // QUERY_TILE,
        [projected, projected, projected, *extras],
        [third(0), third(1), third(2), whole, whole],
        [jax.ShapeDtypeStruct((ROW, WIDTH), BF16), jax.ShapeDtypeStruct((ROW, 128), F32)],
        [pl.BlockSpec((ROW, 2 * HD), lambda p: (0, p)), whole],
        comm=comm,
        key=key,
    )


def attend_back_body(
    pump, q_ref, k_ref, v_ref, mq_ref, mk_ref, o_ref, do_ref, log_ref, out_ref, dk, dv
):
    pair = pl.program_id(0)
    _, in_head = lanes_of_heads()
    pick = jnp.where(
        (lax.broadcasted_iota(jnp.int32, (8, 2 * HD), 1) < HD)
        == (lax.broadcasted_iota(jnp.int32, (8, 2 * HD), 0) == 0),
        jnp.ones((8, 2 * HD), F32),
        jnp.zeros((8, 2 * HD), F32),
    )

    def only(values, head):
        return jnp.where(in_head[head], values, jnp.zeros_like(values))

    dk[...] = jnp.zeros_like(dk)
    dv[...] = jnp.zeros_like(dv)
    for index in range(ROW // BACK_TILE):
        pump(index)
        rows = pl.ds(index * BACK_TILE, BACK_TILE)
        query, grad, extra = q_ref[0, rows, :], do_ref[rows, :], mq_ref[rows, :]
        key, value = k_ref[0], v_ref[0]
        inner = lax.dot_general(
            pick,
            grad.astype(F32) * o_ref[rows, :].astype(F32),
            NT,
            precision=lax.Precision.HIGHEST,
            preferred_element_type=F32,
        )
        dq = None
        for head in range(2):
            log_total = log_ref[
                pl.ds(2 * pair + head, 1), index * BACK_TILE : (index + 1) * BACK_TILE
            ]
            scores = dot(
                jnp.where(in_head[head], key, mk_ref[...]),
                jnp.where(in_head[head], query, extra),
                NT,
            )
            weight = jnp.exp(scores - log_total)
            down = dot(only(value, head), grad, NT)
            slope = (weight * (down - inner[head : head + 1, :])).astype(BF16)
            dv[...] += dot(weight.astype(BF16), only(grad, head))
            dk[...] += dot(slope, only(query, head))
            step = dot(slope, only(key, head), TN)
            dq = step if dq is None else dq + step
        out_ref[0, rows, :] = dq.astype(BF16)
    out_ref[1] = dk[...].astype(BF16)
    out_ref[2] = dv[...].astype(BF16)


def attend_back(projected, extras, mixed, grad_mixed, log_rows, comm=None, key=0):
    whole = pl.BlockSpec((ROW, 128), lambda p: (0, 0))
    column = pl.BlockSpec((ROW, 2 * HD), lambda p: (0, p))
    return call(
        "attend_back",
        attend_back_body,
        PAIRS,
        ROW // BACK_TILE,
        [projected, projected, projected, *extras, mixed, grad_mixed, log_rows],
        [third(0), third(1), third(2), whole, whole, column, column]
        + [pl.BlockSpec((2 * PAIRS, ROW), lambda p: (0, 0))],
        [jax.ShapeDtypeStruct((3, ROW, WIDTH), BF16)],
        [pl.BlockSpec((3, ROW, 2 * HD), lambda p: (0, 0, p))],
        [pltpu.VMEM((ROW, 2 * HD), F32), pltpu.VMEM((ROW, 2 * HD), F32)],
        comm=comm,
        key=key,
    )


def feed_units(pump, n2_ref, cot_ref, widen_ref, narrow_ref, widen_grad_ref, narrow_grad_ref):
    pump(0)
    n2, cot = n2_ref[...], cot_ref[...]
    wide_gate, wide_up, narrow = widen_ref[0], widen_ref[1], narrow_ref[...]
    gate = dot(n2, wide_gate, NT)
    up = dot(n2, wide_up, NT)
    down = dot(cot, narrow, NT)
    square = gate * gate
    bend = jnp.tanh(GELU_SCALE * gate * (1.0 + GELU_CUBE * square))
    half = 0.5 * (1.0 + bend)
    curve = gate * half
    slope = half + 0.5 * gate * (1.0 - bend * bend) * (
        GELU_SCALE * (1.0 + 3.0 * GELU_CUBE * square)
    )
    hidden = (curve * up).astype(BF16)
    grad_gate = (down * up * slope).astype(BF16)
    grad_up = (down * curve).astype(BF16)
    pump(1)
    narrow_grad_ref[...] = dot(hidden, cot, TN).astype(BF16)
    widen_grad_ref[0] = dot(grad_gate, n2, TN).astype(BF16)
    widen_grad_ref[1] = dot(grad_up, n2, TN).astype(BF16)
    return lambda: dot(hidden, narrow), lambda: dot(grad_gate, wide_gate) + dot(grad_up, wide_up)


def feed_start_body(
    pump, n2_ref, cot_ref, widen_ref, narrow_ref, result_ref, back_ref, widen_grad_ref, narrow_grad_ref
):
    result, back = feed_units(
        pump, n2_ref, cot_ref, widen_ref, narrow_ref, widen_grad_ref, narrow_grad_ref
    )

    @pl.when(pl.program_id(0) == 0)
    def _():
        result_ref[...] = jnp.zeros_like(result_ref)
        back_ref[...] = jnp.zeros_like(back_ref)

    result_ref[...] += result()
    back_ref[...] += back()


def feed_end_body(
    pump, n2_ref, cot_ref, h1_ref, gain_ref, result_part, back_part, widen_ref, narrow_ref,
    result_ref, dh1_ref, e_ref, gain_grad_ref, widen_grad_ref, narrow_grad_ref,
    back_ref, part_sem,
):
    step = pl.program_id(0)
    parts = (
        pltpu.make_async_copy(result_part, result_ref, part_sem.at[0]),
        pltpu.make_async_copy(back_part, back_ref, part_sem.at[1]),
    )

    @pl.when(step == 0)
    def _():
        for part in parts:
            part.start()

    result, back = feed_units(
        pump, n2_ref, cot_ref, widen_ref, narrow_ref, widen_grad_ref, narrow_grad_ref
    )

    @pl.when(step == 0)
    def _():
        for part in parts:
            part.wait()

    result_ref[...] += result()
    back_ref[...] += back()

    @pl.when(step == pl.num_programs(0) - 1)
    def _():
        gain = gain_ref[...]

        def tile(i, total):
            rows = pl.ds(pl.multiple_of(i * 64, 64), 64)
            h1 = h1_ref[rows, :]
            grad = back_ref[rows, :]
            result_ref[rows, :] += h1
            scale = lax.rsqrt(jnp.mean(h1 * h1, axis=-1, keepdims=True) + NORM_EPS)
            lifted = gain * grad
            inner = jnp.mean(h1 * lifted, axis=-1, keepdims=True)
            dh1 = (
                cot_ref[rows, :].astype(F32)
                + scale * lifted
                - h1 * (scale * scale * scale * inner)
            )
            dh1_ref[rows, :] = dh1
            e_ref[rows, :] = dh1.astype(BF16)
            return total + jnp.sum((grad * h1 * scale).reshape(8, 8, WIDTH), axis=0)

        total = lax.fori_loop(0, ROW // 64, tile, jnp.zeros((8, WIDTH), F32))
        gain_grad_ref[...] = jnp.sum(total, axis=0, keepdims=True)


def whole_block(*shape):
    return pl.BlockSpec(shape, lambda j: (0,) * len(shape), pipeline_mode=pl.Buffered(1))


WIDE_BLOCK = pl.BlockSpec((2, FF_BLOCK, WIDTH), lambda j: (0, j, 0))
TALL_BLOCK = pl.BlockSpec((FF_BLOCK, WIDTH), lambda j: (j, 0))
ROW_F32 = jax.ShapeDtypeStruct((ROW, WIDTH), F32)
ROW_BF16 = jax.ShapeDtypeStruct((ROW, WIDTH), BF16)


def feed_start(n2, cot, widen, narrow, comm=None, key=0):
    rows = whole_block(ROW, WIDTH)
    return call(
        "feed_start",
        feed_start_body,
        narrow.shape[0] // FF_BLOCK,
        2,
        [n2, cot, widen, narrow],
        [rows, rows, WIDE_BLOCK, TALL_BLOCK],
        [
            ROW_F32,
            ROW_F32,
            jax.ShapeDtypeStruct(widen.shape, BF16),
            jax.ShapeDtypeStruct(narrow.shape, BF16),
        ],
        [rows, rows, WIDE_BLOCK, TALL_BLOCK],
        comm=comm,
        key=key,
    )


def feed_end(n2, cot, h1, gain, result_part, back_part, widen, narrow, comm=None, key=0):
    rows = whole_block(ROW, WIDTH)
    line = whole_block(1, WIDTH)
    return call(
        "feed_end",
        feed_end_body,
        narrow.shape[0] // FF_BLOCK,
        2,
        [n2, cot, h1, gain, result_part, back_part, widen, narrow],
        [rows, rows, rows, line, ANY, ANY, WIDE_BLOCK, TALL_BLOCK],
        [
            ROW_F32,
            ROW_F32,
            ROW_BF16,
            jax.ShapeDtypeStruct((1, WIDTH), F32),
            jax.ShapeDtypeStruct(widen.shape, BF16),
            jax.ShapeDtypeStruct(narrow.shape, BF16),
        ],
        [rows, rows, rows, line, WIDE_BLOCK, TALL_BLOCK],
        [pltpu.VMEM((ROW, WIDTH), F32), DMA((2,))],
        comm=comm,
        key=key,
    )


def rms_scale(values, gain_vector):
    return (
        values
        * lax.rsqrt(jnp.mean(values * values, axis=-1, keepdims=True) + NORM_EPS)
        * gain_vector
    )


def adam_update(master, first, second, gradient, factors, rate, decay):
    clip_factor, first_fix, second_fix = factors
    clipped = clip_factor * gradient
    first_new = BETA_FIRST * first + (1.0 - BETA_FIRST) * clipped
    second_new = BETA_SECOND * second + (1.0 - BETA_SECOND) * clipped * clipped
    master_new = master - rate * (
        first_new / first_fix / (jnp.sqrt(second_new / second_fix) + ADAM_EPS) + decay * master
    )
    return (master_new, first_new, second_new)


def swap_halves(parts):
    core = lax.axis_index("fsdp")
    got = lax.ppermute(parts[1 - core], "fsdp", [(0, 1), (1, 0)])
    return jnp.where(core == 0, jnp.stack([parts[0], got]), jnp.stack([got, parts[1]]))


def with_half(rows, got):
    own = rows.reshape(2, HALF, WIDTH)
    first = lax.axis_index("fsdp") == 0
    return jnp.where(first, jnp.stack([own[0], got]), jnp.stack([got, own[1]]))


def local(
    own_kernels,
    tokens,
    cotangent,
    images,
    attention_weight,
    attention_first,
    attention_second,
    widen_weight,
    widen_first,
    widen_second,
    narrow_weight,
    narrow_first,
    narrow_second,
    norm_gains,
    gains_first,
    gains_second,
):
    axes = ("dp", "fsdp")
    devices = lax.axis_size(axes)
    core = lax.axis_index("fsdp")
    position = lax.axis_index(axes)
    gain_count = norm_gains.shape[0]
    units = narrow_weight.shape[0]
    split = units * 6 // 11
    attention_low = attention_weight.astype(BF16)
    widen_low = widen_weight.astype(BF16).T.reshape(2, units, WIDTH)
    narrow_low = narrow_weight.astype(BF16)
    gains_low = norm_gains.astype(BF16)
    feed_low = [
        (widen_low[:, :split].reshape(-1, WIDTH), narrow_low[:split]),
        (widen_low[:, split:].reshape(-1, WIDTH), narrow_low[split:]),
    ]
    grid = (4, 2, 2, 2)

    def fetch(shards):
        return [lax.all_gather(shard, axes, axis=0, tiled=True) for shard in shards]

    def summed(gradients):
        return [
            lax.psum_scatter(
                g.astype(F32).reshape(-1, 128), axes, scatter_dimension=0, tiled=True
            ).reshape(-1, WIDTH)
            for g in gradients
        ]

    def other_half(parts):
        return lax.ppermute(
            lax.dynamic_index_in_dim(parts, 1 - core, 0, keepdims=False), "fsdp", [(0, 1), (1, 0)]
        )

    def as_feed(shards):
        return shards[0].reshape(2, -1, WIDTH), shards[1].reshape(-1, WIDTH)

    def as_shards(*gradients):
        return [g.reshape(grid + (-1, WIDTH)) for g in gradients]

    gather_a = gather_b = None
    if own_kernels:
        gains_tile = jnp.zeros((16, 128), BF16).at[0, :gain_count].set(gains_low)
        attention_full, gains_full, tokens_row, cotangent_row = gather_now(
            Gather((attention_low, gains_tile), (tokens, cotangent)), 0
        )
        gains_full = gains_full.reshape(devices, 16, 128)[:, 0, :gain_count].reshape(-1)
        gather_a, gather_b = Gather(feed_low[0]), Gather(feed_low[1])
    else:
        attention_full, gains_full = fetch((attention_low, gains_low))
        first = core == 0
        tokens_row, cotangent_row = (
            jnp.where(first, jnp.stack([a[0], got]), jnp.stack([got, a[1]]))
            for a, got in ((a, other_half(a)) for a in (tokens, cotangent))
        )
    counts = lax.dynamic_index_in_dim(images[:, 0, :], core, 0, keepdims=False)
    attention = attention_full.reshape(4, WIDTH, WIDTH)
    cot = cotangent_row.reshape(ROW, WIDTH)
    inputs = tokens_row.reshape(ROW, WIDTH).astype(F32)
    first_gain = gains_full[:WIDTH].astype(F32)
    second_gain = gains_full[WIDTH:].astype(F32)

    normed = rms_scale(inputs, first_gain).astype(BF16)
    projected = jnp.einsum(
        "sd,jde->jse", normed, attention[:3], preferred_element_type=F32
    ).astype(BF16)
    extras = segment_lanes(counts)
    (mixed, log_columns), feed_a = attend(projected, extras, gather_a, 1)
    log_rows = log_columns[:, : WIDTH // HD].T
    h1 = inputs + dot(mixed, attention[3])
    n2 = rms_scale(h1, second_gain).astype(BF16)
    widen_a, narrow_a = as_feed(feed_a if own_kernels else fetch(feed_low[0]))
    (result_part, back_part, *grads_a), feed_b = feed_start(
        n2, cot, widen_a, narrow_a, gather_b, 2
    )
    widen_b, narrow_b = as_feed(feed_b if own_kernels else fetch(feed_low[1]))
    (result, dh1, e, grad_gain_two, *grads_b), sums_a = feed_end(
        n2,
        cot,
        h1,
        second_gain[None],
        result_part,
        back_part,
        widen_b,
        narrow_b,
        Reduce(as_shards(*grads_a)) if own_kernels else None,
        3,
    )
    grad_out = dot(mixed, e, TN).astype(BF16)
    grad_mixed = dot(e, attention[3], NT).astype(BF16)
    (grad_projected,), sums_b = attend_back(
        projected,
        extras,
        mixed,
        grad_mixed,
        log_rows,
        Reduce(as_shards(*grads_b), (result.reshape(2, HALF, WIDTH),)) if own_kernels else None,
        4,
    )
    grad_qkv = jnp.einsum(
        "sd,jse->jde", normed, grad_projected, preferred_element_type=F32
    ).astype(BF16)
    grad_normed = jnp.einsum(
        "jse,jde->sd", grad_projected, attention[:3], preferred_element_type=F32
    )
    scale = lax.rsqrt(jnp.mean(inputs * inputs, axis=-1, keepdims=True) + NORM_EPS)
    lifted = first_gain * grad_normed
    inner = jnp.mean(inputs * lifted, axis=-1, keepdims=True)
    input_rows = dh1 + scale * lifted - inputs * (scale * scale * scale * inner)
    grad_gain_one = jnp.sum(grad_normed * inputs * scale, axis=0)
    grad_attention = jnp.concatenate([grad_qkv, grad_out[None]], axis=0)
    grad_gains = jnp.concatenate([grad_gain_one, grad_gain_two[0]])

    if own_kernels:
        *sums_b, got_result = sums_b
        attention_sum, got_input, gains_total, square_total = reduce_last(
            Reduce(as_shards(grad_attention), (input_rows.reshape(2, HALF, WIDTH),)),
            grad_gains.reshape(16, 128),
            [*sums_a, *sums_b],
            5,
        )
        gains_sum = lax.dynamic_slice_in_dim(
            gains_total.reshape(-1), position * gain_count, gain_count
        )
        squares = square_total[0, 0]
    else:
        sums_a, sums_b, (attention_sum,) = summed(grads_a), summed(grads_b), summed([grad_attention])
        gains_sum = lax.psum_scatter(grad_gains, axes, scatter_dimension=0, tiled=True)
        squares = lax.psum(
            sum(jnp.sum(g * g) for g in (*sums_a, *sums_b, attention_sum, gains_sum)), axes
        )
        got_result = other_half(result.reshape(2, HALF, WIDTH))
        got_input = other_half(input_rows.reshape(2, HALF, WIDTH))
    widen_sum = jnp.concatenate(
        [sums_a[0].reshape(2, -1, WIDTH), sums_b[0].reshape(2, -1, WIDTH)], axis=1
    ).reshape(-1, WIDTH)
    narrow_sum = jnp.concatenate([sums_a[1], sums_b[1]], axis=0)
    grad_norm = jnp.sqrt(squares)
    clip_factor = jnp.minimum(1.0, CLIP_LIMIT / (grad_norm + 1e-06))
    step_value = jnp.float32(STEP_VALUE)
    factors = (
        clip_factor,
        1.0 - jnp.power(jnp.float32(BETA_FIRST), step_value),
        1.0 - jnp.power(jnp.float32(BETA_SECOND), step_value),
    )
    return (
        with_half(result, got_result),
        with_half(input_rows, got_input),
        *adam_update(
            attention_weight,
            attention_first,
            attention_second,
            attention_sum,
            factors,
            MATRIX_RATE,
            DECAY,
        ),
        *adam_update(
            widen_weight, widen_first, widen_second, widen_sum.T, factors, MATRIX_RATE, DECAY
        ),
        *adam_update(
            narrow_weight, narrow_first, narrow_second, narrow_sum, factors, MATRIX_RATE, DECAY
        ),
        *adam_update(norm_gains, gains_first, gains_second, gains_sum, factors, GAIN_RATE, 0.0),
        grad_norm,
    )


def solution(mesh):
    both = ("dp", "fsdp")
    rows = P(None, both, None)
    tall = P(both, None)
    wide = P(None, both)
    flat = P(both)
    weights = (tall, tall, tall, wide, wide, wide, tall, tall, tall, flat, flat, flat)
    own_kernels = dict(mesh.shape) == {"dp": 16, "fsdp": 2}
    return jax.shard_map(
        functools.partial(local, own_kernels),
        mesh=mesh,
        in_specs=(rows, rows, P(None, "dp", None)) + weights,
        out_specs=(rows, rows) + weights + (P(),),
        check_vma=False,
    )
```

time: 1680 us -> 544 us (0.32)
  waiting for transfers between devices: 772 us -> 0 us
  Pallas kernels: 0 us -> 427 us
  matrix products: 350 us -> 48.8 us
  local copies, waits for them, and re-layouts: 247 us -> 24.3 us
  blocking collectives: 170 us -> 0 us
  other arithmetic: 110 us -> 33.2 us
    reduce_scatter x7 -> x0, waiting for transfers between devices: 495 us -> none  [the longest x1 248 us: local(): lax.psum_scatter(flat_list[1], ('dp', 'fsdp'), scatter_dimension=0, tiled...]
    pallas_call x0 -> x6, Pallas kernels: none -> 427 us  [the longest x4 304 us: call(): pl.pallas_call(kernel, grid=(grid,), out_shape=[*out_shapes, *extra[2]],...]
    dot_general x136 -> x6, matrix products: 350 us -> 48.8 us  [the longest x3 18.3 us: dot(): return lax.dot_general(left, right, dims, preferred_element_type=F32)]
    all_gather x10 -> x0, waiting for transfers between devices: 273 us -> none  [the longest x2 111 us: micro_step(): lax.all_gather(narrow_low, ('dp', 'fsdp'), axis=0, tiled=True)]
    while x2 -> x0, blocking collectives: 82.8 us -> none
    dynamic_slice x98 -> x1, local copies, waits for them, and re-layouts: 77.8 us -> 0.01 us  [local(): counts = lax.dynamic_index_in_dim(images[:, 0, :], core, 0, keepdims=False)]
    reshape x11 -> x0, local copies, waits for them, and re-layouts: 76.6 us -> none  [the longest x1 24.6 us: flat_grads(): grads[1].reshape(-1, 128)]
    psum x1 -> x0, blocking collectives: 44.6 us -> none  [local(): grad_norm = jnp.sqrt(lax.psum(local_squares, ('dp', 'fsdp')))]
  transfers between devices with their start and end apart: 17 -> 0, of which waited for: 13 -> 0; matrix products, arithmetic and copies ran while one was open for 19% -> 0% of each run, Pallas kernels for 0% -> 0%
where the time goes in v2:
time: 544 us; the launch traced here: 541 us
  Pallas kernels  427 us (78%)
  matrix products  48.8 us (9%)
  other arithmetic  33.2 us (6%)
  local copies, waits for them, and re-layouts  24.3 us (4%)
  between operations  7.03 us (1%)
    pallas_call x4, Pallas kernels, call(): pl.pallas_call(kernel, grid=(grid,), out_shape=[*out_shapes, *extra[2]],...  304 us
    pallas_call x1, Pallas kernels, reduce_last(): pl.pallas_call(kernel, out_shape=[*comm.out_shapes, jax.ShapeDtypeStruct(...  68.4 us
    pallas_call x1, Pallas kernels, gather_now(): pl.pallas_call(kernel, out_shape=comm.out_shapes, in_specs=comm.in_specs,...  54.9 us
    dot_general x3, matrix products, dot(): return lax.dot_general(left, right, dims, preferred_element_type=F32)  18.3 us
    dot_general x1, matrix products, local(): jnp.einsum('jse,jde->sd', grad_projected, attention[:3], preferred_elemen...  11.9 us

profile of v2, /device:TPU:0, one launch (start us, length us, event | category | flops | bytes accessed | tf_op | source)
XLA Modules:
  0.0 540.7 jit_solution(12280960890796400232)
XLA Ops:
  0.7 0.7 copy-done
  1.3 0.7 convert_bitcast_fusion.1
  2.0 0.6 fusion.24
  6.5 0.6 scatter.4.refs_1_
  7.1 1.0 convert_element_type.126
  8.1 0.6 slice.123.refs_5_
  8.8 0.6 slice.120.refs_6_
  9.4 1.8 convert_element_type.109.refs_0_
  11.2 1.2 convert_element_type.125
  12.3 0.7 slice.122
  13.0 0.7 slice.119
  13.7 1.1 fusion.12
  14.8 54.9 %gather_first.1 = (bf16[4,2,2,2,128,1024]{5,4,3,2,1,0:T(8,128)(2,1)}, bf16[4,2,2,2,16,128]{5,4,3,2,1,0:T(8,128)(2,1)}, bf16[2,576,1024]{2,1,0:T(8,128)(2,1)}, bf16[2,576,1024]{2,1,0:T(8,128)(2,1)}) custom-call(bf16[128,1024]{1,0:T(8,128)(2,1)} %convert_element_type.109.refs_0_, bf16[16,128]{1,0:T(8,128)(2,1)} %scatter.4.refs_1_, ...), custom_call_target="tpu_custom_call" | custom-call | tf_op jit(solution)/shard_map/gather_first/pallas_call | solution.py:539
  69.7 2.2 fusion.2
  72.0 0.8 slice.121
  72.7 0.8 fusion.17
  73.6 0.7 reshape.308.refs_3_
  74.3 3.1 slice.104
  77.4 3.6 slice.96
  81.1 0.6 fusion.4
  81.7 2.0 copy-done.4
  83.7 9.5 %convert_bitcast_fusion.refs_0_.refs_1_.refs_2_ = bf16[3,1152,1024]{2,1,0:T(8,128)(2,1)} fusion(bf16[1152,1024,1]{1,0,2:T(8,128)(2,1)S(1)} %bitcast.126, bf16[3,1024,1024]{2,1,0:T(8,128)(2,1)S(1)} %bitcast.112), kind=kOutput, calls=%fused_computation.1 | convolution fusion | flops 7251296256 | bytes 15728640 | tf_op jit(solution)/shard_map/sd,jde->jse/dot_general | solution.py:1006
  93.2 68.5 %attend.1 = (bf16[1152,1024]{1,0:T(8,128)(2,1)}, f32[1152,128]{1,0:T(8,128)}, bf16[4,2,2,2,96,1024]{5,4,3,2,1,0:T(8,128)(2,1)}, bf16[4,2,2,2,48,1024]{5,4,3,2,1,0:T(8,128)(2,1)}) custom-call(bf16[3,1152,1024]{2,1,0:T(8,128)(2,1)} %convert_bitcast_fusion.refs_0_.refs_1_.refs_2_, bf16[3,1152,1024]{2,1,0:T(8,128)(2,1)} %convert_bitcast_fusion.refs_0_.refs_1_.refs_2_, ...), custom_call_target="tpu_custom_call" | custom-call | tf_op jit(solution)/shard_map/attend/pallas_call | solution.py:517
  161.7 1.3 copy.34
  163.0 0.6 slice_bitcast_fusion.4.refs_7_
  163.7 5.2 multiply_reduce_fusion
  168.9 2.2 copy-done.3
  171.0 1.9 multiply_convert_fusion.refs_0_
  172.9 67.3 %feed_start.1 = (f32[1152,1024]{1,0:T(8,128)}, f32[1152,1024]{1,0:T(8,128)}, bf16[2,1536,1024]{2,1,0:T(8,128)(2,1)}, bf16[1536,1024]{1,0:T(8,128)(2,1)}, bf16[4,...) custom-call(bf16[1152,1024]{1,0:T(8,128)(2,1)} %multiply_convert_fusion.refs_0_, ...), custom_call_target="tpu_custom_call" | custom-call | tf_op jit(solution)/shard_map/feed_start/pallas_call | solution.py:517
  240.2 85.3 %feed_end.1 = (f32[1152,1024]{1,0:T(8,128)}, f32[1152,1024]{1,0:T(8,128)}, bf16[1152,1024]{1,0:T(8,128)(2,1)}, f32[1,1024]{1,0:T(1,128)}, bf16[2,1280,1024]{2,1,...) custom-call(bf16[1152,1024]{1,0:T(8,128)(2,1)} %multiply_convert_fusion.refs_0_, ...), custom_call_target="tpu_custom_call" | custom-call | tf_op jit(solution)/shard_map/feed_end/pallas_call | solution.py:517
  325.6 6.4 %convolution_convert_fusion.refs_6_ = bf16[1152,1024]{1,0:T(8,128)(2,1)} fusion(bf16[1152,1024]{1,0:T(8,128)(2,1)} %get-tuple-element.71, bf16[1024,1024]{1,0:T(8,128)(2,1)} %bitcast.128), kind=kOutput, calls=%fused_computation.23 | convolution fusion | flops 2417098752 | bytes 6815744 | tf_op jit(solution)/shard_map/dot_general | solution.py:46
  331.9 82.8 %attend_back.1 = (bf16[3,1152,1024]{2,1,0:T(8,128)(2,1)}, f32[80,1024]{1,0:T(8,128)}, f32[40,1024]{1,0:T(8,128)}, f32[576,1024]{1,0:T(8,128)}) custom-call(bf16[3,1152,1024]{2,1,0:T(8,128)(2,1)} %convert_bitcast_fusion.refs_0_.refs_1_.refs_2_, bf16[3,1152,1024]{2,1,0:T(8,128)(2,1)} %convert_bitcast_fusion.refs_0_.refs_1_.refs_2_, ...), custom_call_target="tpu_custom_call" | custom-call | tf_op jit(solution)/shard_map/attend_back/pallas_call | solution.py:517
  414.7 6.8 %convolution_convert_fusion.2 = bf16[1024,1024]{1,0:T(8,128)(2,1)} fusion(bf16[1152,1024]{1,0:T(8,128)(2,1)} %get-tuple-element.60.refs_5_, bf16[1152,1024]{1,0:T(8,128)(2,1)} %get-tuple-element.71), kind=kOutput, calls=%fused_computation.30 | convolution fusion | flops 2416967680 | bytes 6815744 | tf_op jit(solution)/shard_map/dot_general | solution.py:46
  421.5 11.9 %fusion.1 = (f32[1024]{0:T(1024)S(1)}, f32[1152]{0:T(1024)S(1)}, f32[1152,1024,1]{1,0,2:T(8,128)S(1)}) fusion(bf16[2,576,1024]{2,1,0:T(8,128)(2,1)S(1)} %copy-done.2, f32[1152]{0:T(1024)S(1)} %rsqrt.26, f32[1024]{0:T(1024)S(1)} %reshape.306, bf16[3,1152,1024]{2,1,0:T(8,128)(2,1)S(1)} %copy-done.20, bf16[3,1024,1024]{2,1,0:T(8,128)(2,1)} %bitcast.113), kind=kOutput, calls=%fused_computation.7 | convolution fusion | flops 7256012800 | bytes 20464640 | tf_op jit(solution)/shard_map/jse,jde->sd/dot_general | solution.py:1045
  433.4 0.6 pad_maximum_fusion.1.refs_2_
  434.1 3.0 fusion.6
  437.1 9.1 %convolution_convert_fusion.1 = bf16[3,1024,1024]{1,2,0:T(8,128)(2,1)S(1)} fusion(bf16[3,1152,1024]{2,1,0:T(8,128)(2,1)S(1)} %copy-done.20, bf16[1152,1024]{1,0:T(8,128)(2,1)S(1)} %get-tuple-element.106), kind=kOutput, calls=%fused_computation.24 | convolution fusion | flops 7250903040 | bytes 15728640 | tf_op jit(solution)/shard_map/sd,jse->jde/dot_general | solution.py:1042
  446.2 5.6 %pad_maximum_fusion.refs_0_ = bf16[4,2,2,2,128,1024]{5,4,3,2,1,0:T(8,128)(2,1)} fusion(bf16[1,2,2,2,128,1024]{5,4,3,2,1,0:T(8,128)(2,1)} %bitcast.129, bf16[3,2,2,2,128,1024]{5,4,3,2,1,0:T(8,128)(2,1)S(1)} %bitcast.115), kind=kLoop, calls=%fused_computation | loop fusion | flops 4194304 | bytes 16777216 | tf_op jit(solution)/shard_map/concatenate | solution.py:1053
  451.9 68.4 %reduce_last.1 = (f32[128,1024]{1,0:T(8,128)}, f32[576,1024]{1,0:T(8,128)}, f32[16,128]{1,0:T(8,128)}, f32[8,128]{1,0:T(8,128)}) custom-call(bf16[4,2,2,2,128,1024]{5,4,3,2,1,0:T(8,128)(2,1)} %pad_maximum_fusion.refs_0_, f32[2,576,1024]{2,1,0:T(8,128)} %bitcast.103, f32[16,128]{1,0:T(8,128)} %pad_maximum_fusion.1.refs_2_, ...), custom_call_target="tpu_custom_call" | custom-call | tf_op jit(solution)/shard_map/reduce_last/pallas_call | solution.py:581
  520.3 1.3 slice.117
  522.5 1.4 multiply_subtract_fusion.3
  523.9 2.4 multiply_subtract_fusion.2
  526.3 2.9 multiply_subtract_fusion.1
  529.2 1.7 multiply_subtract_fusion
  531.3 0.9 slice-done.2
  532.9 1.3 copy-done.6
  534.1 0.7 copy-done.7
  534.9 4.4 maximum_select_fusion
  (65 shorter events, 1.5 us)
Async XLA Ops:
  0.6 0.7 copy-start
  77.4 3.7 copy-start.2
  81.1 2.6 copy-start.4
  168.8 2.2 copy-start.3
  414.7 6.8 %copy-start.20 = (bf16[3,1152,1024]{2,1,0:T(8,128)(2,1)S(1)}, bf16[3,1152,1024]{2,1,0:T(8,128)(2,1)}, u32[]{:S(2)}) copy-start(bf16[3,1152,1024]{2,1,0:T(8,128)(2,1)} %get-tuple-element.77) | copy-start | bytes 21233668
  414.7 19.3 %slice-start.4 = ((s8[4718592]{0:T(1024)(128)(4,1)}), s8[4194304]{0:T(1024)(128)(4,1)S(1)}, s32[]{:S(2)}) async-start(s8[4718592]{0:T(1024)(128)(4,1)} %bitcast.118), calls=%async_computation.4 | async-start | bytes 8388608
  421.5 11.9 %copy-start.16 = (f32[1,1024]{1,0:T(1,128)S(1)}, f32[1,1024]{1,0:T(1,128)}, u32[]{:S(2)}) copy-start(f32[1,1024]{1,0:T(1,128)} %get-tuple-element.78) | copy-start | bytes 12292
  421.5 12.5 %slice-start.5 = ((s8[4718592]{0:T(1024)(128)(4,1)}), s8[524288]{0:T(1024)(128)(4,1)S(1)}, s32[]{:S(2)}) async-start(s8[4718592]{0:T(1024)(128)(4,1)} %bitcast.118), calls=%async_computation.5 | async-start | bytes 1048576
  451.8 70.5 %copy-start.9 = (f32[96,1024]{1,0:T(8,128)S(1)}, f32[96,1024]{1,0:T(8,128)}, u32[]{:S(2)}) copy-start(f32[96,1024]{1,0:T(8,128)} %get-tuple-element.79.refs_3_) | copy-start | bytes 1179652
  451.8 70.6 %copy-start.11 = (f32[80,1024]{1,0:T(8,128)S(1)}, f32[80,1024]{1,0:T(8,128)}, u32[]{:S(2)}) copy-start(f32[80,1024]{1,0:T(8,128)} %get-tuple-element.81.refs_5_) | copy-start | bytes 983044
  451.8 70.6 %copy-start.17 = (f32[64]{0:T(128)S(1)}, f32[64]{0:T(128)}, u32[]{:S(2)}) copy-start(f32[64]{0:T(128)} %param.29) | copy-start | bytes 772
  451.8 70.6 %copy-start.18 = (f32[64]{0:T(128)S(1)}, f32[64]{0:T(128)}, u32[]{:S(2)}) copy-start(f32[64]{0:T(128)} %param.31) | copy-start | bytes 772
  451.8 70.6 %copy-start.19 = (f32[64]{0:T(128)S(1)}, f32[64]{0:T(128)}, u32[]{:S(2)}) copy-start(f32[64]{0:T(128)} %param.30) | copy-start | bytes 772
  451.8 72.0 %copy-start.10 = (f32[88,1024]{1,0:T(8,128)S(1)}, f32[88,1024]{1,0:T(8,128)}, u32[]{:S(2)}) copy-start(f32[88,1024]{1,0:T(8,128)} %param.26) | copy-start | bytes 1081348
  451.8 72.0 %copy-start.12 = (f32[48,1024]{1,0:T(8,128)S(1)}, f32[48,1024]{1,0:T(8,128)}, u32[]{:S(2)}) copy-start(f32[48,1024]{1,0:T(8,128)} %get-tuple-element.80.refs_4_) | copy-start | bytes 589828
  451.9 72.0 %copy-start.15 = (f32[40,1024]{1,0:T(8,128)S(1)}, f32[40,1024]{1,0:T(8,128)}, u32[]{:S(2)}) copy-start(f32[40,1024]{1,0:T(8,128)} %get-tuple-element.82.refs_6_) | copy-start | bytes 491524
  451.9 74.4 %copy-start.8 = (f32[128,1024]{1,0:T(8,128)S(1)}, f32[128,1024]{1,0:T(8,128)}, u32[]{:S(2)}) copy-start(f32[128,1024]{1,0:T(8,128)} %param.20) | copy-start | bytes 1572868
  520.3 8.9 %copy-start.5 = (f32[1024,176]{0,1:T(8,128)S(1)}, f32[1024,176]{0,1:T(8,128)}, u32[]{:S(2)}) copy-start(f32[1024,176]{0,1:T(8,128)} %param.23) | copy-start | bytes 2162692
  520.3 8.9 %copy-start.13 = (f32[1024,176]{0,1:T(8,128)S(1)}, f32[1024,176]{0,1:T(8,128)}, u32[]{:S(2)}) copy-start(f32[1024,176]{0,1:T(8,128)} %param.25) | copy-start | bytes 2162692
  522.3 6.8 %copy-start.14 = (f32[1024,176]{0,1:T(8,128)S(1)}, f32[1024,176]{0,1:T(8,128)}, u32[]{:S(2)}) copy-start(f32[1024,176]{0,1:T(8,128)} %param.24) | copy-start | bytes 2162692
  523.8 7.1 %slice-start = ((s8[4718592]{0:T(1024)(128)(4,1)}), s8[4194304]{0:T(1024)(128)(4,1)S(1)}, s32[]{:S(2)}) async-start(s8[4718592]{0:T(1024)(128)(4,1)} %bitcast.104), calls=%async_computation | async-start | bytes 8388608
  526.3 4.6 slice-start.1
  529.2 3.0 slice-start.2
  530.9 1.6 slice-start.3
  532.5 1.7 copy-start.6
  532.5 2.4 copy-start.7
  534.9 4.4 copy-start.1

commit v3 on v2

--- a/solution.py
+++ b/solution.py
@@ -16,6 +16,9 @@
 QUERY_TILE = 576
 BACK_TILE = 384
 FF_BLOCK = 256
+GATHER_ROWS = 16
+REDUCE_ROWS = 16
+LAG = 2
 
 NORM_EPS = 1e-06
 MASKED = -(2.0**30)
@@ -103,14 +106,15 @@
 
 
 class Gather:
-    def __init__(self, shards, swaps=(), most=48):
+    def __init__(self, shards, swaps=(), most=GATHER_ROWS, lag=LAG):
         self.arrays = [*shards, *swaps]
         self.shards, self.swaps = len(shards), len(swaps)
         self.chunks = []
         for index, shard in enumerate(shards):
-            self.chunks += cut(index, shard.shape[0], most)
+            self.chunks += cut(index, shard.shape[0], most * WIDTH // shard.shape[1])
         count = len(self.chunks)
-        self.ticks = count + 3
+        self.lag = lag
+        self.ticks = count + 3 * lag
         self.in_specs = [VMEM_WHOLE] * len(self.arrays)
         self.out_shapes = [jax.ShapeDtypeStruct((4, 2, 2, 2) + a.shape, a.dtype) for a in shards]
         self.out_shapes += [jax.ShapeDtypeStruct(a.shape, a.dtype) for a in swaps]
@@ -142,6 +146,7 @@
             self.s_send,
             self.s_recv,
         ) = scratch
+        self.claimed = set()
         self.here = Place()
         self.columns = (self.here.own, self.here.first, self.here.second, self.here.across)
 
@@ -217,7 +222,7 @@
             for index in range(self.swaps):
                 for copy in self.swap(index):
                     copy.start()
-        k = tick - 1
+        k = tick - self.lag
         if 0 <= k < count:
             self.keep(k).wait()
             for step in (1, 2, 3):
@@ -225,17 +230,22 @@
             self.plane(k, 1).start()
             self.plane(k, 0).start()
             self.to_sibling(k, 0).start()
-        k = tick - 2
+        k = tick - 2 * self.lag
         if 0 <= k < count:
             self.plane(k, 0).wait_recv()
             self.plane(k, 2).start()
             self.to_sibling(k, 1).start()
             self.plane(k, 1).wait_recv()
             self.to_sibling(k, 2).start()
-        k = tick - 3
+        k = tick - 3 * self.lag
         if 0 <= k < count:
             self.plane(k, 2).wait_recv()
             self.to_sibling(k, 3).start()
+
+    def arrived(self, k):
+        self.claimed.add(k)
+        for index in range(4):
+            self.to_sibling(k, index).wait_recv()
 
     def finish(self):
         for k in range(len(self.chunks)):
@@ -244,29 +254,37 @@
             for index in range(3):
                 self.plane(k, index).wait_send()
             for index in range(4):
-                self.to_sibling(k, index).wait()
+                self.to_sibling(k, index).wait_send()
+                if k not in self.claimed:
+                    self.to_sibling(k, index).wait_recv()
         for index in range(self.swaps):
             for copy in self.swap(index):
                 copy.wait()
 
 
 class Reduce:
-    def __init__(self, gradients, swaps=(), most=48):
+    def __init__(self, gradients, inside=(), swaps=(), most=REDUCE_ROWS, lag=LAG):
         self.arrays = [*gradients, *swaps]
-        self.gradients, self.swaps = len(gradients), len(swaps)
+        self.outside, self.inside, self.swaps = len(gradients), list(inside), len(swaps)
         self.chunks = []
         for index, gradient in enumerate(gradients):
             self.chunks += cut(index, gradient.shape[4], most)
+        shapes = [g.shape[4:] for g in gradients] + self.inside
+        for index, shape in enumerate(self.inside):
+            made = cut(self.outside + index, shape[0], most * WIDTH // shape[1])
+            self.weave(made)
         count = len(self.chunks)
-        self.ticks = count + 4
-        shapes = [g.shape[4:] for g in gradients]
+        self.lag = lag
+        self.ticks = count + 4 * lag
         padded = [(-(-s[0] // 16) * 16, s[1]) for s in shapes]
+        self.total_count = len(shapes)
         self.in_specs = [ANY] * len(self.arrays)
         self.out_shapes = [jax.ShapeDtypeStruct(s, F32) for s in shapes]
         self.out_shapes += [jax.ShapeDtypeStruct(a.shape[1:], a.dtype) for a in swaps]
-        self.out_specs = [VMEM_WHOLE] * len(gradients) + [ANY] * len(swaps)
-        self.scratch = []
-        for lead in ((4, 2, 2), (4, 2, 2), (2, 4), (4,), (3,)):
+        self.out_specs = [VMEM_WHOLE] * len(shapes) + [ANY] * len(swaps)
+        self.scratch = [pltpu.VMEM((4, 2, 2) + s, BF16) for s in padded[: self.outside]]
+        self.scratch += [pltpu.VMEM((4, 2, 2, 2) + s, BF16) for s in self.inside]
+        for lead in ((4, 2, 2), (2, 4), (4,), (3,)):
             self.scratch += [pltpu.VMEM(lead + s, BF16) for s in padded]
         self.scratch += [
             DMA((count,)),
@@ -280,11 +298,22 @@
             DMA((max(self.swaps, 1),)),
         ]
 
+    def weave(self, made):
+        others, self.chunks, self.starts = self.chunks, [], []
+        for index, chunk in enumerate(made):
+            for _ in range(2 if index == 0 else 1):
+                if others:
+                    self.chunks.append(others.pop(0))
+            self.starts.append(len(self.chunks))
+            self.chunks.append(chunk)
+        self.chunks += others
+
     def bind(self, ins, outs, scratch):
-        n = self.gradients
+        n = self.total_count
         self.ins, self.outs = ins, outs
-        self.own, self.from_core, self.from_second, self.from_first, self.from_z = (
-            scratch[i * n : (i + 1) * n] for i in range(5)
+        self.own = scratch[:n]
+        self.from_core, self.from_second, self.from_first, self.from_z = (
+            scratch[i * n : (i + 1) * n] for i in range(1, 5)
         )
         (
             self.own_sem,
@@ -303,6 +332,12 @@
         array, start, rows = self.chunks[k]
         return array, pl.ds(start, rows)
 
+    def own_at(self, k, z, y, x):
+        array, rows = self.part(k)
+        if array < self.outside:
+            return self.own[array].at[z, y, x, rows, :]
+        return self.own[array].at[z, y, x, self.here.core, rows, :]
+
     def load(self, k):
         array, rows = self.part(k)
         return pltpu.make_async_copy(
@@ -313,8 +348,9 @@
 
     def swap_core(self, k):
         array, rows = self.part(k)
+        source = self.ins[array] if array < self.outside else self.own[array]
         return remote(
-            self.ins[array].at[:, :, :, 1 - self.here.core, rows, :],
+            source.at[:, :, :, 1 - self.here.core, rows, :],
             self.from_core[array].at[:, :, :, rows, :],
             self.c_send.at[k],
             self.c_recv.at[k],
@@ -325,7 +361,7 @@
         array, rows = self.part(k)
         where = self.here.second if index == 0 else self.here.across
         return remote(
-            self.own[array].at[:, where[0], where[1], rows, :],
+            self.own_at(k, slice(None), *where),
             self.from_second[array].at[index, :, rows, :],
             self.p_send.at[k, index],
             self.p_recv.at[k, index],
@@ -334,9 +370,8 @@
 
     def send_first(self, k):
         array, rows = self.part(k)
-        where = self.here.first
         return remote(
-            self.own[array].at[:, where[0], where[1], rows, :],
+            self.own_at(k, slice(None), *self.here.first),
             self.from_first[array].at[:, rows, :],
             self.p_send.at[k, 2],
             self.p_recv.at[k, 2],
@@ -347,7 +382,7 @@
         array, rows = self.part(k)
         here = self.here
         return remote(
-            self.own[array].at[lax.rem(here.z + step, 4), here.y, here.x, rows, :],
+            self.own_at(k, lax.rem(here.z + step, 4), *here.own),
             self.from_z[array].at[step - 1, rows, :],
             self.z_send.at[k, step - 1],
             self.z_recv.at[k, step - 1],
@@ -355,10 +390,10 @@
         )
 
     def swap(self, index):
-        source = self.ins[self.gradients + index]
+        source = self.ins[self.outside + index]
         return remote(
             source.at[1 - self.here.core],
-            self.outs[self.gradients + index],
+            self.outs[self.total_count + index],
             self.s_send.at[index],
             self.s_recv.at[index],
             self.here.sibling(),
@@ -366,31 +401,29 @@
 
     def add_all(self, k):
         array, rows = self.part(k)
-        own, other = self.own[array], self.from_core[array]
+        other = self.from_core[array]
 
         def body(i, carry):
             z, y, x = i // 4, lax.rem(i // 2, 2), lax.rem(i, 2)
-            own[z, y, x, rows, :] = both_sum(own[z, y, x, rows, :], other[z, y, x, rows, :])
+            own = self.own_at(k, z, y, x)
+            own[...] = both_sum(own[...], other[z, y, x, rows, :])
             return carry
 
         lax.fori_loop(0, 16, body, 0)
 
     def add_column(self, k, where, other):
-        array, rows = self.part(k)
-        own = self.own[array]
+        rows = self.part(k)[1]
 
         def body(z, carry):
-            own[z, where[0], where[1], rows, :] = both_sum(
-                own[z, where[0], where[1], rows, :], other[z, rows, :]
-            )
+            own = self.own_at(k, z, *where)
+            own[...] = both_sum(own[...], other[z, rows, :])
             return carry
 
         lax.fori_loop(0, 4, body, 0)
 
     def total(self, k):
         array, rows = self.part(k)
-        here = self.here
-        total = self.own[array][here.z, here.y, here.x, rows, :].astype(F32)
+        total = self.own_at(k, self.here.z, *self.here.own)[...].astype(F32)
         for step in range(3):
             total = total + self.from_z[array][step, rows, :].astype(F32)
         self.outs[array][rows, :] = total
@@ -399,18 +432,22 @@
         count = len(self.chunks)
         if tick < count:
             self.swap_core(tick).start()
-            self.load(tick).start()
+            if self.chunks[tick][0] < self.outside:
+                self.load(tick).start()
         if tick == 1:
             for index in range(self.swaps):
                 self.swap(index).start()
-        k = tick - 1
+        k = tick - self.lag
         if 0 <= k < count:
-            self.load(k).wait()
+            if self.chunks[k][0] < self.outside:
+                self.load(k).wait()
+            else:
+                self.swap_core(k).wait_send()
             self.swap_core(k).wait_recv()
             self.add_all(k)
             for index in (1, 0):
                 self.send_second(k, index).start()
-        k = tick - 2
+        k = tick - 2 * self.lag
         if 0 <= k < count:
             array = self.chunks[k][0]
             self.send_second(k, 1).wait_recv()
@@ -418,14 +455,14 @@
             self.send_first(k).start()
             self.send_second(k, 0).wait_recv()
             self.add_column(k, self.here.own, self.from_second[array].at[0])
-        k = tick - 3
+        k = tick - 3 * self.lag
         if 0 <= k < count:
             array = self.chunks[k][0]
             self.send_first(k).wait_recv()
             self.add_column(k, self.here.own, self.from_first[array])
             for step in (2, 1, 3):
                 self.send_z(k, step).start()
-        k = tick - 4
+        k = tick - 4 * self.lag
         if 0 <= k < count:
             for step in (1, 2, 3):
                 self.send_z(k, step).wait_recv()
@@ -433,7 +470,8 @@
 
     def finish(self):
         for k in range(len(self.chunks)):
-            self.swap_core(k).wait_send()
+            if self.chunks[k][0] < self.outside:
+                self.swap_core(k).wait_send()
             for index in (1, 0):
                 self.send_second(k, index).wait_send()
             self.send_first(k).wait_send()
@@ -476,7 +514,7 @@
     yield (buffer[6] + buffer[7]) + (buffer[8] + buffer[9])
 
 
-def call(name, body, grid, inner, ins, in_specs, out_shapes, out_specs, scratch=(), comm=None, key=0):
+def call(name, body, grid, inner, ins, in_specs, out_shapes, out_specs, scratch=(), comm=None, key=0, plan=None):
     params = {"vmem_limit_bytes": VMEM_LIMIT}
     if comm is None:
 
@@ -499,7 +537,7 @@
 
             def pump(point):
                 for tick in range(comm.ticks):
-                    slot = tick * grid * inner // comm.ticks
+                    slot = plan[tick] if plan else tick * grid * inner // comm.ticks
                     if slot % inner == point:
 
                         @pl.when(step == slot // inner)
@@ -527,80 +565,44 @@
     return results[: len(out_shapes)], results[len(out_shapes) :]
 
 
-def gather_now(comm, key):
-    def kernel(*refs):
-        sizes = (len(comm.arrays), len(comm.out_shapes))
-        comm.bind(refs[: sizes[0]], refs[sizes[0] : sum(sizes)], refs[sum(sizes) :])
-        comm.here.greet()
-        for tick in range(comm.ticks):
-            comm.tick(tick)
-        comm.finish()
+def settle(rows, gains, sums, key):
+    def kernel(rows_ref, gains_ref, *refs):
+        sums_refs = refs[: len(sums)]
+        got_ref, gains_out, square_out, buffer, send, recv, s_send, s_recv = refs[len(sums) :]
+        here = Place()
+        here.greet()
+        swap = remote(rows_ref.at[1 - here.core], got_ref, s_send, s_recv, here.sibling())
+        swap.start()
+        squares = jnp.zeros((8, 128), F32)
+        for ref in sums_refs:
+            values = ref[...]
+            squares = squares + jnp.sum((values * values).reshape(-1, 8, 128), axis=0)
+        for total in everywhere(
+            here, buffer, jnp.concatenate([gains_ref[...], squares], axis=0), send, recv
+        ):
+            pass
+        gains_total = total[:16]
+        gains_out[...] = gains_total
+        square_out[...] = jnp.broadcast_to(
+            jnp.sum(total[16:]) + jnp.sum(gains_total * gains_total), (8, 128)
+        )
+        swap.wait()
 
     return pl.pallas_call(
         kernel,
-        out_shape=comm.out_shapes,
-        in_specs=comm.in_specs,
-        out_specs=comm.out_specs,
-        scratch_shapes=comm.scratch,
+        out_shape=[
+            jax.ShapeDtypeStruct(rows.shape[1:], F32),
+            jax.ShapeDtypeStruct((16, 128), F32),
+            jax.ShapeDtypeStruct((8, 128), F32),
+        ],
+        in_specs=[ANY, VMEM_WHOLE] + [VMEM_WHOLE] * len(sums),
+        out_specs=[ANY, VMEM_WHOLE, VMEM_WHOLE],
+        scratch_shapes=[pltpu.VMEM((10, 24, 128), F32), DMA((6,)), DMA((6,)), DMA, DMA],
         compiler_params=pltpu.CompilerParams(
             collective_id=key, has_side_effects=True, vmem_limit_bytes=VMEM_LIMIT
         ),
-        name="gather_first",
-    )(*comm.arrays)
-
-
-def reduce_last(comm, gains, sums, key):
-    def kernel(*refs):
-        outs = len(comm.out_shapes)
-        ins = refs[: len(comm.arrays)]
-        gains_ref = refs[len(ins)]
-        sums_refs = refs[len(ins) + 1 : len(ins) + 1 + len(sums)]
-        at = len(ins) + 1 + len(sums)
-        comm_outs, gains_out, square_out = refs[at : at + outs], refs[at + outs], refs[at + outs + 1]
-        small, tiny, g_send, g_recv, n_send, n_recv = refs[at + outs + 2 : at + outs + 8]
-        comm.bind(ins, comm_outs, refs[at + outs + 8 :])
-        here = comm.here
-        here.greet()
-        gains_steps = everywhere(here, small, gains_ref[...], g_send, g_recv)
-        for tick in range(comm.ticks):
-            comm.tick(tick)
-            if tick < 5:
-                gains_total = next(gains_steps)
-        gains_out[...] = gains_total
-        squares = jnp.zeros((8, 128), F32)
-        for ref in (*sums_refs, *comm_outs[: comm.gradients]):
-            values = ref[...]
-            squares = squares + jnp.sum((values * values).reshape(-1, 8, 128), axis=0)
-        for total in everywhere(here, tiny, squares, n_send, n_recv):
-            pass
-        square_out[...] = jnp.broadcast_to(
-            jnp.sum(total) + jnp.sum(gains_total * gains_total), (8, 128)
-        )
-        comm.finish()
-
-    return pl.pallas_call(
-        kernel,
-        out_shape=[
-            *comm.out_shapes,
-            jax.ShapeDtypeStruct((16, 128), F32),
-            jax.ShapeDtypeStruct((8, 128), F32),
-        ],
-        in_specs=[*comm.in_specs, VMEM_WHOLE, *([VMEM_WHOLE] * len(sums))],
-        out_specs=[*comm.out_specs, VMEM_WHOLE, VMEM_WHOLE],
-        scratch_shapes=[
-            pltpu.VMEM((10, 16, 128), F32),
-            pltpu.VMEM((10, 8, 128), F32),
-            DMA((6,)),
-            DMA((6,)),
-            DMA((6,)),
-            DMA((6,)),
-            *comm.scratch,
-        ],
-        compiler_params=pltpu.CompilerParams(
-            collective_id=key, has_side_effects=True, vmem_limit_bytes=VMEM_LIMIT
-        ),
-        name="reduce_last",
-    )(*comm.arrays, gains, *sums)
+        name="settle",
+    )(rows, gains, *sums)
 
 
 def segment_lanes(counts):
@@ -619,21 +621,15 @@
     return lane, (lane < HD, lane >= HD)
 
 
-def attend_body(pump, q_ref, k_ref, v_ref, mq_ref, mk_ref, o_ref, log_ref):
-    pair = pl.program_id(0)
+def attend_tiles(pump, pair, q_ref, k_ref, v_ref, mq_ref, mk_ref, o_ref, log_ref):
     lane, in_head = lanes_of_heads()
-
-    @pl.when(pair == 0)
-    def _():
-        log_ref[...] = jnp.zeros_like(log_ref)
-
-    key = jnp.concatenate([k_ref[0], mk_ref[...]], axis=1)
-    value = v_ref[0]
+    key = jnp.concatenate([k_ref[...], mk_ref[...]], axis=1)
+    value = v_ref[...]
     values = [jnp.where(mine, value, jnp.ones_like(value)) for mine in in_head]
     for index in range(ROW // QUERY_TILE):
         pump(index)
         rows = pl.ds(index * QUERY_TILE, QUERY_TILE)
-        query, extra = q_ref[0, rows, :], mq_ref[rows, :]
+        query, extra = q_ref[rows, :], mq_ref[rows, :]
         mixed = []
         logs = log_ref[rows, :]
         for head in range(2):
@@ -650,6 +646,18 @@
         o_ref[rows, :] = jnp.where(in_head[0], mixed[0], mixed[1]).astype(BF16)
 
 
+def attend_body(pump, q_ref, k_ref, v_ref, mq_ref, mk_ref, o_ref, log_ref):
+    pair = pl.program_id(0)
+
+    @pl.when(pair == 0)
+    def _():
+        log_ref[...] = jnp.zeros_like(log_ref)
+
+    attend_tiles(
+        pump, pair, q_ref.at[0], k_ref.at[0], v_ref.at[0], mq_ref, mk_ref, o_ref, log_ref
+    )
+
+
 PAIRS = WIDTH // (2 * HD)
 
 
@@ -657,7 +665,7 @@
     return pl.BlockSpec((1, ROW, 2 * HD), lambda p: (which, 0, p))
 
 
-def attend(projected, extras, comm=None, key=0):
+def attend(projected, extras):
     whole = pl.BlockSpec((ROW, 128), lambda p: (0, 0))
     return call(
         "attend",
@@ -668,15 +676,12 @@
         [third(0), third(1), third(2), whole, whole],
         [jax.ShapeDtypeStruct((ROW, WIDTH), BF16), jax.ShapeDtypeStruct((ROW, 128), F32)],
         [pl.BlockSpec((ROW, 2 * HD), lambda p: (0, p)), whole],
-        comm=comm,
-        key=key,
-    )
-
-
-def attend_back_body(
-    pump, q_ref, k_ref, v_ref, mq_ref, mk_ref, o_ref, do_ref, log_ref, out_ref, dk, dv
+    )
+
+
+def attend_back_tiles(
+    pump, pair, q_ref, k_ref, v_ref, mq_ref, mk_ref, o_ref, do_ref, log_ref, dq_ref, dk, dv
 ):
-    pair = pl.program_id(0)
     _, in_head = lanes_of_heads()
     pick = jnp.where(
         (lax.broadcasted_iota(jnp.int32, (8, 2 * HD), 1) < HD)
@@ -693,8 +698,8 @@
     for index in range(ROW // BACK_TILE):
         pump(index)
         rows = pl.ds(index * BACK_TILE, BACK_TILE)
-        query, grad, extra = q_ref[0, rows, :], do_ref[rows, :], mq_ref[rows, :]
-        key, value = k_ref[0], v_ref[0]
+        query, grad, extra = q_ref[rows, :], do_ref[rows, :], mq_ref[rows, :]
+        key, value = k_ref[...], v_ref[...]
         inner = lax.dot_general(
             pick,
             grad.astype(F32) * o_ref[rows, :].astype(F32),
@@ -719,12 +724,21 @@
             dk[...] += dot(slope, only(query, head))
             step = dot(slope, only(key, head), TN)
             dq = step if dq is None else dq + step
-        out_ref[0, rows, :] = dq.astype(BF16)
+        dq_ref[rows, :] = dq.astype(BF16)
+
+
+def attend_back_body(
+    pump, q_ref, k_ref, v_ref, mq_ref, mk_ref, o_ref, do_ref, log_ref, out_ref, dk, dv
+):
+    attend_back_tiles(
+        pump, pl.program_id(0), q_ref.at[0], k_ref.at[0], v_ref.at[0], mq_ref, mk_ref, o_ref,
+        do_ref, log_ref, out_ref.at[0], dk, dv,
+    )
     out_ref[1] = dk[...].astype(BF16)
     out_ref[2] = dv[...].astype(BF16)
 
 
-def attend_back(projected, extras, mixed, grad_mixed, log_rows, comm=None, key=0):
+def attend_back(projected, extras, mixed, grad_mixed, log_rows):
     whole = pl.BlockSpec((ROW, 128), lambda p: (0, 0))
     column = pl.BlockSpec((ROW, 2 * HD), lambda p: (0, p))
     return call(
@@ -738,8 +752,6 @@
         [jax.ShapeDtypeStruct((3, ROW, WIDTH), BF16)],
         [pl.BlockSpec((3, ROW, 2 * HD), lambda p: (0, 0, p))],
         [pltpu.VMEM((ROW, 2 * HD), F32), pltpu.VMEM((ROW, 2 * HD), F32)],
-        comm=comm,
-        key=key,
     )
 
 
@@ -889,6 +901,314 @@
         [pltpu.VMEM((ROW, WIDTH), F32), DMA((2,))],
         comm=comm,
         key=key,
+    )
+
+
+def front(attention_shard, gains_tile, feed_shards, tokens, cotangent, extras, key):
+    comm = Gather((gains_tile, attention_shard, *feed_shards), (cotangent,), most=16, lag=2)
+    points = [0] * 7 + [1] * 2
+    rest = comm.ticks - len(points)
+    points += [2 + tick * (5 * PAIRS - 2) // rest for tick in range(rest)]
+
+    def body(
+        pump, tokens_ref, mq_ref, mk_ref,
+        turned_ref, row_ref, qkv_ref, o_ref, o_turned_ref, log_ref, h1_ref, n2_ref,
+        normed, landed, parts, out_weights, o_all, gains, t_send, t_recv, part_sem, gains_sem,
+    ):
+        pair = pl.program_id(0)
+        here = comm.here
+        core = here.core
+        across = remote(tokens_ref.at[1 - core], landed, t_send, t_recv, here.sibling())
+
+        def fetch(p, slot):
+            return pltpu.make_async_copy(
+                comm.outs[1].at[:, :, :, :, pl.ds(128 * p, 128), :], parts.at[slot], part_sem.at[slot]
+            )
+
+        pump(0)
+
+        @pl.when(pair == 0)
+        def _():
+            across.start()
+            log_ref[...] = jnp.zeros_like(log_ref)
+            row_ref[core] = tokens_ref[core]
+            across.wait_recv()
+            row_ref[1 - core] = landed[...]
+            comm.arrived(0)
+            copy = pltpu.make_async_copy(comm.outs[0], gains, gains_sem)
+            copy.start()
+            copy.wait()
+
+        def gain_of(which):
+            tiles = [
+                gains[which * 2 + z, y, x, 0, 0:1, :] + gains[which * 2 + z, y, x, 1, 0:1, :]
+                for z in range(2)
+                for y in range(2)
+                for x in range(2)
+            ]
+            return jnp.concatenate(tiles, axis=1).astype(F32)
+
+        @pl.when(pair == 0)
+        def _():
+            gain = gain_of(0)
+            for half in range(2):
+
+                def tile(i, carry, half=half):
+                    rows = pl.ds(pl.multiple_of(i * 64, 64), 64)
+                    x = row_ref[half, rows, :].astype(F32)
+                    scale = lax.rsqrt(jnp.mean(x * x, axis=-1, keepdims=True) + NORM_EPS)
+                    normed[pl.ds(pl.multiple_of(half * HALF + i * 64, 64), 64), :] = (
+                        x * scale * gain
+                    ).astype(BF16)
+                    return carry
+
+                lax.fori_loop(0, HALF // 64, tile, 0)
+            turned_ref[...] = normed[...].T
+
+        pump(1)
+
+        @pl.when(pair == 0)
+        def _():
+            comm.arrived(1)
+            fetch(0, 0).start()
+
+        slot = lax.rem(pair, 2)
+        fetch(pair, slot).wait()
+        weights = parts[slot].reshape(4, WIDTH, 128)
+        three = dot(normed[...], jnp.concatenate([weights[0], weights[1], weights[2]], axis=1))
+        for index in range(3):
+            qkv_ref[index] = three[:, 128 * index : 128 * (index + 1)].astype(BF16)
+        out_weights[pair] = weights[3]
+        pump(2)
+        for p in range(1, PAIRS):
+
+            @pl.when(pair == p - 1)
+            def _(p=p):
+                comm.arrived(1 + p)
+                fetch(p, p % 2).start()
+
+        attend_tiles(
+            lambda index: pump(3 + index),
+            pair,
+            qkv_ref.at[0],
+            qkv_ref.at[1],
+            qkv_ref.at[2],
+            mq_ref,
+            mk_ref,
+            o_ref,
+            log_ref,
+        )
+        mixed = o_ref[...]
+        o_all[:, pl.ds(pl.multiple_of(pair * 128, 128), 128)] = mixed
+        o_turned_ref[...] = mixed.T
+
+        @pl.when(pair == PAIRS - 1)
+        def _():
+            across.wait_send()
+            full = jnp.concatenate([out_weights[p] for p in range(PAIRS)], axis=1)
+            gain = gain_of(1)
+            for part in range(4):
+                rows = pl.ds(part * (ROW // 4), ROW // 4)
+                x = row_ref[part // 2, pl.ds((part % 2) * (ROW // 4), ROW // 4), :].astype(F32)
+                h1_ref[rows, :] = x + dot(o_all[rows, :], full)
+
+            def tile(i, carry):
+                rows = pl.ds(pl.multiple_of(i * 64, 64), 64)
+                h1 = h1_ref[rows, :]
+                scale = lax.rsqrt(jnp.mean(h1 * h1, axis=-1, keepdims=True) + NORM_EPS)
+                n2_ref[rows, :] = (h1 * scale * gain).astype(BF16)
+                return carry
+
+            lax.fori_loop(0, ROW // 64, tile, 0)
+
+    whole = pl.BlockSpec((ROW, 128), lambda p: (0, 0))
+    turned = jax.ShapeDtypeStruct((WIDTH, ROW), BF16)
+    return call(
+        "front",
+        body,
+        PAIRS,
+        5,
+        [tokens, *extras],
+        [VMEM_WHOLE, whole, whole],
+        [
+            turned,
+            jax.ShapeDtypeStruct((2, HALF, WIDTH), BF16),
+            jax.ShapeDtypeStruct((3, ROW, WIDTH), BF16),
+            ROW_BF16,
+            turned,
+            jax.ShapeDtypeStruct((ROW, 128), F32),
+            ROW_F32,
+            ROW_BF16,
+        ],
+        [
+            whole_block(WIDTH, ROW),
+            whole_block(2, HALF, WIDTH),
+            pl.BlockSpec((3, ROW, 128), lambda p: (0, 0, p)),
+            pl.BlockSpec((ROW, 128), lambda p: (0, p)),
+            pl.BlockSpec((128, ROW), lambda p: (p, 0)),
+            whole,
+            whole_block(ROW, WIDTH),
+            whole_block(ROW, WIDTH),
+        ],
+        [
+            pltpu.VMEM((ROW, WIDTH), BF16),
+            pltpu.VMEM((HALF, WIDTH), BF16),
+            pltpu.VMEM((2, 4, 2, 2, 2, 128, 128), BF16),
+            pltpu.VMEM((PAIRS, WIDTH, 128), BF16),
+            pltpu.VMEM((ROW, WIDTH), BF16),
+            pltpu.VMEM((4, 2, 2, 2, 16, 128), BF16),
+            DMA,
+            DMA,
+            DMA((2,)),
+            DMA,
+        ],
+        comm,
+        key,
+        points,
+    )
+
+
+PART = 144
+
+
+def back(
+    gradients, result, e, dh1, tokens_row, gain, projected, extras, mixed, log_rows,
+    attention_parts, normed_turned, mixed_turned, key,
+):
+    comm = Reduce(gradients, [(PAIRS * 128, 128)], (result,), most=16, lag=1)
+    inner, made, rest = 6, 4, 5
+    plan = []
+    for tick in range(comm.ticks):
+        if tick in comm.starts:
+            plan.append(comm.starts.index(tick) * inner + made)
+        elif tick < 2:
+            plan.append(tick)
+        elif tick < comm.starts[-1]:
+            plan.append((plan[-1] // inner + 1) * inner + 2)
+        else:
+            plan.append((PAIRS - 1) * inner + rest)
+
+    def body(
+        pump, q_ref, k_ref, v_ref, mq_ref, mk_ref, o_ref, log_ref, parts_ref, rows_ref,
+        e_ref, n_turned_ref, o_turned_ref, gain_ref, tokens_ref, dh1_ref,
+        da_ref, gain_grad_ref,
+        do, three, dk, dv, x_part, dh1_part, x_sem, dh1_sem,
+    ):
+        pair = pl.program_id(0)
+        pump(0)
+        out_rows = rows_ref[0, 0, 0, 0]
+        out_rows = jnp.concatenate(
+            [out_rows[128 * p : 128 * (p + 1)] for p in range(PAIRS)], axis=1
+        )
+        do[...] = dot(e_ref[...], out_rows, NT).astype(BF16)
+        attend_back_tiles(
+            lambda index: pump(1 + index), pair, q_ref.at[0], k_ref.at[0], v_ref.at[0],
+            mq_ref, mk_ref, o_ref, do, log_ref, three.at[:, 0:128], dk, dv,
+        )
+        three[:, 128:256] = dk[...].astype(BF16)
+        three[:, 256:384] = dv[...].astype(BF16)
+        made_ref = comm.own[comm.outside]
+        mine = pl.ds(pl.multiple_of(pair * 128, 128), 128)
+        grads = dot(n_turned_ref[...], three[...]).astype(BF16)
+        for index in range(3):
+            made_ref[index, :, :, :, mine, :] = grads[
+                :, 128 * index : 128 * (index + 1)
+            ].reshape(2, 2, 2, 128, 128)
+        made_ref[3, :, :, :, mine, :] = (
+            dot(o_turned_ref[...], e_ref[:, mine]).astype(BF16).reshape(2, 2, 2, 128, 128)
+        )
+        pump(made)
+        weights = parts_ref[...].reshape(4, WIDTH, 128)
+        columns = jnp.concatenate([weights[0], weights[1], weights[2]], axis=1)
+
+        @pl.when(pair == 0)
+        def _():
+            da_ref[...] = dot(three[...], columns, NT)
+
+        @pl.when(pair > 0)
+        def _():
+            da_ref[...] += dot(three[...], columns, NT)
+
+        @pl.when(pair == PAIRS - 1)
+        def _():
+            def fetch(i):
+                rows = pl.ds(i * PART, PART)
+                slot = i % 2
+                return (
+                    pltpu.make_async_copy(tokens_ref.at[rows, :], x_part.at[slot], x_sem.at[slot]),
+                    pltpu.make_async_copy(dh1_ref.at[rows, :], dh1_part.at[slot], dh1_sem.at[slot]),
+                )
+
+            gain_row = gain_ref[...]
+            total = jnp.zeros((8, WIDTH), F32)
+            for copy in fetch(0):
+                copy.start()
+            for i in range(ROW // PART):
+                if i + 1 < ROW // PART:
+                    for copy in fetch(i + 1):
+                        copy.start()
+                for copy in fetch(i):
+                    copy.wait()
+
+                def tile(j, total, i=i):
+                    near = pl.ds(pl.multiple_of(j * 48, 16), 48)
+                    rows = pl.ds(pl.multiple_of(i * PART + j * 48, 16), 48)
+                    x = x_part[i % 2, near, :].astype(F32)
+                    grad = da_ref[rows, :]
+                    scale = lax.rsqrt(jnp.mean(x * x, axis=-1, keepdims=True) + NORM_EPS)
+                    lifted = gain_row * grad
+                    middle = jnp.mean(x * lifted, axis=-1, keepdims=True)
+                    da_ref[rows, :] = (
+                        dh1_part[i % 2, near, :]
+                        + scale * lifted
+                        - x * (scale * scale * scale * middle)
+                    )
+                    return total + jnp.sum((grad * x * scale).reshape(6, 8, WIDTH), axis=0)
+
+                total = lax.fori_loop(0, PART // 48, tile, total)
+            gain_grad_ref[...] = jnp.sum(total, axis=0, keepdims=True)
+
+        pump(rest)
+
+    extra = pl.BlockSpec((ROW, 128), lambda p: (0, 0), pipeline_mode=pl.Buffered(1))
+    line = whole_block(1, WIDTH)
+    return call(
+        "back",
+        body,
+        PAIRS,
+        inner,
+        [projected, projected, projected, *extras, mixed, log_rows, attention_parts, attention_parts]
+        + [e, normed_turned, mixed_turned, gain, tokens_row, dh1],
+        [third(0), third(1), third(2), extra, extra]
+        + [
+            pl.BlockSpec((ROW, 128), lambda p: (0, p)),
+            whole_block(2 * PAIRS, ROW),
+            pl.BlockSpec((4, 2, 2, 2, 128, 128), lambda p: (0, 0, 0, 0, p, 0)),
+            pl.BlockSpec(
+                (1, 1, 1, 1, WIDTH, 128), lambda p: (3, p // 4, lax.rem(p // 2, 2), lax.rem(p, 2), 0, 0)
+            ),
+            whole_block(ROW, WIDTH),
+            whole_block(WIDTH, ROW),
+            whole_block(WIDTH, ROW),
+            line,
+            ANY,
+            ANY,
+        ],
+        [ROW_F32, jax.ShapeDtypeStruct((1, WIDTH), F32)],
+        [whole_block(ROW, WIDTH), line],
+        [
+            pltpu.VMEM((ROW, 128), BF16),
+            pltpu.VMEM((ROW, 384), BF16),
+            pltpu.VMEM((ROW, 128), F32),
+            pltpu.VMEM((ROW, 128), F32),
+            pltpu.VMEM((2, PART, WIDTH), BF16),
+            pltpu.VMEM((2, PART, WIDTH), F32),
+            DMA((2,)),
+            DMA((2,)),
+        ],
+        comm,
+        key,
+        plan,
     )
 
 
@@ -980,14 +1300,23 @@
     def as_shards(*gradients):
         return [g.reshape(grid + (-1, WIDTH)) for g in gradients]
 
-    gather_a = gather_b = None
+    counts = lax.dynamic_index_in_dim(images[:, 0, :], core, 0, keepdims=False)
+    extras = segment_lanes(counts)
+    gather_b = None
     if own_kernels:
-        gains_tile = jnp.zeros((16, 128), BF16).at[0, :gain_count].set(gains_low)
-        attention_full, gains_full, tokens_row, cotangent_row = gather_now(
-            Gather((attention_low, gains_tile), (tokens, cotangent)), 0
-        )
-        gains_full = gains_full.reshape(devices, 16, 128)[:, 0, :gain_count].reshape(-1)
-        gather_a, gather_b = Gather(feed_low[0]), Gather(feed_low[1])
+        spread = jnp.zeros((2, gain_count), BF16).at[core].set(gains_low).reshape(1, -1)
+        gains_tile = jnp.concatenate([spread, jnp.zeros((15, 2 * gain_count), BF16)], axis=0)
+        columns = attention_low.reshape(-1, PAIRS, 2 * HD).transpose(1, 0, 2).reshape(-1, 2 * HD)
+        (
+            (normed_turned, tokens_row, projected, mixed, mixed_turned, log_columns, h1, n2),
+            (gains_full, attention_parts, *feed_a, cotangent_row),
+        ) = front(columns, gains_tile, feed_low[0], tokens, cotangent, extras, 0)
+        gains_full = gains_full[:, :, :, :, 0, :].sum(axis=3).reshape(-1)
+        gather_b = Gather(feed_low[1])
+        cot = cotangent_row.reshape(ROW, WIDTH)
+        inputs = tokens_row.reshape(ROW, WIDTH).astype(F32)
+        first_gain = gains_full[:WIDTH].astype(F32)
+        second_gain = gains_full[WIDTH:].astype(F32)
     else:
         attention_full, gains_full = fetch((attention_low, gains_low))
         first = core == 0
@@ -995,22 +1324,19 @@
             jnp.where(first, jnp.stack([a[0], got]), jnp.stack([got, a[1]]))
             for a, got in ((a, other_half(a)) for a in (tokens, cotangent))
         )
-    counts = lax.dynamic_index_in_dim(images[:, 0, :], core, 0, keepdims=False)
-    attention = attention_full.reshape(4, WIDTH, WIDTH)
-    cot = cotangent_row.reshape(ROW, WIDTH)
-    inputs = tokens_row.reshape(ROW, WIDTH).astype(F32)
-    first_gain = gains_full[:WIDTH].astype(F32)
-    second_gain = gains_full[WIDTH:].astype(F32)
-
-    normed = rms_scale(inputs, first_gain).astype(BF16)
-    projected = jnp.einsum(
-        "sd,jde->jse", normed, attention[:3], preferred_element_type=F32
-    ).astype(BF16)
-    extras = segment_lanes(counts)
-    (mixed, log_columns), feed_a = attend(projected, extras, gather_a, 1)
+        attention = attention_full.reshape(4, WIDTH, WIDTH)
+        cot = cotangent_row.reshape(ROW, WIDTH)
+        inputs = tokens_row.reshape(ROW, WIDTH).astype(F32)
+        first_gain = gains_full[:WIDTH].astype(F32)
+        second_gain = gains_full[WIDTH:].astype(F32)
+        normed = rms_scale(inputs, first_gain).astype(BF16)
+        projected = jnp.einsum(
+            "sd,jde->jse", normed, attention[:3], preferred_element_type=F32
+        ).astype(BF16)
+        (mixed, log_columns), _ = attend(projected, extras)
+        h1 = inputs + dot(mixed, attention[3])
+        n2 = rms_scale(h1, second_gain).astype(BF16)
     log_rows = log_columns[:, : WIDTH // HD].T
-    h1 = inputs + dot(mixed, attention[3])
-    n2 = rms_scale(h1, second_gain).astype(BF16)
     widen_a, narrow_a = as_feed(feed_a if own_kernels else fetch(feed_low[0]))
     (result_part, back_part, *grads_a), feed_b = feed_start(
         n2, cot, widen_a, narrow_a, gather_b, 2
@@ -1028,44 +1354,53 @@
         Reduce(as_shards(*grads_a)) if own_kernels else None,
         3,
     )
-    grad_out = dot(mixed, e, TN).astype(BF16)
-    grad_mixed = dot(e, attention[3], NT).astype(BF16)
-    (grad_projected,), sums_b = attend_back(
-        projected,
-        extras,
-        mixed,
-        grad_mixed,
-        log_rows,
-        Reduce(as_shards(*grads_b), (result.reshape(2, HALF, WIDTH),)) if own_kernels else None,
-        4,
-    )
-    grad_qkv = jnp.einsum(
-        "sd,jse->jde", normed, grad_projected, preferred_element_type=F32
-    ).astype(BF16)
-    grad_normed = jnp.einsum(
-        "jse,jde->sd", grad_projected, attention[:3], preferred_element_type=F32
-    )
-    scale = lax.rsqrt(jnp.mean(inputs * inputs, axis=-1, keepdims=True) + NORM_EPS)
-    lifted = first_gain * grad_normed
-    inner = jnp.mean(inputs * lifted, axis=-1, keepdims=True)
-    input_rows = dh1 + scale * lifted - inputs * (scale * scale * scale * inner)
-    grad_gain_one = jnp.sum(grad_normed * inputs * scale, axis=0)
-    grad_attention = jnp.concatenate([grad_qkv, grad_out[None]], axis=0)
-    grad_gains = jnp.concatenate([grad_gain_one, grad_gain_two[0]])
-
     if own_kernels:
-        *sums_b, got_result = sums_b
-        attention_sum, got_input, gains_total, square_total = reduce_last(
-            Reduce(as_shards(grad_attention), (input_rows.reshape(2, HALF, WIDTH),)),
-            grad_gains.reshape(16, 128),
-            [*sums_a, *sums_b],
+        (input_rows, grad_gain_one), (*sums_b, attention_sum, got_result) = back(
+            as_shards(*grads_b),
+            result.reshape(2, HALF, WIDTH),
+            e,
+            dh1,
+            tokens_row.reshape(ROW, WIDTH),
+            first_gain[None],
+            projected,
+            extras,
+            mixed,
+            log_rows,
+            attention_parts,
+            normed_turned,
+            mixed_turned,
+            4,
+        )
+        got_input, gains_total, square_total = settle(
+            input_rows.reshape(2, HALF, WIDTH),
+            jnp.concatenate([grad_gain_one, grad_gain_two]).reshape(16, 128),
+            [*sums_a, *sums_b, attention_sum],
             5,
+        )
+        attention_sum = (
+            attention_sum.reshape(PAIRS, -1, 128).transpose(1, 0, 2).reshape(-1, WIDTH)
         )
         gains_sum = lax.dynamic_slice_in_dim(
             gains_total.reshape(-1), position * gain_count, gain_count
         )
         squares = square_total[0, 0]
     else:
+        grad_out = dot(mixed, e, TN).astype(BF16)
+        grad_mixed = dot(e, attention[3], NT).astype(BF16)
+        (grad_projected,), _ = attend_back(projected, extras, mixed, grad_mixed, log_rows)
+        grad_qkv = jnp.einsum(
+            "sd,jse->jde", normed, grad_projected, preferred_element_type=F32
+        ).astype(BF16)
+        grad_normed = jnp.einsum(
+            "jse,jde->sd", grad_projected, attention[:3], preferred_element_type=F32
+        )
+        scale = lax.rsqrt(jnp.mean(inputs * inputs, axis=-1, keepdims=True) + NORM_EPS)
+        lifted = first_gain * grad_normed
+        inner = jnp.mean(inputs * lifted, axis=-1, keepdims=True)
+        input_rows = dh1 + scale * lifted - inputs * (scale * scale * scale * inner)
+        grad_gain_one = jnp.sum(grad_normed * inputs * scale, axis=0)
+        grad_attention = jnp.concatenate([grad_qkv, grad_out[None]], axis=0)
+        grad_gains = jnp.concatenate([grad_gain_one, grad_gain_two[0]])
         sums_a, sums_b, (attention_sum,) = summed(grads_a), summed(grads_b), summed([grad_attention])
         gains_sum = lax.psum_scatter(grad_gains, axes, scatter_dimension=0, tiled=True)
         squares = lax.psum(

time: 544 us -> 476 us (0.88); the launches traced: 541 us -> 467 us
  matrix products: 48.8 us -> 0 us
  local copies, waits for them, and re-layouts: 24.3 us -> 11.8 us
  other arithmetic: 33.2 us -> 21.5 us
    pallas_call x2 -> x1, Pallas kernels: 123 us -> 17 us  [settle(): pl.pallas_call(kernel, out_shape=[jax.ShapeDtypeStruct(rows.shape[1:], F3...]
    pallas_call x4, Pallas kernels: 304 us -> 410 us  [call(): pl.pallas_call(kernel, grid=(grid,), out_shape=[*out_shapes, *extra[2]],...]
    dot_general x6 -> x0, matrix products: 48.8 us -> none  [the longest x3 18.3 us: dot(): return lax.dot_general(left, right, dims, preferred_element_type=F32)]
    slice x3 -> x0, local copies, waits for them, and re-layouts: 7.49 us -> none  [the longest x1 3.64 us: local(): attention[:3]]
where the time goes in v3:
time: 476 us; the launch traced here: 467 us
  Pallas kernels  427 us (90%)
  other arithmetic  21.5 us (5%)
  local copies, waits for them, and re-layouts  11.8 us (2%)
  between operations  6.98 us (1%)
    pallas_call x4, Pallas kernels, call(): pl.pallas_call(kernel, grid=(grid,), out_shape=[*out_shapes, *extra[2]],...  410 us
    pallas_call x1, Pallas kernels, settle(): pl.pallas_call(kernel, out_shape=[jax.ShapeDtypeStruct(rows.shape[1:], F3...  17 us

profile of v3, /device:TPU:0, one launch (start us, length us, event | category | flops | bytes accessed | tf_op | source)
XLA Modules:
  0.0 467.1 jit_solution(3574303009857088980)
XLA Ops:
  0.6 0.0 copy-start
  0.7 1.4 and_reduce_fusion
  2.0 1.3 fusion.8
  3.4 0.1 reshape.243
  3.5 0.6 fusion.15
  8.0 0.6 concatenate.17.refs_3_
  8.6 1.0 convert_element_type.78
  9.6 0.6 slice.106.refs_5_
  10.2 0.6 slice.103.refs_6_
  10.9 1.8 copy_bitcast_fusion
  12.7 1.2 convert_element_type.77
  13.8 0.7 slice.105
  14.5 0.7 slice.102
  15.2 1.1 fusion.2
  16.3 111.8 %front.1 = (bf16[1024,1152]{1,0:T(8,128)(2,1)}, bf16[2,576,1024]{2,1,0:T(8,128)(2,1)}, bf16[3,1152,1024]{2,1,0:T(8,128)(2,1)}, bf16[1152,1024]{1,0:T(8,128)(2,1)...) custom-call(bf16[2,576,1024]{2,1,0:T(8,128)(2,1)} %refs_0_.1, ...), custom_call_target="tpu_custom_call" | custom-call | tf_op jit(solution)/shard_map/front/pallas_call | solution.py:555
  128.1 0.9 slice_reduce_fusion
  129.0 0.6 slice_convert_fusion
  129.6 1.3 copy.31
  130.9 0.6 slice_bitcast_fusion.4.refs_6_
  131.5 68.9 %feed_start.1 = (f32[1152,1024]{1,0:T(8,128)}, f32[1152,1024]{1,0:T(8,128)}, bf16[2,1536,1024]{2,1,0:T(8,128)(2,1)}, bf16[1536,1024]{1,0:T(8,128)(2,1)}, bf16[4,...) custom-call(bf16[1152,1024]{1,0:T(8,128)(2,1)} %get-tuple-element.63.refs_0_, ...), custom_call_target="tpu_custom_call" | custom-call | tf_op jit(solution)/shard_map/feed_start/pallas_call | solution.py:555
  200.4 76.3 %feed_end.1 = (f32[1152,1024]{1,0:T(8,128)}, f32[1152,1024]{1,0:T(8,128)}, bf16[1152,1024]{1,0:T(8,128)(2,1)}, f32[1,1024]{1,0:T(1,128)}, bf16[2,1280,1024]{2,1,...) custom-call(bf16[1152,1024]{1,0:T(8,128)(2,1)} %get-tuple-element.63.refs_0_, ...), custom_call_target="tpu_custom_call" | custom-call | tf_op jit(solution)/shard_map/feed_end/pallas_call | solution.py:555
  276.7 152.8 %back.1 = (f32[1152,1024]{1,0:T(8,128)}, f32[1,1024]{1,0:T(1,128)}, f32[80,1024]{1,0:T(8,128)}, f32[40,1024]{1,0:T(8,128)}, f32[1024,128]{1,0:T(8,128)}, /*index=5*/f32[576,1024]{1,0:T(8,128)}) custom-call(bf16[3,1152,1024]{2,1,0:T(8,128)(2,1)} %get-tuple-element.76.refs_0_.refs_1_.refs_2_, bf16[3,1152,1024]{2,1,0:T(8,128)(2,1)} %get-tuple-element.76.refs_0_.refs_1_.refs_2_, ...), custom_call_target="tpu_custom_call" | custom-call | tf_op jit(solution)/shard_map/back/pallas_call | solution.py:555
  429.6 0.0 copy-start.17
  429.6 0.0 copy-start.18
  429.6 0.0 copy-start.19
  429.6 0.0 copy-start.8
  429.6 0.8 pad_maximum_fusion
  430.5 0.6 reshape.261.gains_ref
  431.1 17.0 %settle.1 = (f32[576,1024]{1,0:T(8,128)}, f32[16,128]{1,0:T(8,128)}, f32[8,128]{1,0:T(8,128)}) custom-call(f32[2,576,1024]{2,1,0:T(8,128)} %bitcast.72, f32[16,128]{1,0:T(8,128)} %reshape.261.gains_ref, f32[96,1024]{1,0:T(8,128)} %get-tuple-element.91.refs_0_, f32[48,1024]{1,0:T(8,128)} %get-tuple-element.92.refs_1_, f32[80,1024]{1,0:T(8,128)} %get-tuple-element.93.refs_2_, ...), custom_call_target="tpu_custom_call" | custom-call | tf_op jit(solution)/shard_map/settle/pallas_call | solution.py:591
  448.0 0.0 copy-start.2
  448.0 1.3 slice.101
  450.0 0.0 copy-start.14
  450.1 0.0 copy-start.15
  450.1 0.0 copy-start.11
  450.1 0.0 copy-start.12
  450.1 0.1 maximum_multiply_fusion
  450.3 1.4 multiply_subtract_fusion.3
  451.7 0.0 slice-start.2
  451.7 2.4 multiply_subtract_fusion.2
  454.2 1.4 multiply_subtract_fusion.1
  455.6 1.7 multiply_subtract_fusion
  457.3 0.4 slice_bitcast_fusion
  457.7 0.9 slice-done
  458.5 0.3 slice-done.1
  458.9 0.4 slice_bitcast_fusion.2
  459.3 1.3 copy-done.3
  460.5 0.7 copy-done.4
  461.3 4.4 maximum_select_fusion
  (42 shorter events, 0.2 us)
Async XLA Ops:
  0.6 2.7 copy-start
  276.7 152.9 %copy-start.16 = (f32[1,1024]{1,0:T(1,128)S(1)}, f32[1,1024]{1,0:T(1,128)}, u32[]{:S(2)}) copy-start(f32[1,1024]{1,0:T(1,128)} %get-tuple-element.90) | copy-start | bytes 12292
  429.5 20.6 %copy-start.7 = (f32[96,1024]{1,0:T(8,128)S(1)}, f32[96,1024]{1,0:T(8,128)}, u32[]{:S(2)}) copy-start(f32[96,1024]{1,0:T(8,128)} %get-tuple-element.91.refs_0_) | copy-start | bytes 1179652
  429.5 20.6 %copy-start.9 = (f32[80,1024]{1,0:T(8,128)S(1)}, f32[80,1024]{1,0:T(8,128)}, u32[]{:S(2)}) copy-start(f32[80,1024]{1,0:T(8,128)} %get-tuple-element.93.refs_2_) | copy-start | bytes 983044
  429.5 20.6 %copy-start.6 = (f32[1024,128]{1,0:T(8,128)S(1)}, f32[1024,128]{1,0:T(8,128)}, u32[]{:S(2)}) copy-start(f32[1024,128]{1,0:T(8,128)} %get-tuple-element.95.refs_4_) | copy-start | bytes 1572868
  429.6 20.7 %copy-start.17 = (f32[64]{0:T(128)S(1)}, f32[64]{0:T(128)}, u32[]{:S(2)}) copy-start(f32[64]{0:T(128)} %param.29) | copy-start | bytes 772
  429.6 20.7 %copy-start.18 = (f32[64]{0:T(128)S(1)}, f32[64]{0:T(128)}, u32[]{:S(2)}) copy-start(f32[64]{0:T(128)} %param.31) | copy-start | bytes 772
  429.6 20.7 %copy-start.19 = (f32[64]{0:T(128)S(1)}, f32[64]{0:T(128)}, u32[]{:S(2)}) copy-start(f32[64]{0:T(128)} %param.30) | copy-start | bytes 772
  429.6 22.1 %copy-start.8 = (f32[88,1024]{1,0:T(8,128)S(1)}, f32[88,1024]{1,0:T(8,128)}, u32[]{:S(2)}) copy-start(f32[88,1024]{1,0:T(8,128)} %param.26) | copy-start | bytes 1081348
  429.6 22.1 %copy-start.10 = (f32[48,1024]{1,0:T(8,128)S(1)}, f32[48,1024]{1,0:T(8,128)}, u32[]{:S(2)}) copy-start(f32[48,1024]{1,0:T(8,128)} %get-tuple-element.92.refs_1_) | copy-start | bytes 589828
  429.6 22.1 %copy-start.13 = (f32[40,1024]{1,0:T(8,128)S(1)}, f32[40,1024]{1,0:T(8,128)}, u32[]{:S(2)}) copy-start(f32[40,1024]{1,0:T(8,128)} %get-tuple-element.94.refs_3_) | copy-start | bytes 491524
  431.1 23.1 %copy-start.5 = (f32[128,1024]{1,0:T(8,128)S(1)}, f32[128,1024]{1,0:T(8,128)}, u32[]{:S(2)}) copy-start(f32[128,1024]{1,0:T(8,128)} %param.20) | copy-start | bytes 1572868
  448.0 7.5 %copy-start.2 = (f32[1024,176]{0,1:T(8,128)S(1)}, f32[1024,176]{0,1:T(8,128)}, u32[]{:S(2)}) copy-start(f32[1024,176]{0,1:T(8,128)} %param.23) | copy-start | bytes 2162692
  450.0 4.1 copy-start.14
  450.1 4.1 copy-start.15
  450.1 5.5 %copy-start.11 = (f32[1024,176]{0,1:T(8,128)S(1)}, f32[1024,176]{0,1:T(8,128)}, u32[]{:S(2)}) copy-start(f32[1024,176]{0,1:T(8,128)} %param.25) | copy-start | bytes 2162692
  450.1 5.5 %copy-start.12 = (f32[1024,176]{0,1:T(8,128)S(1)}, f32[1024,176]{0,1:T(8,128)}, u32[]{:S(2)}) copy-start(f32[1024,176]{0,1:T(8,128)} %param.24) | copy-start | bytes 2162692
  451.7 5.6 %slice-start.2 = ((s8[4718592]{0:T(1024)(128)(4,1)}), s8[4194304]{0:T(1024)(128)(4,1)S(1)}, s32[]{:S(2)}) async-start(s8[4718592]{0:T(1024)(128)(4,1)} %bitcast.73), calls=%async_computation.2 | async-start | bytes 8388608
  454.1 3.2 slice-start.3
  455.6 3.0 slice-start
  457.3 1.6 slice-start.1
  458.9 1.7 copy-start.3
  458.9 2.4 copy-start.4
  461.3 4.4 copy-start.1
